TPU v7x, 32 devices: a whole 2x2x4 slice. The times are simulated.
32 devices in a mesh: runner: 4 (over z), cells: 8 (over y, x, core).
Axes of the slice: x: 2, y: 2, z: 4, core: 2. Of those that a mesh axis runs over, the one named last changes fastest.
Arguments:
- states: float32 [512, 64, 128], P('runner', 'cells'), may hold values from -4 to 4
- diffusivity: float32 [64, 128], P('cells'), may hold values from 0.03 to 0.2
- velocity: float32 [2, 64, 128], P(None, 'cells'), may hold values from -0.15 to 0.15
- counts: int32 [4], replicated, may hold values from 1 to 128, 256 in all
- obs_index: int32 [4096], P('cells'), may hold values from 0 to 1023
- obs_value: float32 [4096], P('cells'), may hold values from -6 to 6
- obs_weight: float32 [4096], P('cells'), may hold values from 0.3 to 3
Outputs:
- analysed: float32 [512, 64, 128], P('runner', 'cells')
Inputs may be any that keep to these rules, and one draw needn't show every extreme that they name: Runner r's members fill its first counts[r] slots, in runner order; the counts sum to 256 and the largest is exactly 128. Observation k lies in the rows of cells index k // 512; obs_index counts cells within those 8 x 128 cells, row by row; a cell may be observed more than once.
All inputs are finite; a program needn't handle non-finite values.
Results may differ from a plain program's by a relative error of at most 0.013.
Values may be sent and summed in bfloat16 or wider, within the bound.
No kernel may reach another device: no remote copies, remote signals or barrier semaphores. Data moves between devices by JAX's collectives and lax.ppermute only.
A program may use at most 64 MiB of HBM per device.

v0:
```python
import functools

import jax
import jax.numpy as jnp
from jax import lax
from jax.experimental import pallas as pl
from jax.experimental.pallas import tpu as pltpu
from jax.sharding import PartitionSpec as P


STEPS = 4
PAD = 16
F32 = jnp.float32
BF16 = jnp.bfloat16

PARTS = 2


def partners(count, step):
    return [(i, i ^ step) for i in range(count)]


def pieces(row):
    high = row.astype(BF16).astype(F32)
    rest = row - high
    middle = rest.astype(BF16).astype(F32)
    return high, middle, rest - middle


def stacked(rows, height, dtype=BF16):
    width = rows[0].shape[1]
    place = lax.broadcasted_iota(jnp.int32, (height, width), 0)
    total = jnp.zeros((height, width), F32)
    for index, row in enumerate(rows):
        total = jnp.where(place == index, row, total)
    return total.astype(dtype)


def joined(block, first):
    block = block.astype(F32)
    return block[first : first + 1] + block[first + 1 : first + 2] + block[first + 2 : first + 3]


def offset_of(counts_ref, runner, runners):
    total = jnp.int32(0)
    for index in range(runners):
        total = total + jnp.where(index < runner, counts_ref[index], 0)
    return total


def as_row(scalar, width):
    return jnp.full((1, width), scalar, jnp.int32).astype(F32)


def size_of(shape):
    size = shape.dtype.itemsize
    for extent in shape.shape:
        size = size * extent
    return size


def call(kernel, out_shape, scalars, vectors, scratch=()):
    vector = pl.BlockSpec(memory_space=pltpu.VMEM)
    scalar = pl.BlockSpec(memory_space=pltpu.SMEM)
    many = isinstance(out_shape, list)
    shapes = list(vectors) + (out_shape if many else [out_shape])
    held = sum(size_of(shape) for shape in shapes)
    return pl.pallas_call(
        kernel,
        out_shape=out_shape,
        in_specs=[scalar] * len(scalars) + [vector] * len(vectors),
        out_specs=[vector] * len(out_shape) if many else vector,
        scratch_shapes=list(scratch),
        compiler_params=pltpu.CompilerParams(
            vmem_limit_bytes=min(56 << 20, (12 << 20) + 3 * held)
        ),
        cost_estimate=pl.CostEstimate(flops=0, bytes_accessed=1 << 20, transcendentals=0),
    )(*scalars, *vectors)


def edge_kernel(slots, rows, states_ref, fields_ref, last_ref, first_ref):
    for out_ref, base in ((last_ref, rows - STEPS), (first_ref, 0)):
        for j in range(STEPS):
            row = base + j
            out_ref[j, :slots, :] = states_ref[pl.ds(row, slots, stride=rows), :].astype(BF16)
            packed = []
            for field in range(3):
                packed.extend(pieces(fields_ref[field, row : row + 1]))
            out_ref[j, slots:, :] = stacked(packed, PAD)


def forecast_kernel(
    slots, rows, shares, counts_ref, rank_ref, states_ref, low_ref, high_ref, fields_ref, pick_ref,
    *rest,
):
    (coef_ref, value_ref, cells_ref) = rest[-3:]
    seen_refs, part_refs = rest[:shares], rest[shares:-3]
    columns = states_ref.shape[1]
    total_rows = rows + 2 * STEPS
    count = counts_ref[rank_ref[0]]

    for row in range(1, total_rows - 1):
        if STEPS <= row < STEPS + rows:
            own = row - STEPS
            diff, along, across = (fields_ref[field, own : own + 1] for field in range(3))
        else:
            block = (low_ref[row] if row < STEPS else high_ref[row - STEPS - rows])[slots:]
            diff, along, across = joined(block, 0), joined(block, 3), joined(block, 6)
        for index, coef in enumerate(
            (
                1.0 - 4.0 * diff,
                diff - 0.5 * along,
                diff + 0.5 * along,
                diff - 0.5 * across,
                diff + 0.5 * across,
            )
        ):
            coef_ref[row, index] = jnp.broadcast_to(coef, (8, columns))

    chunk = 16
    halves = chunk // 8
    sums = [jnp.zeros((8, columns), F32)] * rows
    for start in range(0, slots, chunk):
        values = []
        for row in range(total_rows):
            if row < STEPS:
                block = low_ref[row, start : start + chunk, :].astype(F32)
            elif row < STEPS + rows:
                block = states_ref[pl.ds(start * rows + row - STEPS, chunk, stride=rows), :]
            else:
                block = high_ref[row - STEPS - rows, start : start + chunk, :].astype(F32)
            values.append([block[8 * h : 8 * h + 8] for h in range(halves)])
        for step in range(STEPS):
            after = list(values)
            for row in range(step + 1, total_rows - step - 1):
                coefs = [coef_ref[row, index] for index in range(5)]
                new = []
                for h in range(halves):
                    u = values[row][h]
                    right = pltpu.roll(u, columns - 1, 1)
                    left = pltpu.roll(u, 1, 1)
                    new.append(
                        u * (coefs[0] - 0.05 * (u * u))
                        + coefs[1] * values[row + 1][h]
                        + coefs[2] * values[row - 1][h]
                        + coefs[3] * right
                        + coefs[4] * left
                    )
                after[row] = new
            values = after
        for h in range(halves):
            place = lax.broadcasted_iota(jnp.int32, (8, columns), 0) + (start + 8 * h)
            live = place < count
            for row in range(rows):
                u = jnp.where(live, values[row + STEPS][h], 0.0)
                sums[row] = sums[row] + u
                value_ref[row, start + 8 * h : start + 8 * h + 8, :] = u

    live = lax.broadcasted_iota(jnp.int32, (slots, columns), 0) < count
    inverse = 1.0 / as_row(count, columns)
    means = []
    for row in range(rows):
        mean = jnp.sum(sums[row], axis=0, keepdims=True) * inverse
        part = jnp.where(live, value_ref[row] - mean, 0.0).astype(BF16)
        cells_ref[:slots, row * columns : (row + 1) * columns] = part
        cells_ref[slots:, row * columns : (row + 1) * columns] = stacked(pieces(mean), PAD)
        means.append(mean)
    width = rows * columns // len(part_refs)
    for index, part_ref in enumerate(part_refs):
        part_ref[...] = cells_ref[:slots, index * width : (index + 1) * width]
    seen = jnp.dot(cells_ref[...], pick_ref[...], preferred_element_type=F32)
    share = seen.shape[1] // shares
    packed = [jnp.zeros((1, share), F32)] * 3
    for first in range(0, rows, share // columns):
        packed.extend(
            pieces(jnp.concatenate(means[first : first + share // columns], axis=1))
        )
    packed = stacked(packed, seen_refs[0].shape[0] - slots)
    for index, seen_ref in enumerate(seen_refs):
        part = seen[:, index * share : (index + 1) * share].astype(BF16)
        seen_ref[:slots, :] = part[:slots]
        seen_ref[slots : slots + PAD, :] = part[slots:] + packed[:PAD]
        if packed.shape[0] > PAD:
            seen_ref[slots + PAD :, :] = packed[PAD:]


def placing(slots, runners, members, counts_ref, runner, by_slot):
    shape, slot_dim = ((slots, members), 0) if by_slot else ((members, slots), 1)
    slot = lax.broadcasted_iota(jnp.int32, shape, slot_dim)
    member = lax.broadcasted_iota(jnp.int32, shape, 1 - slot_dim)
    offset = offset_of(counts_ref, runner, runners)
    hit = (member - slot == offset) & (slot < counts_ref[runner])
    return jnp.where(hit, 1.0, 0.0).astype(BF16)


def triangles(members):
    half = members // 2
    row = lax.broadcasted_iota(jnp.int32, (half, half), 0)
    column = lax.broadcasted_iota(jnp.int32, (half, half), 1)
    return half, row, column


def gram_kernel(slots, runners, members, counts_ref, rank_ref, *refs):
    seen_refs, (value_ref, weight_ref, out_ref) = refs[:runners], refs[runners:]
    rank = rank_ref[0]
    counts = [counts_ref[rank ^ step] for step in range(runners)]
    own_means = [joined(ref[slots:, :], 0) for ref in seen_refs]
    width = value_ref.shape[1]
    mean = 0.0
    for row, count in zip(own_means, counts):
        mean = mean + row * as_row(count, width)
    mean = mean * (1.0 / members)
    observed = 0.0
    for step, ref in enumerate(seen_refs):
        live = lax.broadcasted_iota(jnp.int32, (slots, width), 0) < counts[step]
        part = ref[:slots, :].astype(F32) + (own_means[step] - mean)
        part = jnp.where(live, part, 0.0).astype(BF16)
        place = placing(slots, runners, members, counts_ref, rank ^ step, False)
        observed = observed + jnp.dot(place, part, preferred_element_type=F32)
    weighted = (observed * weight_ref[...]).astype(BF16)
    across = (((1,), (1,)), ((), ()))
    gram = lax.dot_general(
        weighted, observed.astype(BF16), across, preferred_element_type=F32
    )
    innovation = stacked(pieces(value_ref[...] - mean), PAD)
    bias = lax.dot_general(innovation, weighted, across, preferred_element_type=F32)
    half, row, column = triangles(members)
    last = gram[half:, half:]
    out_ref[:half, :half] = jnp.where(row >= column, gram[:half, :half], last)
    out_ref[:half, half:] = gram[:half, half:]
    diagonal = jnp.sum(jnp.where(row == column, last, 0.0), axis=0, keepdims=True)
    diagonal = jnp.concatenate([diagonal, jnp.zeros_like(diagonal)], axis=1)
    out_ref[half:, :] = stacked([bias[0:1] + bias[1:2] + bias[2:3], diagonal], 8, F32)


def total_of(half, part_refs):
    packed, bias, diagonal = 0.0, 0.0, 0.0
    for ref in part_refs:
        packed = packed + ref[:half, :].astype(F32)
        if ref.dtype == BF16:
            bias = bias + joined(ref[half:, :], 0)
            diagonal = diagonal + joined(ref[half:, :], 3)
        else:
            bias = bias + ref[half : half + 1, :]
            diagonal = diagonal + ref[half + 1 : half + 2, :]
    return packed, bias, diagonal


def sum_kernel(half, *refs):
    part_refs, out_ref = refs[:-1], refs[-1]
    packed, bias, diagonal = total_of(half, part_refs)
    out_ref[:half, :] = packed.astype(BF16)
    out_ref[half:, :] = stacked([*pieces(bias), *pieces(diagonal)], PAD)


def transform_kernel(slots, runners, members, counts_ref, rank_ref, *refs):
    part_refs, out_refs = refs[:-2], refs[-2:]
    rank = rank_ref[0]
    half, row, column = triangles(members)
    packed, bias, diagonal = total_of(half, part_refs)
    corner, side = packed[:, :half], packed[:, half:]
    mirror = jnp.transpose(corner)
    first = jnp.where(row >= column, corner, mirror)
    last = jnp.where(
        row < column, corner, jnp.where(row == column, diagonal[:, :half], mirror)
    )
    gram = jnp.concatenate(
        [
            jnp.concatenate([first, side], axis=1),
            jnp.concatenate([jnp.transpose(side), last], axis=1),
        ],
        axis=0,
    )
    trace = jnp.sum(
        jnp.sum(jnp.where(row == column, first + last, 0.0), axis=0, keepdims=True),
        axis=1, keepdims=True,
    )
    scaling = float(members) / trace
    scaled = (gram * scaling).astype(BF16)
    bias = (bias * scaling).astype(BF16).astype(F32)

    def times(left):
        return jnp.dot(left, scaled, preferred_element_type=F32)

    first_power = times(jnp.concatenate([scaled, stacked([bias], PAD)], axis=0))
    square = first_power[:members].astype(BF16)
    bias_1 = first_power[members : members + 1]
    second_power = times(jnp.concatenate([square, stacked(pieces(bias_1), PAD)], axis=0))
    cubed = second_power[:members]
    bias_2 = joined(second_power[members:], 0)
    bias_3 = joined(times(stacked(pieces(bias_2), PAD)), 0)
    shift = bias - 0.5 * bias_1 + 0.375 * bias_2 - 0.3125 * bias_3
    identity = lax.broadcasted_iota(jnp.int32, (members, members), 0) == (
        lax.broadcasted_iota(jnp.int32, (members, members), 1)
    )
    transform = (
        jnp.where(identity, 1.0, 0.0)
        - 0.5 * scaled.astype(F32)
        + 0.375 * square.astype(F32)
        - 0.3125 * cubed
    ).astype(BF16)
    places = [
        placing(slots, runners, members, counts_ref, rank ^ step, False)
        for step in range(0, runners, 2)
    ]
    shift = stacked(pieces(shift), PAD)
    for side, out_ref in enumerate(out_refs):
        own = placing(slots, runners, members, counts_ref, rank ^ (1 - side), True)
        rows = jnp.dot(own, transform, preferred_element_type=F32).astype(BF16)
        left = jnp.concatenate([rows, shift], axis=0)
        for index, place in enumerate(places):
            out_ref[:, index * slots : (index + 1) * slots] = jnp.dot(
                left, place, preferred_element_type=F32
            ).astype(BF16)


def own_means_of(slots, members, counts_ref, rank, seen_refs, cells):
    share = seen_refs[0].shape[1]
    own_means, mean = [], 0.0
    for step, ref in enumerate(seen_refs):
        packed = ref[slots:, :]
        row = jnp.concatenate(
            [joined(packed, 3 + 3 * index) for index in range(cells // share)], axis=1
        )
        own_means.append(row)
        mean = mean + row * as_row(counts_ref[rank ^ step], cells)
    return own_means, mean * (1.0 / members)


def product_kernel(slots, members, runners, with_mean, counts_ref, rank_ref, left_ref, *refs):
    parts = len(refs) - runners
    parts = parts // (runners // 2 + 1)
    seen_refs, cell_refs, out_refs = refs[:runners], refs[runners:-parts], refs[-parts:]
    width = out_refs[0].shape[1]
    own_means, mean = own_means_of(
        slots, members, counts_ref, rank_ref[0], seen_refs, width * parts
    )
    lefts = [
        left_ref[:, index * slots : (index + 1) * slots] for index in range(runners // 2)
    ]
    sums = [jnp.sum(left.astype(F32), axis=1, keepdims=True) for left in lefts]
    for part, out_ref in enumerate(out_refs):
        span = slice(part * width, (part + 1) * width)
        total = 0.0
        for index, left in enumerate(lefts):
            total = total + jnp.dot(
                left, cell_refs[index * parts + part][...], preferred_element_type=F32
            )
            total = total + sums[index] * (own_means[2 * index] - mean)[:, span]
        shift = joined(total[slots:], 0)
        if with_mean:
            shift = shift + mean[:, span]
        out_ref[...] = (total[:slots] + shift).astype(out_ref.dtype)


def final_kernel(slots, rows, counts_ref, rank_ref, *refs):
    own_refs, other_refs, out_ref = refs[: len(refs) // 2], refs[len(refs) // 2 : -1], refs[-1]
    columns = out_ref.shape[1]
    live = lax.broadcasted_iota(jnp.int32, (slots, columns), 0) < counts_ref[rank_ref[0]]
    row = 0
    for own_ref, other_ref in zip(own_refs, other_refs):
        for first in range(0, own_ref.shape[1], columns):
            span = slice(first, first + columns)
            out_ref[pl.ds(row, slots, stride=rows), :] = jnp.where(
                live, own_ref[:, span] + other_ref[:, span].astype(F32), 0.0
            )
            row = row + 1


def body(states, diffusivity, velocity, counts, obs_index, obs_value, obs_weight):
    runners = lax.axis_size("runner")
    blocks = lax.axis_size("cells")
    slots, rows, columns = states.shape
    members = slots // 2 * runners
    half = members // 2
    cells = rows * columns
    seen = obs_index.shape[0]
    shares = 2
    share = seen // shares
    height = slots + PAD
    shape = jax.ShapeDtypeStruct

    rank = lax.axis_index("runner").astype(jnp.int32).reshape(1)
    parity = rank[0] % shares
    flat = states.reshape(slots * rows, columns)
    fields = jnp.concatenate([diffusivity[None], velocity], axis=0)
    last, first = call(
        functools.partial(edge_kernel, slots, rows),
        [shape((STEPS, height, columns), BF16)] * 2,
        [],
        [flat, fields],
    )
    forward = [(i, (i + 1) % blocks) for i in range(blocks)]
    backward = [(target, source) for source, target in forward]
    low = lax.ppermute(last, "cells", forward)
    high = lax.ppermute(first, "cells", backward)

    def own_first(array):
        return jnp.where(parity == 0, array, jnp.roll(array, -share))

    pick = (
        lax.broadcasted_iota(jnp.int32, (cells, seen), 0) == own_first(obs_index)[None, :]
    ).astype(BF16)
    own_value = own_first(obs_value)[None, :share]
    own_weight = own_first(obs_weight)[None, :share]

    lower = -(-(3 + 3 * (cells // share)) // PAD) * PAD
    kept, given, *own_cells = call(
        functools.partial(forecast_kernel, slots, rows, shares),
        [shape((slots + lower, share), BF16)] * shares
        + [shape((slots, cells // PARTS), BF16)] * PARTS,
        [counts, rank],
        [flat, low, high, fields, pick],
        [
            pltpu.VMEM((rows + 2 * STEPS, 5, 8, columns), F32),
            pltpu.VMEM((rows, slots, columns), F32),
            pltpu.VMEM((height, cells), BF16),
        ],
    )

    def moved(array, bit, axis="runner"):
        return lax.ppermute(array, axis, partners(lax.axis_size(axis), bit))

    all_seen = [kept] + [
        moved(given if step % shares else kept, step)
        for step in range(1, runners)
    ]
    all_cells = {0: own_cells}
    bit = runners // 2
    while bit > 1:
        for step in list(all_cells):
            all_cells[step + bit] = [moved(array, bit) for array in all_cells[step]]
        bit = bit // 2
    held = [array for step in sorted(all_cells) for array in all_cells[step]]

    part = call(
        functools.partial(gram_kernel, slots, runners, members),
        shape((half + 8, members), F32),
        [counts, rank],
        [*all_seen, own_value, own_weight],
    )
    stages = [("cells", [1]), ("runner", [1])]
    width = 2
    while width < blocks:
        reach = min(4, blocks // width)
        stages.append(("cells", [width * step for step in range(1, reach)]))
        width = width * reach
    for index, (axis, stage) in enumerate(stages):
        parts = [part] + [moved(part, step, axis) for step in stage]
        if index + 1 < len(stages):
            part = call(
                functools.partial(sum_kernel, half),
                shape((half + PAD, members), BF16),
                [],
                parts,
            )
    give, keep = call(
        functools.partial(transform_kernel, slots, runners, members),
        [shape((height, runners // 2 * slots), BF16)] * 2,
        [counts, rank],
        parts,
    )
    given_products = call(
        functools.partial(product_kernel, slots, members, runners, False),
        [shape((slots, cells // PARTS), BF16)] * PARTS,
        [counts, rank],
        [give, *all_seen, *held],
    )
    other_products = [moved(array, 1) for array in given_products]
    own_products = call(
        functools.partial(product_kernel, slots, members, runners, True),
        [shape((slots, cells // PARTS), F32)] * PARTS,
        [counts, rank],
        [keep, *all_seen, *held],
    )
    analysed = call(
        functools.partial(final_kernel, slots, rows),
        shape((slots * rows, columns), F32),
        [counts, rank],
        [*own_products, *other_products],
    )
    return analysed.reshape(slots, rows, columns)


def solution(mesh):
    return jax.shard_map(
        body,
        mesh=mesh,
        in_specs=(
            P("runner", "cells", None),
            P("cells", None),
            P(None, "cells", None),
            P(),
            P("cells"),
            P("cells"),
            P("cells"),
        ),
        out_specs=P("runner", "cells", None),
        check_vma=False,
    )
```

profile of v0, /device:TPU:0, one launch (start us, length us, event | category | flops | bytes accessed | tf_op | source)
XLA Modules:
  0.0 51.6 jit_solution(17426261100145393311)
XLA Ops:
  0.0 0.0 copy-start.4
  0.0 0.0 copy-start.3
  0.0 0.0 copy-start.2
  0.0 0.7 %pad_maximum_fusion.fields_ref = f32[3,8,128]{2,1,0:T(8,128)S(1)} fusion(f32[2,8,128]{2,1,0:T(8,128)} %param.9, f32[1,8,128]{2,1,0:T(8,128)} %bitcast.10), kind=kLoop, calls=%fused_computation.2 | loop fusion | flops 3072 | bytes 24576 | tf_op jit(solution)/shard_map/concatenate | solution.py:386
  0.8 0.0 copy-start
  0.8 1.0 %copy-done = f32[128,8,128]{2,1,0:T(8,128)S(1)} copy-done((f32[128,8,128]{2,1,0:T(8,128)S(1)}, f32[128,8,128]{2,1,0:T(8,128)}, u32[]{:S(2)}) %copy-start) | copy-done | bytes 524312
  1.8 0.0 copy-start.1
  1.8 0.1 shard_map.73
  1.9 0.5 %collective-permute-start = (bf16[4,144,128]{2,1,0:T(8,128)(2,1)S(1)}, bf16[4,144,128]{2,1,0:T(8,128)(2,1)S(1)}, u32[]{:S(2)}, u32[]{:S(2)}) collective-permute-start(bf16[4,144,128]{2,1,0:T(8,128)(2,1)S(1)} %get-tuple-element.17), channel_id=1, source_target_pairs={{0,1},{1,2},{2,3},{3,4},{4,5},{5,6},{6,7},{7,0},{8,9},{9,10},{10,1... | collective-permute-start | bytes 442376 | tf_op jit(solution)/shard_map/ppermute | solution.py:395
  2.5 2.9 %collective-permute-start.1 = (bf16[4,144,128]{2,1,0:T(8,128)(2,1)S(1)}, bf16[4,144,128]{2,1,0:T(8,128)(2,1)S(1)}, u32[]{:S(2)}, u32[]{:S(2)}) collective-permute-start(bf16[4,144,128]{2,1,0:T(8,128)(2,1)S(1)} %get-tuple-element.18), channel_id=1, source_target_pairs={{1,0},{2,1},{3,2},{4,3},{5,4},{6,5},{7,6},{0,7},{9,8},{10,9},{11,1... | collective-permute-start | bytes 442376 | tf_op jit(solution)/shard_map/ppermute | solution.py:396
  5.4 0.8 %fusion.3 = (s32[256]{0:T(256)S(1)}, s32[256]{0:T(256)S(1)}) fusion(s32[512]{0:T(512)} %param.11), kind=kLoop, calls=%fused_computation.8 | loop fusion | bytes 4096 | tf_op jit(solution)/shard_map/jit(_roll_static)/slice | solution.py:399
  6.1 0.7 %add_select_fusion = s32[512]{0:T(512)S(1)} fusion(s32[512]{0:T(512)} %param.11, s32[256]{0:T(256)S(1)} %get-tuple-element.34, s32[256]{0:T(256)S(1)} %get-tuple-element.33, pred[]{:T(512)S(6)} %eq.8), kind=kLoop, calls=%fused_computation.3 | loop fusion | flops 1024 | bytes 6145 | tf_op jit(solution)/shard_map/jit(_where)/select_n | solution.py:399
  6.8 0.4 fusion.pick_ref
  7.3 0.0 copy-done.4
  7.3 0.0 copy-done.3
  7.3 0.8 %collective-permute-done.low_ref = bf16[4,144,128]{2,1,0:T(8,128)(2,1)S(1)} collective-permute-done((bf16[4,144,128]{2,1,0:T(8,128)(2,1)S(1)}, bf16[4,144,128]{2,1,0:T(8,128)(2,1)S(1)}, u32[]{:S(2)}, u32[]{:S(2)}) %collective-permute-start) | collective-permute-done | bytes 147488 | tf_op jit(solution)/shard_map/ppermute | solution.py:395
  8.2 0.4 collective-permute-done.1.high_ref
  8.6 0.0 copy-done.2
  8.6 0.0 copy-done.1
  8.6 2.8 %shard_map.74 = (bf16[144,256]{1,0:T(8,128)(2,1)S(1)}, bf16[144,256]{1,0:T(8,128)(2,1)S(1)}, bf16[128,512]{1,0:T(8,128)(2,1)S(1)}, bf16[128,512]{1,0:T(8,128)(2,1)S(1)}) custom-call(s32[4]{0:T(128)S(1)} %copy-done.2, s32[1]{0:T(128)} %bitcast.rank_ref, f32[1024,128]{1,0:T(8,128)S(1)} %bitcast.7, bf16[4,144,128]{2,1,0:T(8,128)(2,1)S(1)} %collective-permute-done.low_ref, ...), custom_call_target="tpu_custom_call" | custom-call | bytes 1048576 | tf_op jit(solution)/shard_map/pallas_call | solution.py:68
  11.4 2.0 %collective-permute-start.2 = (bf16[144,256]{1,0:T(8,128)(2,1)S(1)}, bf16[144,256]{1,0:T(8,128)(2,1)S(1)}, u32[]{:S(2)}, u32[]{:S(2)}) collective-permute-start(bf16[144,256]{1,0:T(8,128)(2,1)S(1)} %get-tuple-element.20), channel_id=1, source_target_pairs={{0,8},{8,0},{16,24},{24,16},{1,9},{9,1},{17,25},{25,17},{2,10},{10... | collective-permute-start | bytes 221192 | tf_op jit(solution)/shard_map/ppermute | solution.py:422
  13.3 2.5 %collective-permute-start.4 = (bf16[144,256]{1,0:T(8,128)(2,1)S(1)}, bf16[144,256]{1,0:T(8,128)(2,1)S(1)}, u32[]{:S(2)}, u32[]{:S(2)}) collective-permute-start(bf16[144,256]{1,0:T(8,128)(2,1)S(1)} %get-tuple-element.20), channel_id=1, source_target_pairs={{0,24},{8,16},{16,8},{24,0},{1,25},{9,17},{17,9},{25,1},{2,26},{10... | collective-permute-start | bytes 221192 | tf_op jit(solution)/shard_map/ppermute | solution.py:422
  15.8 0.1 collective-permute-start.3
  15.9 0.0 collective-permute-done.2.refs_1_
  15.9 7.8 %collective-permute-done.3.refs_2_ = bf16[144,256]{1,0:T(8,128)(2,1)S(1)} collective-permute-done((bf16[144,256]{1,0:T(8,128)(2,1)S(1)}, bf16[144,256]{1,0:T(8,128)(2,1)S(1)}, u32[]{:S(2)}, u32[]{:S(2)}) %collective-permute-start.3) | collective-permute-done | bytes 73760 | tf_op jit(solution)/shard_map/ppermute | solution.py:422
  23.8 0.0 collective-permute-done.4.refs_3_
  23.8 1.1 %shard_map.75.refs_0_ = f32[136,256]{1,0:T(8,128)S(1)} custom-call(s32[4]{0:T(128)S(1)} %copy-done.2, s32[1]{0:T(128)} %bitcast.rank_ref, bf16[144,256]{1,0:T(8,128)(2,1)S(1)} %get-tuple-element.19.refs_0_, bf16[144,256]{1,0:T(8,128)(2,1)S(1)} %collective-permute-done.2.refs_1_, bf16[144,256]{1,0:T(8,128)(2,1)S(1)} %collective-permute-done.3.refs_2_, ...), custom_call_target="tpu_custom_call" | custom-call | bytes 1048576 | tf_op jit(solution)/shard_map/pallas_call | solution.py:68
  24.8 0.2 collective-permute-start.5
  25.0 1.2 %collective-permute-done.5.refs_1_ = f32[136,256]{1,0:T(8,128)S(1)} collective-permute-done((f32[136,256]{1,0:T(8,128)S(1)}, f32[136,256]{1,0:T(8,128)S(1)}, u32[]{:S(2)}, u32[]{:S(2)}) %collective-permute-start.5) | collective-permute-done | bytes 139296 | tf_op jit(solution)/shard_map/ppermute | solution.py:422
  26.3 0.1 collective-permute-start.6
  26.4 3.3 %collective-permute-start.10 = (bf16[128,512]{1,0:T(8,128)(2,1)S(1)}, bf16[128,512]{1,0:T(8,128)(2,1)S(1)}, u32[]{:S(2)}, u32[]{:S(2)}) collective-permute-start(bf16[128,512]{1,0:T(8,128)(2,1)S(1)} %get-tuple-element.22.refs_4_), channel_id=1, source_target_pairs={{0,16},{8,24},{16,0},{24,8},{1,17},{9,25},{17,1},{25,9},{2,18},{10... | collective-permute-start | bytes 393224 | tf_op jit(solution)/shard_map/ppermute | solution.py:422
  29.7 0.0 collective-permute-start.11
  29.7 2.2 %collective-permute-done.6.refs_1_ = bf16[144,256]{1,0:T(8,128)(2,1)S(1)} collective-permute-done((bf16[144,256]{1,0:T(8,128)(2,1)S(1)}, bf16[144,256]{1,0:T(8,128)(2,1)S(1)}, u32[]{:S(2)}, u32[]{:S(2)}) %collective-permute-start.6) | collective-permute-done | bytes 73760 | tf_op jit(solution)/shard_map/ppermute | solution.py:422
  31.9 1.6 %collective-permute-start.7 = (bf16[144,256]{1,0:T(8,128)(2,1)S(1)}, bf16[144,256]{1,0:T(8,128)(2,1)S(1)}, u32[]{:S(2)}, u32[]{:S(2)}) collective-permute-start(bf16[144,256]{1,0:T(8,128)(2,1)S(1)} %shard_map.77.refs_0_), channel_id=1, source_target_pairs={{0,2},{1,3},{2,0},{3,1},{4,6},{5,7},{6,4},{7,5},{8,10},{9,11},{10,... | collective-permute-start | bytes 221192 | tf_op jit(solution)/shard_map/ppermute | solution.py:422
  33.5 0.6 %collective-permute-start.8 = (bf16[144,256]{1,0:T(8,128)(2,1)S(1)}, bf16[144,256]{1,0:T(8,128)(2,1)S(1)}, u32[]{:S(2)}, u32[]{:S(2)}) collective-permute-start(bf16[144,256]{1,0:T(8,128)(2,1)S(1)} %shard_map.77.refs_0_), channel_id=1, source_target_pairs={{0,4},{1,5},{2,6},{3,7},{4,0},{5,1},{6,2},{7,3},{8,12},{9,13},{10,... | collective-permute-start | bytes 221192 | tf_op jit(solution)/shard_map/ppermute | solution.py:422
  34.1 1.3 %collective-permute-start.9 = (bf16[144,256]{1,0:T(8,128)(2,1)S(1)}, bf16[144,256]{1,0:T(8,128)(2,1)S(1)}, u32[]{:S(2)}, u32[]{:S(2)}) collective-permute-start(bf16[144,256]{1,0:T(8,128)(2,1)S(1)} %shard_map.77.refs_0_), channel_id=1, source_target_pairs={{0,6},{1,7},{2,4},{3,5},{4,2},{5,3},{6,0},{7,1},{8,14},{9,15},{10,... | collective-permute-start | bytes 221192 | tf_op jit(solution)/shard_map/ppermute | solution.py:422
  35.5 0.9 %collective-permute-done.7.refs_1_ = bf16[144,256]{1,0:T(8,128)(2,1)S(1)} collective-permute-done((bf16[144,256]{1,0:T(8,128)(2,1)S(1)}, bf16[144,256]{1,0:T(8,128)(2,1)S(1)}, u32[]{:S(2)}, u32[]{:S(2)}) %collective-permute-start.7) | collective-permute-done | bytes 73760 | tf_op jit(solution)/shard_map/ppermute | solution.py:422
  36.3 1.6 %collective-permute-done.8.refs_2_ = bf16[144,256]{1,0:T(8,128)(2,1)S(1)} collective-permute-done((bf16[144,256]{1,0:T(8,128)(2,1)S(1)}, bf16[144,256]{1,0:T(8,128)(2,1)S(1)}, u32[]{:S(2)}, u32[]{:S(2)}) %collective-permute-start.8) | collective-permute-done | bytes 73760 | tf_op jit(solution)/shard_map/ppermute | solution.py:422
  37.9 1.5 %collective-permute-done.9.refs_3_ = bf16[144,256]{1,0:T(8,128)(2,1)S(1)} collective-permute-done((bf16[144,256]{1,0:T(8,128)(2,1)S(1)}, bf16[144,256]{1,0:T(8,128)(2,1)S(1)}, u32[]{:S(2)}, u32[]{:S(2)}) %collective-permute-start.9) | collective-permute-done | bytes 73760 | tf_op jit(solution)/shard_map/ppermute | solution.py:422
  39.4 1.6 %shard_map.78 = (bf16[144,256]{1,0:T(8,128)(2,1)S(1)}, bf16[144,256]{1,0:T(8,128)(2,1)S(1)}) custom-call(s32[4]{0:T(128)S(1)} %copy-done.2, s32[1]{0:T(128)} %bitcast.rank_ref, bf16[144,256]{1,0:T(8,128)(2,1)S(1)} %shard_map.77.refs_0_, bf16[144,256]{1,0:T(8,128)(2,1)S(1)} %collective-permute-done.7.refs_1_, ...), custom_call_target="tpu_custom_call" | custom-call | bytes 1048576 | tf_op jit(solution)/shard_map/pallas_call | solution.py:68
  41.0 0.0 collective-permute-done.10.refs_6_
  41.0 0.7 %collective-permute-done.11.refs_7_ = bf16[128,512]{1,0:T(8,128)(2,1)S(1)} collective-permute-done((bf16[128,512]{1,0:T(8,128)(2,1)S(1)}, bf16[128,512]{1,0:T(8,128)(2,1)S(1)}, u32[]{:S(2)}, u32[]{:S(2)}) %collective-permute-start.11) | collective-permute-done | bytes 131104 | tf_op jit(solution)/shard_map/ppermute | solution.py:422
  41.6 0.9 %shard_map.80 = (bf16[128,512]{1,0:T(8,128)(2,1)S(1)}, bf16[128,512]{1,0:T(8,128)(2,1)S(1)}) custom-call(s32[4]{0:T(128)S(1)} %copy-done.2, s32[1]{0:T(128)} %bitcast.rank_ref, bf16[144,256]{1,0:T(8,128)(2,1)S(1)} %get-tuple-element.26.left_ref, bf16[144,256]{1,0:T(8,128)(2,1)S(1)} %get-tuple-element.19.refs_0_, ...), custom_call_target="tpu_custom_call" | custom-call | bytes 1048576 | tf_op jit(solution)/shard_map/pallas_call | solution.py:68
  42.5 0.1 collective-permute-start.12
  42.6 2.0 %collective-permute-start.13 = (bf16[128,512]{1,0:T(8,128)(2,1)S(1)}, bf16[128,512]{1,0:T(8,128)(2,1)S(1)}, u32[]{:S(2)}, u32[]{:S(2)}) collective-permute-start(bf16[128,512]{1,0:T(8,128)(2,1)S(1)} %get-tuple-element.28), channel_id=1, source_target_pairs={{0,8},{8,0},{16,24},{24,16},{1,9},{9,1},{17,25},{25,17},{2,10},{10... | collective-permute-start | bytes 393224 | tf_op jit(solution)/shard_map/ppermute | solution.py:422
  44.6 0.9 %shard_map.79 = (f32[128,512]{1,0:T(8,128)S(1)}, f32[128,512]{1,0:T(8,128)S(1)}) custom-call(s32[4]{0:T(128)S(1)} %copy-done.2, s32[1]{0:T(128)} %bitcast.rank_ref, bf16[144,256]{1,0:T(8,128)(2,1)S(1)} %get-tuple-element.21.left_ref, bf16[144,256]{1,0:T(8,128)(2,1)S(1)} %get-tuple-element.19.refs_0_, bf16[144,256]{1,0:T(8,128)(2,1)S(1)} %collective-permute-done.2.refs_1_, ...), custom_call_target="tpu_custom_call" | custom-call | bytes 1048576 | tf_op jit(solution)/shard_map/pallas_call | solution.py:68
  45.6 3.2 %collective-permute-done.12.refs_2_ = bf16[128,512]{1,0:T(8,128)(2,1)S(1)} collective-permute-done((bf16[128,512]{1,0:T(8,128)(2,1)S(1)}, bf16[128,512]{1,0:T(8,128)(2,1)S(1)}, u32[]{:S(2)}, u32[]{:S(2)}) %collective-permute-start.12) | collective-permute-done | bytes 131104 | tf_op jit(solution)/shard_map/ppermute | solution.py:422
  48.7 1.4 %collective-permute-done.13.refs_3_ = bf16[128,512]{1,0:T(8,128)(2,1)S(1)} collective-permute-done((bf16[128,512]{1,0:T(8,128)(2,1)S(1)}, bf16[128,512]{1,0:T(8,128)(2,1)S(1)}, u32[]{:S(2)}, u32[]{:S(2)}) %collective-permute-start.13) | collective-permute-done | bytes 131104 | tf_op jit(solution)/shard_map/ppermute | solution.py:422
  50.1 1.5 %shard_map.81 = f32[1024,128]{1,0:T(8,128)} custom-call(s32[4]{0:T(128)S(1)} %copy-done.2, s32[1]{0:T(128)} %bitcast.rank_ref, f32[128,512]{1,0:T(8,128)S(1)} %get-tuple-element.24.refs_0_, f32[128,512]{1,0:T(8,128)S(1)} %get-tuple-element.25.refs_1_, bf16[128,512]{1,0:T(8,128)(2,1)S(1)} %collective-permute-done.12.refs_2_, ...), custom_call_target="tpu_custom_call" | custom-call | bytes 1048576 | tf_op jit(solution)/shard_map/pallas_call | solution.py:68
  (7 shorter events, 0.1 us)
Async XLA Ops:
  0.0 7.3 %copy-start.4 = (f32[512]{0:T(512)S(1)}, f32[512]{0:T(512)}, u32[]{:S(2)}) copy-start(f32[512]{0:T(512)} %param.13) | copy-start | bytes 6148
  0.0 7.3 %copy-start.3 = (f32[512]{0:T(512)S(1)}, f32[512]{0:T(512)}, u32[]{:S(2)}) copy-start(f32[512]{0:T(512)} %param.12) | copy-start | bytes 6148
  0.0 8.6 %copy-start.2 = (s32[4]{0:T(128)S(1)}, s32[4]{0:T(128)}, u32[]{:S(2)}) copy-start(s32[4]{0:T(128)} %counts_ref.11) | copy-start | bytes 52
  0.8 1.0 %copy-start = (f32[128,8,128]{2,1,0:T(8,128)S(1)}, f32[128,8,128]{2,1,0:T(8,128)}, u32[]{:S(2)}) copy-start(f32[128,8,128]{2,1,0:T(8,128)} %param.7) | copy-start | bytes 1572868
  1.8 6.8 %copy-start.1 = (f32[128,8,128]{2,1,0:T(8,128)S(1)}, f32[128,8,128]{2,1,0:T(8,128)}, u32[]{:S(2)}) copy-start(f32[128,8,128]{2,1,0:T(8,128)} %param.7) | copy-start | bytes 1572868
  1.9 6.2 %collective-permute-start = (bf16[4,144,128]{2,1,0:T(8,128)(2,1)S(1)}, bf16[4,144,128]{2,1,0:T(8,128)(2,1)S(1)}, u32[]{:S(2)}, u32[]{:S(2)}) collective-permute-start(bf16[4,144,128]{2,1,0:T(8,128)(2,1)S(1)} %get-tuple-element.17), channel_id=1, source_target_pairs={{0,1},{1,2},{2,3},{3,4},{4,5},{5,6},{6,7},{7,0},{8,9},{9,10},{10,1... | collective-permute-start | bytes 442376 | tf_op jit(solution)/shard_map/ppermute | solution.py:395
  2.5 6.1 %collective-permute-start.1 = (bf16[4,144,128]{2,1,0:T(8,128)(2,1)S(1)}, bf16[4,144,128]{2,1,0:T(8,128)(2,1)S(1)}, u32[]{:S(2)}, u32[]{:S(2)}) collective-permute-start(bf16[4,144,128]{2,1,0:T(8,128)(2,1)S(1)} %get-tuple-element.18), channel_id=1, source_target_pairs={{1,0},{2,1},{3,2},{4,3},{5,4},{6,5},{7,6},{0,7},{9,8},{10,9},{11,1... | collective-permute-start | bytes 442376 | tf_op jit(solution)/shard_map/ppermute | solution.py:396
  11.4 4.6 %collective-permute-start.2 = (bf16[144,256]{1,0:T(8,128)(2,1)S(1)}, bf16[144,256]{1,0:T(8,128)(2,1)S(1)}, u32[]{:S(2)}, u32[]{:S(2)}) collective-permute-start(bf16[144,256]{1,0:T(8,128)(2,1)S(1)} %get-tuple-element.20), channel_id=1, source_target_pairs={{0,8},{8,0},{16,24},{24,16},{1,9},{9,1},{17,25},{25,17},{2,10},{10... | collective-permute-start | bytes 221192 | tf_op jit(solution)/shard_map/ppermute | solution.py:422
  13.3 10.4 %collective-permute-start.4 = (bf16[144,256]{1,0:T(8,128)(2,1)S(1)}, bf16[144,256]{1,0:T(8,128)(2,1)S(1)}, u32[]{:S(2)}, u32[]{:S(2)}) collective-permute-start(bf16[144,256]{1,0:T(8,128)(2,1)S(1)} %get-tuple-element.20), channel_id=1, source_target_pairs={{0,24},{8,16},{16,8},{24,0},{1,25},{9,17},{17,9},{25,1},{2,26},{10... | collective-permute-start | bytes 221192 | tf_op jit(solution)/shard_map/ppermute | solution.py:422
  15.8 8.0 %collective-permute-start.3 = (bf16[144,256]{1,0:T(8,128)(2,1)S(1)}, bf16[144,256]{1,0:T(8,128)(2,1)S(1)}, u32[]{:S(2)}, u32[]{:S(2)}) collective-permute-start(bf16[144,256]{1,0:T(8,128)(2,1)S(1)} %get-tuple-element.19.refs_0_), channel_id=1, source_target_pairs={{0,16},{8,24},{16,0},{24,8},{1,17},{9,25},{17,1},{25,9},{2,18},{10... | collective-permute-start | bytes 221192 | tf_op jit(solution)/shard_map/ppermute | solution.py:422
  24.8 1.4 %collective-permute-start.5 = (f32[136,256]{1,0:T(8,128)S(1)}, f32[136,256]{1,0:T(8,128)S(1)}, u32[]{:S(2)}, u32[]{:S(2)}) collective-permute-start(f32[136,256]{1,0:T(8,128)S(1)} %shard_map.75.refs_0_), channel_id=1, source_target_pairs={{0,1},{1,0},{2,3},{3,2},{4,5},{5,4},{6,7},{7,6},{8,9},{9,8},{10,11... | collective-permute-start | bytes 417800 | tf_op jit(solution)/shard_map/ppermute | solution.py:422
  26.3 5.5 %collective-permute-start.6 = (bf16[144,256]{1,0:T(8,128)(2,1)S(1)}, bf16[144,256]{1,0:T(8,128)(2,1)S(1)}, u32[]{:S(2)}, u32[]{:S(2)}) collective-permute-start(bf16[144,256]{1,0:T(8,128)(2,1)S(1)} %shard_map.76.refs_0_), channel_id=1, source_target_pairs={{0,8},{8,0},{16,24},{24,16},{1,9},{9,1},{17,25},{25,17},{2,10},{10... | collective-permute-start | bytes 221192 | tf_op jit(solution)/shard_map/ppermute | solution.py:422
  26.4 14.6 %collective-permute-start.10 = (bf16[128,512]{1,0:T(8,128)(2,1)S(1)}, bf16[128,512]{1,0:T(8,128)(2,1)S(1)}, u32[]{:S(2)}, u32[]{:S(2)}) collective-permute-start(bf16[128,512]{1,0:T(8,128)(2,1)S(1)} %get-tuple-element.22.refs_4_), channel_id=1, source_target_pairs={{0,16},{8,24},{16,0},{24,8},{1,17},{9,25},{17,1},{25,9},{2,18},{10... | collective-permute-start | bytes 393224 | tf_op jit(solution)/shard_map/ppermute | solution.py:422
  29.7 12.0 %collective-permute-start.11 = (bf16[128,512]{1,0:T(8,128)(2,1)S(1)}, bf16[128,512]{1,0:T(8,128)(2,1)S(1)}, u32[]{:S(2)}, u32[]{:S(2)}) collective-permute-start(bf16[128,512]{1,0:T(8,128)(2,1)S(1)} %get-tuple-element.23.refs_5_), channel_id=1, source_target_pairs={{0,16},{8,24},{16,0},{24,8},{1,17},{9,25},{17,1},{25,9},{2,18},{10... | collective-permute-start | bytes 393224 | tf_op jit(solution)/shard_map/ppermute | solution.py:422
  31.9 4.4 %collective-permute-start.7 = (bf16[144,256]{1,0:T(8,128)(2,1)S(1)}, bf16[144,256]{1,0:T(8,128)(2,1)S(1)}, u32[]{:S(2)}, u32[]{:S(2)}) collective-permute-start(bf16[144,256]{1,0:T(8,128)(2,1)S(1)} %shard_map.77.refs_0_), channel_id=1, source_target_pairs={{0,2},{1,3},{2,0},{3,1},{4,6},{5,7},{6,4},{7,5},{8,10},{9,11},{10,... | collective-permute-start | bytes 221192 | tf_op jit(solution)/shard_map/ppermute | solution.py:422
  33.5 4.4 %collective-permute-start.8 = (bf16[144,256]{1,0:T(8,128)(2,1)S(1)}, bf16[144,256]{1,0:T(8,128)(2,1)S(1)}, u32[]{:S(2)}, u32[]{:S(2)}) collective-permute-start(bf16[144,256]{1,0:T(8,128)(2,1)S(1)} %shard_map.77.refs_0_), channel_id=1, source_target_pairs={{0,4},{1,5},{2,6},{3,7},{4,0},{5,1},{6,2},{7,3},{8,12},{9,13},{10,... | collective-permute-start | bytes 221192 | tf_op jit(solution)/shard_map/ppermute | solution.py:422
  34.1 5.3 %collective-permute-start.9 = (bf16[144,256]{1,0:T(8,128)(2,1)S(1)}, bf16[144,256]{1,0:T(8,128)(2,1)S(1)}, u32[]{:S(2)}, u32[]{:S(2)}) collective-permute-start(bf16[144,256]{1,0:T(8,128)(2,1)S(1)} %shard_map.77.refs_0_), channel_id=1, source_target_pairs={{0,6},{1,7},{2,4},{3,5},{4,2},{5,3},{6,0},{7,1},{8,14},{9,15},{10,... | collective-permute-start | bytes 221192 | tf_op jit(solution)/shard_map/ppermute | solution.py:422
  42.5 6.2 %collective-permute-start.12 = (bf16[128,512]{1,0:T(8,128)(2,1)S(1)}, bf16[128,512]{1,0:T(8,128)(2,1)S(1)}, u32[]{:S(2)}, u32[]{:S(2)}) collective-permute-start(bf16[128,512]{1,0:T(8,128)(2,1)S(1)} %get-tuple-element.27), channel_id=1, source_target_pairs={{0,8},{8,0},{16,24},{24,16},{1,9},{9,1},{17,25},{25,17},{2,10},{10... | collective-permute-start | bytes 393224 | tf_op jit(solution)/shard_map/ppermute | solution.py:422
  42.6 7.5 %collective-permute-start.13 = (bf16[128,512]{1,0:T(8,128)(2,1)S(1)}, bf16[128,512]{1,0:T(8,128)(2,1)S(1)}, u32[]{:S(2)}, u32[]{:S(2)}) collective-permute-start(bf16[128,512]{1,0:T(8,128)(2,1)S(1)} %get-tuple-element.28), channel_id=1, source_target_pairs={{0,8},{8,0},{16,24},{24,16},{1,9},{9,1},{17,25},{25,17},{2,10},{10... | collective-permute-start | bytes 393224 | tf_op jit(solution)/shard_map/ppermute | solution.py:422
where the time goes:
time: 51.9 us; the launch traced here: 51.6 us
  waiting for transfers between devices  21.7 us (42%)
  starting transfers between devices  17.2 us (33%)
  Pallas kernels  8.88 us (17%)
  other arithmetic  1.87 us (4%)
  local copies, waits for them, and re-layouts  1.83 us (4%)
    ppermute x12, waiting for transfers between devices, moved(): return lax.ppermute(array, axis, partners(lax.axis_size(axis), bit))  20.4 us
    ppermute x12, starting transfers between devices, moved(): return lax.ppermute(array, axis, partners(lax.axis_size(axis), bit))  13.8 us
    pallas_call x9, Pallas kernels, call(): pl.pallas_call(kernel, out_shape=out_shape, in_specs=[scalar] * len(scala...  8.88 us
    ppermute x1, starting transfers between devices, body(): high = lax.ppermute(first, 'cells', backward)  2.93 us
    unnamed x10, local copies, waits for them, and re-layouts  1.06 us
  transfers between devices with their start and end apart: 14, of which 11 were waited for; matrix products, arithmetic and copies ran while one was open for 4% of the time, Pallas kernels for 5%

commit v1 on v0

--- a/solution.py
+++ b/solution.py
@@ -14,6 +14,8 @@
 BF16 = jnp.bfloat16
 
 PARTS = 2
+WRITES = 4
+GATHERED = 1
 
 
 def partners(count, step):
@@ -59,17 +61,20 @@
     return size
 
 
-def call(kernel, out_shape, scalars, vectors, scratch=()):
+def call(kernel, out_shape, scalars, vectors, scratch=(), outside=False, write=False):
     vector = pl.BlockSpec(memory_space=pltpu.VMEM)
     scalar = pl.BlockSpec(memory_space=pltpu.SMEM)
+    hbm = pl.BlockSpec(memory_space=pltpu.HBM)
+    if outside:
+        vectors = [pltpu.with_memory_space_constraint(array, pltpu.HBM) for array in vectors]
     many = isinstance(out_shape, list)
     shapes = list(vectors) + (out_shape if many else [out_shape])
     held = sum(size_of(shape) for shape in shapes)
     return pl.pallas_call(
         kernel,
         out_shape=out_shape,
-        in_specs=[scalar] * len(scalars) + [vector] * len(vectors),
-        out_specs=[vector] * len(out_shape) if many else vector,
+        in_specs=[scalar] * len(scalars) + [hbm if outside else vector] * len(vectors),
+        out_specs=hbm if write else [vector] * len(out_shape) if many else vector,
         scratch_shapes=list(scratch),
         compiler_params=pltpu.CompilerParams(
             vmem_limit_bytes=min(56 << 20, (12 << 20) + 3 * held)
@@ -78,7 +83,18 @@
     )(*scalars, *vectors)
 
 
-def edge_kernel(slots, rows, states_ref, fields_ref, last_ref, first_ref):
+def edge_kernel(
+    slots, rows, states_hbm, diff_hbm, vel_hbm, last_ref, first_ref, states_ref, fields_ref, sems
+):
+    copies = [
+        pltpu.make_async_copy(states_hbm, states_ref, sems.at[0]),
+        pltpu.make_async_copy(diff_hbm, fields_ref.at[0], sems.at[1]),
+        pltpu.make_async_copy(vel_hbm, fields_ref.at[pl.ds(1, 2)], sems.at[2]),
+    ]
+    for copy in copies:
+        copy.start()
+    for copy in copies:
+        copy.wait()
     for out_ref, base in ((last_ref, rows - STEPS), (first_ref, 0)):
         for j in range(STEPS):
             row = base + j
@@ -89,9 +105,63 @@
             out_ref[j, slots:, :] = stacked(packed, PAD)
 
 
+def coefficients(diff, along, across):
+    columns = diff.shape[1]
+    return [
+        jnp.broadcast_to(coef, (8, columns))
+        for coef in (
+            1.0 - 4.0 * diff,
+            diff - 0.5 * along,
+            diff + 0.5 * along,
+            diff - 0.5 * across,
+            diff + 0.5 * across,
+        )
+    ]
+
+
+def advanced(u, above, below, coefs):
+    columns = u.shape[1]
+    return (
+        u * (coefs[0] - 0.05 * (u * u))
+        + coefs[1] * above
+        + coefs[2] * below
+        + coefs[3] * pltpu.roll(u, columns - 1, 1)
+        + coefs[4] * pltpu.roll(u, 1, 1)
+    )
+
+
+def inner_rows(rows):
+    return [range(step, rows - step) for step in range(1, STEPS) if step < rows - step]
+
+
+def inner_kernel(slots, rows, states_ref, fields_ref, coef_ref, inner_ref):
+    for row in range(rows):
+        fields = [fields_ref[field, row : row + 1] for field in range(3)]
+        for index, coef in enumerate(coefficients(*fields)):
+            coef_ref[row, index] = coef
+    for start in range(0, slots, 16):
+        values = []
+        for row in range(rows):
+            block = states_ref[pl.ds(start * rows + row, 16, stride=rows), :]
+            values.append([block[8 * h : 8 * h + 8] for h in range(2)])
+        place = 0
+        for inside in inner_rows(rows):
+            after = list(values)
+            for row in inside:
+                coefs = [coef_ref[row, index] for index in range(5)]
+                after[row] = [
+                    advanced(values[row][h], values[row + 1][h], values[row - 1][h], coefs)
+                    for h in range(2)
+                ]
+                for h in range(2):
+                    inner_ref[place, start + 8 * h : start + 8 * h + 8, :] = after[row][h]
+                place = place + 1
+            values = after
+
+
 def forecast_kernel(
-    slots, rows, shares, counts_ref, rank_ref, states_ref, low_ref, high_ref, fields_ref, pick_ref,
-    *rest,
+    slots, rows, shares, counts_ref, rank_ref, states_ref, low_ref, high_ref, own_coef_ref,
+    inner_ref, pick_ref, *rest,
 ):
     (coef_ref, value_ref, cells_ref) = rest[-3:]
     seen_refs, part_refs = rest[:shares], rest[shares:-3]
@@ -99,24 +169,16 @@
     total_rows = rows + 2 * STEPS
     count = counts_ref[rank_ref[0]]
 
-    for row in range(1, total_rows - 1):
-        if STEPS <= row < STEPS + rows:
-            own = row - STEPS
-            diff, along, across = (fields_ref[field, own : own + 1] for field in range(3))
-        else:
-            block = (low_ref[row] if row < STEPS else high_ref[row - STEPS - rows])[slots:]
-            diff, along, across = joined(block, 0), joined(block, 3), joined(block, 6)
-        for index, coef in enumerate(
-            (
-                1.0 - 4.0 * diff,
-                diff - 0.5 * along,
-                diff + 0.5 * along,
-                diff - 0.5 * across,
-                diff + 0.5 * across,
-            )
-        ):
-            coef_ref[row, index] = jnp.broadcast_to(coef, (8, columns))
-
+    for row in [*range(1, STEPS), *range(STEPS + rows, total_rows - 1)]:
+        block = (low_ref[row] if row < STEPS else high_ref[row - STEPS - rows])[slots:]
+        fields = [joined(block, 3 * field) for field in range(3)]
+        for index, coef in enumerate(coefficients(*fields)):
+            coef_ref[row, index] = coef
+
+    known = {}
+    for step, inside in enumerate(inner_rows(rows)):
+        for row in inside:
+            known[step, row + STEPS] = len(known)
     chunk = 16
     halves = chunk // 8
     sums = [jnp.zeros((8, columns), F32)] * rows
@@ -133,20 +195,18 @@
         for step in range(STEPS):
             after = list(values)
             for row in range(step + 1, total_rows - step - 1):
-                coefs = [coef_ref[row, index] for index in range(5)]
-                new = []
-                for h in range(halves):
-                    u = values[row][h]
-                    right = pltpu.roll(u, columns - 1, 1)
-                    left = pltpu.roll(u, 1, 1)
-                    new.append(
-                        u * (coefs[0] - 0.05 * (u * u))
-                        + coefs[1] * values[row + 1][h]
-                        + coefs[2] * values[row - 1][h]
-                        + coefs[3] * right
-                        + coefs[4] * left
-                    )
-                after[row] = new
+                if (step, row) in known:
+                    block = inner_ref[known[step, row], start : start + chunk, :]
+                    after[row] = [block[8 * h : 8 * h + 8] for h in range(halves)]
+                    continue
+                if STEPS <= row < STEPS + rows:
+                    coefs = [own_coef_ref[row - STEPS, index] for index in range(5)]
+                else:
+                    coefs = [coef_ref[row, index] for index in range(5)]
+                after[row] = [
+                    advanced(values[row][h], values[row + 1][h], values[row - 1][h], coefs)
+                    for h in range(halves)
+                ]
             values = after
         for h in range(halves):
             place = lax.broadcasted_iota(jnp.int32, (8, columns), 0) + (start + 8 * h)
@@ -193,6 +253,29 @@
     return jnp.where(hit, 1.0, 0.0).astype(BF16)
 
 
+def setup_kernel(
+    slots, runners, members, shares, counts_ref, rank_ref, index_ref, value_ref, weight_ref,
+    pick_ref, seen_ref, place_ref, own_ref,
+):
+    rank = rank_ref[0]
+    share = index_ref.shape[1] // shares
+
+    def own_first(ref):
+        swapped = jnp.concatenate([ref[:, share:], ref[:, :share]], axis=1)
+        return jnp.where(jnp.bitwise_and(rank, 1) == 0, ref[...], swapped)
+
+    wanted = own_first(index_ref)
+    cell = lax.broadcasted_iota(jnp.int32, pick_ref.shape, 0)
+    pick_ref[...] = jnp.where(cell == wanted, 1.0, 0.0).astype(BF16)
+    seen_ref[...] = stacked([own_first(value_ref)[:, :share], own_first(weight_ref)[:, :share]], 8, F32)
+    for step in range(runners):
+        place_ref[:, step * slots : (step + 1) * slots] = placing(
+            slots, runners, members, counts_ref, rank ^ step, False
+        )
+    for side in range(2):
+        own_ref[side] = placing(slots, runners, members, counts_ref, rank ^ (1 - side), True)
+
+
 def triangles(members):
     half = members // 2
     row = lax.broadcasted_iota(jnp.int32, (half, half), 0)
@@ -201,11 +284,11 @@
 
 
 def gram_kernel(slots, runners, members, counts_ref, rank_ref, *refs):
-    seen_refs, (value_ref, weight_ref, out_ref) = refs[:runners], refs[runners:]
+    seen_refs, (both_ref, place_ref, out_ref) = refs[:runners], refs[runners:]
     rank = rank_ref[0]
     counts = [counts_ref[rank ^ step] for step in range(runners)]
     own_means = [joined(ref[slots:, :], 0) for ref in seen_refs]
-    width = value_ref.shape[1]
+    width = both_ref.shape[1]
     mean = 0.0
     for row, count in zip(own_means, counts):
         mean = mean + row * as_row(count, width)
@@ -215,34 +298,30 @@
         live = lax.broadcasted_iota(jnp.int32, (slots, width), 0) < counts[step]
         part = ref[:slots, :].astype(F32) + (own_means[step] - mean)
         part = jnp.where(live, part, 0.0).astype(BF16)
-        place = placing(slots, runners, members, counts_ref, rank ^ step, False)
+        place = place_ref[:, step * slots : (step + 1) * slots]
         observed = observed + jnp.dot(place, part, preferred_element_type=F32)
-    weighted = (observed * weight_ref[...]).astype(BF16)
+    weighted = (observed * both_ref[1:2, :]).astype(BF16)
     across = (((1,), (1,)), ((), ()))
     gram = lax.dot_general(
         weighted, observed.astype(BF16), across, preferred_element_type=F32
     )
-    innovation = stacked(pieces(value_ref[...] - mean), PAD)
+    innovation = stacked(pieces(both_ref[0:1, :] - mean), PAD)
     bias = lax.dot_general(innovation, weighted, across, preferred_element_type=F32)
     half, row, column = triangles(members)
     last = gram[half:, half:]
-    out_ref[:half, :half] = jnp.where(row >= column, gram[:half, :half], last)
-    out_ref[:half, half:] = gram[:half, half:]
+    out_ref[:half, :half] = jnp.where(row >= column, gram[:half, :half], last).astype(BF16)
+    out_ref[:half, half:] = gram[:half, half:].astype(BF16)
     diagonal = jnp.sum(jnp.where(row == column, last, 0.0), axis=0, keepdims=True)
     diagonal = jnp.concatenate([diagonal, jnp.zeros_like(diagonal)], axis=1)
-    out_ref[half:, :] = stacked([bias[0:1] + bias[1:2] + bias[2:3], diagonal], 8, F32)
+    out_ref[half:, :] = stacked([*pieces(joined(bias, 0)), *pieces(diagonal)], PAD)
 
 
 def total_of(half, part_refs):
     packed, bias, diagonal = 0.0, 0.0, 0.0
     for ref in part_refs:
         packed = packed + ref[:half, :].astype(F32)
-        if ref.dtype == BF16:
-            bias = bias + joined(ref[half:, :], 0)
-            diagonal = diagonal + joined(ref[half:, :], 3)
-        else:
-            bias = bias + ref[half : half + 1, :]
-            diagonal = diagonal + ref[half + 1 : half + 2, :]
+        bias = bias + joined(ref[half:, :], 0)
+        diagonal = diagonal + joined(ref[half:, :], 3)
     return packed, bias, diagonal
 
 
@@ -253,9 +332,8 @@
     out_ref[half:, :] = stacked([*pieces(bias), *pieces(diagonal)], PAD)
 
 
-def transform_kernel(slots, runners, members, counts_ref, rank_ref, *refs):
-    part_refs, out_refs = refs[:-2], refs[-2:]
-    rank = rank_ref[0]
+def transform_kernel(slots, members, *refs):
+    part_refs, (place_ref, own_ref), out_refs = refs[:-4], refs[-4:-2], refs[-2:]
     half, row, column = triangles(members)
     packed, bias, diagonal = total_of(half, part_refs)
     corner, side = packed[:, :half], packed[:, half:]
@@ -299,16 +377,13 @@
         + 0.375 * square.astype(F32)
         - 0.3125 * cubed
     ).astype(BF16)
-    places = [
-        placing(slots, runners, members, counts_ref, rank ^ step, False)
-        for step in range(0, runners, 2)
-    ]
     shift = stacked(pieces(shift), PAD)
     for side, out_ref in enumerate(out_refs):
-        own = placing(slots, runners, members, counts_ref, rank ^ (1 - side), True)
-        rows = jnp.dot(own, transform, preferred_element_type=F32).astype(BF16)
+        rows = jnp.dot(own_ref[side], transform, preferred_element_type=F32).astype(BF16)
         left = jnp.concatenate([rows, shift], axis=0)
-        for index, place in enumerate(places):
+        for index in range(out_ref.shape[1] // slots):
+            step = index if side else 2 * index
+            place = place_ref[:, step * slots : (step + 1) * slots]
             out_ref[:, index * slots : (index + 1) * slots] = jnp.dot(
                 left, place, preferred_element_type=F32
             ).astype(BF16)
@@ -327,44 +402,63 @@
     return own_means, mean * (1.0 / members)
 
 
-def product_kernel(slots, members, runners, with_mean, counts_ref, rank_ref, left_ref, *refs):
-    parts = len(refs) - runners
-    parts = parts // (runners // 2 + 1)
-    seen_refs, cell_refs, out_refs = refs[:runners], refs[runners:-parts], refs[-parts:]
+def product_kernel(slots, members, runners, plan, stride, counts_ref, rank_ref, left_ref, *refs):
+    seen_refs, refs = refs[:runners], refs[runners:]
+    cell_refs, out_refs = refs[: -len(plan)], refs[-len(plan) :]
     width = out_refs[0].shape[1]
     own_means, mean = own_means_of(
-        slots, members, counts_ref, rank_ref[0], seen_refs, width * parts
-    )
-    lefts = [
-        left_ref[:, index * slots : (index + 1) * slots] for index in range(runners // 2)
-    ]
-    sums = [jnp.sum(left.astype(F32), axis=1, keepdims=True) for left in lefts]
-    for part, out_ref in enumerate(out_refs):
+        slots, members, counts_ref, rank_ref[0], seen_refs, width * PARTS
+    )
+    lefts, sums = {}, {}
+    for step in range(0, runners, stride):
+        first = step // stride * slots
+        lefts[step] = left_ref[:, first : first + slots]
+        sums[step] = jnp.sum(lefts[step].astype(F32), axis=1, keepdims=True)
+    place = 0
+    for (part, steps), out_ref in zip(plan, out_refs):
         span = slice(part * width, (part + 1) * width)
         total = 0.0
-        for index, left in enumerate(lefts):
+        for step in steps:
             total = total + jnp.dot(
-                left, cell_refs[index * parts + part][...], preferred_element_type=F32
+                lefts[step], cell_refs[place][...], preferred_element_type=F32
             )
-            total = total + sums[index] * (own_means[2 * index] - mean)[:, span]
+            total = total + sums[step] * (own_means[step] - mean)[:, span]
+            place = place + 1
         shift = joined(total[slots:], 0)
-        if with_mean:
+        if stride == 1:
             shift = shift + mean[:, span]
         out_ref[...] = (total[:slots] + shift).astype(out_ref.dtype)
 
 
 def final_kernel(slots, rows, counts_ref, rank_ref, *refs):
-    own_refs, other_refs, out_ref = refs[: len(refs) // 2], refs[len(refs) // 2 : -1], refs[-1]
+    own_refs, refs = refs[:PARTS], refs[PARTS:]
+    other_refs, (out_hbm, out_ref, sems) = refs[:-3], refs[-3:]
     columns = out_ref.shape[1]
-    live = lax.broadcasted_iota(jnp.int32, (slots, columns), 0) < counts_ref[rank_ref[0]]
-    row = 0
-    for own_ref, other_ref in zip(own_refs, other_refs):
-        for first in range(0, own_ref.shape[1], columns):
-            span = slice(first, first + columns)
-            out_ref[pl.ds(row, slots, stride=rows), :] = jnp.where(
-                live, own_ref[:, span] + other_ref[:, span].astype(F32), 0.0
-            )
-            row = row + 1
+    count = counts_ref[rank_ref[0]]
+    chunk = slots // WRITES
+    copies = []
+    for index in range(WRITES):
+        start = index * chunk
+        live = lax.broadcasted_iota(jnp.int32, (chunk, columns), 0) + start < count
+        row = 0
+        for part, own_ref in enumerate(own_refs):
+            for first in range(0, own_ref.shape[1], columns):
+                span = slice(first, first + columns)
+                total = own_ref[start : start + chunk, span]
+                if part >= GATHERED:
+                    other = other_refs[part - GATHERED][start : start + chunk, span]
+                    total = total + other.astype(F32)
+                out_ref[pl.ds(start * rows + row, chunk, stride=rows), :] = jnp.where(
+                    live, total, 0.0
+                )
+                row = row + 1
+        span = pl.ds(start * rows, chunk * rows)
+        copies.append(
+            pltpu.make_async_copy(out_ref.at[span], out_hbm.at[span], sems.at[index])
+        )
+        copies[-1].start()
+    for copy in copies:
+        copy.wait()
 
 
 def body(states, diffusivity, velocity, counts, obs_index, obs_value, obs_weight):
@@ -381,36 +475,47 @@
     shape = jax.ShapeDtypeStruct
 
     rank = lax.axis_index("runner").astype(jnp.int32).reshape(1)
-    parity = rank[0] % shares
-    flat = states.reshape(slots * rows, columns)
-    fields = jnp.concatenate([diffusivity[None], velocity], axis=0)
-    last, first = call(
+    last, first, flat, fields = call(
         functools.partial(edge_kernel, slots, rows),
-        [shape((STEPS, height, columns), BF16)] * 2,
+        [shape((STEPS, height, columns), BF16)] * 2
+        + [shape((slots * rows, columns), F32), shape((3, rows, columns), F32)],
         [],
-        [flat, fields],
+        [states.reshape(slots * rows, columns), diffusivity, velocity],
+        [pltpu.SemaphoreType.DMA((3,))],
+        outside=True,
     )
     forward = [(i, (i + 1) % blocks) for i in range(blocks)]
     backward = [(target, source) for source, target in forward]
     low = lax.ppermute(last, "cells", forward)
     high = lax.ppermute(first, "cells", backward)
-
-    def own_first(array):
-        return jnp.where(parity == 0, array, jnp.roll(array, -share))
-
-    pick = (
-        lax.broadcasted_iota(jnp.int32, (cells, seen), 0) == own_first(obs_index)[None, :]
-    ).astype(BF16)
-    own_value = own_first(obs_value)[None, :share]
-    own_weight = own_first(obs_weight)[None, :share]
-
+    pick, both, place, own = call(
+        functools.partial(setup_kernel, slots, runners, members, shares),
+        [
+            shape((cells, seen), BF16),
+            shape((8, share), F32),
+            shape((members, runners * slots), BF16),
+            shape((2, slots, members), BF16),
+        ],
+        [counts, rank],
+        [obs_index[None, :], obs_value[None, :], obs_weight[None, :]],
+    )
+
+    coefs, inner = call(
+        functools.partial(inner_kernel, slots, rows),
+        [
+            shape((rows, 5, 8, columns), F32),
+            shape((sum(len(inside) for inside in inner_rows(rows)), slots, columns), F32),
+        ],
+        [],
+        [flat, fields],
+    )
     lower = -(-(3 + 3 * (cells // share)) // PAD) * PAD
     kept, given, *own_cells = call(
         functools.partial(forecast_kernel, slots, rows, shares),
         [shape((slots + lower, share), BF16)] * shares
         + [shape((slots, cells // PARTS), BF16)] * PARTS,
         [counts, rank],
-        [flat, low, high, fields, pick],
+        [flat, low, high, coefs, inner, pick],
         [
             pltpu.VMEM((rows + 2 * STEPS, 5, 8, columns), F32),
             pltpu.VMEM((rows, slots, columns), F32),
@@ -418,8 +523,10 @@
         ],
     )
 
-    def moved(array, bit, axis="runner"):
-        return lax.ppermute(array, axis, partners(lax.axis_size(axis), bit))
+    def moved(array, runner_bit, block_bit=0):
+        count = runners * blocks
+        step = runner_bit * blocks + block_bit
+        return lax.ppermute(array, ("runner", "cells"), partners(count, step))
 
     all_seen = [kept] + [
         moved(given if step % shares else kept, step)
@@ -431,22 +538,25 @@
         for step in list(all_cells):
             all_cells[step + bit] = [moved(array, bit) for array in all_cells[step]]
         bit = bit // 2
-    held = [array for step in sorted(all_cells) for array in all_cells[step]]
+    even = sorted(all_cells)
+    for part in range(GATHERED):
+        for step in even:
+            all_cells.setdefault(step + 1, []).append(moved(all_cells[step][part], 1))
 
     part = call(
         functools.partial(gram_kernel, slots, runners, members),
-        shape((half + 8, members), F32),
+        shape((half + PAD, members), BF16),
         [counts, rank],
-        [*all_seen, own_value, own_weight],
-    )
-    stages = [("cells", [1]), ("runner", [1])]
+        [*all_seen, both, place],
+    )
+    stages = [[(0, 1)], [(1, 0)]]
     width = 2
     while width < blocks:
         reach = min(4, blocks // width)
-        stages.append(("cells", [width * step for step in range(1, reach)]))
+        stages.append([(0, width * step) for step in reversed(range(1, reach))])
         width = width * reach
-    for index, (axis, stage) in enumerate(stages):
-        parts = [part] + [moved(part, step, axis) for step in stage]
+    for index, stage in enumerate(stages):
+        parts = [part] + [moved(part, r, c) for r, c in stage]
         if index + 1 < len(stages):
             part = call(
                 functools.partial(sum_kernel, half),
@@ -455,29 +565,34 @@
                 parts,
             )
     give, keep = call(
-        functools.partial(transform_kernel, slots, runners, members),
-        [shape((height, runners // 2 * slots), BF16)] * 2,
-        [counts, rank],
-        parts,
-    )
-    given_products = call(
-        functools.partial(product_kernel, slots, members, runners, False),
-        [shape((slots, cells // PARTS), BF16)] * PARTS,
-        [counts, rank],
-        [give, *all_seen, *held],
-    )
-    other_products = [moved(array, 1) for array in given_products]
-    own_products = call(
-        functools.partial(product_kernel, slots, members, runners, True),
-        [shape((slots, cells // PARTS), F32)] * PARTS,
-        [counts, rank],
-        [keep, *all_seen, *held],
-    )
+        functools.partial(transform_kernel, slots, members),
+        [
+            shape((height, runners // 2 * slots), BF16),
+            shape((height, runners * slots), BF16),
+        ],
+        [],
+        [*parts, place, own],
+    )
+
+    def product(left, plan, stride, dtype):
+        return call(
+            functools.partial(product_kernel, slots, members, runners, plan, stride),
+            [shape((slots, cells // PARTS), dtype)] * len(plan),
+            [counts, rank],
+            [left, *all_seen] + [all_cells[step][part] for part, steps in plan for step in steps],
+        )
+
+    shared = [(part, even) for part in range(GATHERED, PARTS)]
+    other_products = [moved(array, 1) for array in product(give, shared, 2, BF16)]
+    whole = [(part, sorted(all_cells)) for part in range(GATHERED)]
+    own_products = product(keep, whole + shared, 1, F32)
     analysed = call(
         functools.partial(final_kernel, slots, rows),
         shape((slots * rows, columns), F32),
         [counts, rank],
         [*own_products, *other_products],
+        [pltpu.VMEM((slots * rows, columns), F32), pltpu.SemaphoreType.DMA((WRITES,))],
+        write=True,
     )
     return analysed.reshape(slots, rows, columns)
 

time: 51.9 us -> 49.6 us (0.956)
  waiting for transfers between devices: 21.7 us -> 18.9 us
  Pallas kernels: 8.88 us -> 10.8 us
  other arithmetic: 1.87 us -> 0 us
  starting transfers between devices: 17.2 us -> 18.9 us
  local copies, waits for them, and re-layouts: 1.83 us -> 0.67 us
    ppermute x12 -> x13, waiting for transfers between devices: 20.4 us -> 18.2 us  [moved(): return lax.ppermute(array, ('runner', 'cells'), partners(count, step))]
    pallas_call x9 -> x11, Pallas kernels: 8.88 us -> 10.8 us  [call(): pl.pallas_call(kernel, out_shape=out_shape, in_specs=[scalar] * len(scala...]
    ppermute x12 -> x13, starting transfers between devices: 13.8 us -> 15.4 us  [moved(): return lax.ppermute(array, ('runner', 'cells'), partners(count, step))]
    slice x5 -> x0, local copies, waits for them, and re-layouts: 0.78 us -> none  [the longest x3 0.77 us: own_first(): return jnp.where(parity == 0, array, jnp.roll(array, -share))]
    concatenate x1 -> x0, other arithmetic: 0.75 us -> none  [body(): fields = jnp.concatenate([diffusivity[None], velocity], axis=0)]
    select_n x2 -> x0, other arithmetic: 0.7 us -> none  [own_first(): return jnp.where(parity == 0, array, jnp.roll(array, -share))]
    ppermute x1, waiting for transfers between devices: 0.84 us -> 0.28 us  [body(): low = lax.ppermute(last, 'cells', forward)]
    unnamed x10 -> x8, local copies, waits for them, and re-layouts: 1.06 us -> 0.67 us
  transfers between devices with their start and end apart: 14 -> 15, of which waited for: 11 -> 10; matrix products, arithmetic and copies ran while one was open for 4% -> 0% of each run, Pallas kernels for 5% -> 9%
where the time goes in v1:
time: 49.6 us; the launch traced here: 49.4 us
  starting transfers between devices  18.9 us (38%)
  waiting for transfers between devices  18.9 us (38%)
  Pallas kernels  10.8 us (22%)
  local copies, waits for them, and re-layouts  0.67 us (1%)
    ppermute x13, waiting for transfers between devices, moved(): return lax.ppermute(array, ('runner', 'cells'), partners(count, step))  18.2 us
    ppermute x13, starting transfers between devices, moved(): return lax.ppermute(array, ('runner', 'cells'), partners(count, step))  15.4 us
    pallas_call x11, Pallas kernels, call(): pl.pallas_call(kernel, out_shape=out_shape, in_specs=[scalar] * len(scala...  10.8 us
    ppermute x1, starting transfers between devices, body(): high = lax.ppermute(first, 'cells', backward)  2.93 us
  transfers between devices with their start and end apart: 15, of which 10 were waited for; matrix products, arithmetic and copies ran while one was open for 0% of the time, Pallas kernels for 9%

profile of v1, /device:TPU:0, one launch (start us, length us, event | category | flops | bytes accessed | tf_op | source)
XLA Modules:
  0.0 49.4 jit_solution(4816137633554477064)
XLA Ops:
  0.0 1.2 %shard_map.73 = (bf16[4,144,128]{2,1,0:T(8,128)(2,1)S(1)}, bf16[4,144,128]{2,1,0:T(8,128)(2,1)S(1)}, f32[1024,128]{1,0:T(8,128)S(1)}, f32[3,8,128]{2,1,0:T(8,128)S(1)}) custom-call(f32[1024,128]{1,0:T(8,128)} %bitcast.9, f32[8,128]{1,0:T(8,128)} %diff_hbm.1, f32[2,8,128]{2,1,0:T(8,128)} %vel_hbm.1), custom_call_target="tpu_custom_call" | custom-call | bytes 1048576 | tf_op jit(solution)/shard_map/pallas_call | solution.py:73
  1.2 0.5 %collective-permute-start = (bf16[4,144,128]{2,1,0:T(8,128)(2,1)S(1)}, bf16[4,144,128]{2,1,0:T(8,128)(2,1)S(1)}, u32[]{:S(2)}, u32[]{:S(2)}) collective-permute-start(bf16[4,144,128]{2,1,0:T(8,128)(2,1)S(1)} %get-tuple-element.24), channel_id=1, source_target_pairs={{0,1},{1,2},{2,3},{3,4},{4,5},{5,6},{6,7},{7,0},{8,9},{9,10},{10,1... | collective-permute-start | bytes 442376 | tf_op jit(solution)/shard_map/ppermute | solution.py:489
  1.7 2.9 %collective-permute-start.1 = (bf16[4,144,128]{2,1,0:T(8,128)(2,1)S(1)}, bf16[4,144,128]{2,1,0:T(8,128)(2,1)S(1)}, u32[]{:S(2)}, u32[]{:S(2)}) collective-permute-start(bf16[4,144,128]{2,1,0:T(8,128)(2,1)S(1)} %get-tuple-element.25), channel_id=1, source_target_pairs={{1,0},{2,1},{3,2},{4,3},{5,4},{6,5},{7,6},{0,7},{9,8},{10,9},{11,1... | collective-permute-start | bytes 442376 | tf_op jit(solution)/shard_map/ppermute | solution.py:490
  4.7 0.0 copy-start.3
  4.7 0.9 %shard_map.74 = (f32[8,5,8,128]{3,2,1,0:T(8,128)S(1)}, f32[12,128,128]{2,1,0:T(8,128)S(1)}) custom-call(f32[1024,128]{1,0:T(8,128)S(1)} %get-tuple-element.23.states_ref, f32[3,8,128]{2,1,0:T(8,128)S(1)} %get-tuple-element.26.fields_ref), custom_call_target="tpu_custom_call" | custom-call | bytes 1048576 | tf_op jit(solution)/shard_map/pallas_call | solution.py:73
  5.6 0.0 copy-start.2
  5.6 0.0 copy-start.1
  5.6 0.0 copy-start
  5.6 0.0 copy-done.3
  5.7 0.6 %copy-done.2 = f32[512]{0:T(512)S(1)} copy-done((f32[512]{0:T(512)S(1)}, f32[512]{0:T(512)}, u32[]{:S(2)}) %copy-start.2) | copy-done | bytes 2072
  6.3 0.0 copy-done.1
  6.3 0.0 copy-done
  6.3 0.8 %shard_map.75 = (bf16[1024,512]{1,0:T(8,128)(2,1)S(1)}, f32[8,256]{1,0:T(8,128)S(1)}, bf16[256,512]{1,0:T(8,128)(2,1)S(1)}, bf16[2,128,256]{2,1,0:T(8,128)(2,1)S(1)}) custom-call(s32[4]{0:T(128)S(1)} %copy-done, s32[1]{0:T(128)} %bitcast.rank_ref, s32[1,512]{1,0:T(1,128)S(1)} %bitcast.6, f32[1,512]{1,0:T(1,128)S(1)} %bitcast.7, f32[1,512]{1,0:T(1,128)S(1)} %bitcast.8), custom_call_target="tpu_custom_call" | custom-call | bytes 1048576 | tf_op jit(solution)/shard_map/pallas_call | solution.py:73
  7.1 0.3 collective-permute-done.low_ref
  7.4 0.4 collective-permute-done.1.high_ref
  7.9 2.5 %shard_map.76 = (bf16[144,256]{1,0:T(8,128)(2,1)S(1)}, bf16[144,256]{1,0:T(8,128)(2,1)S(1)}, bf16[128,512]{1,0:T(8,128)(2,1)S(1)}, bf16[128,512]{1,0:T(8,128)(2,1)S(1)}) custom-call(s32[4]{0:T(128)S(1)} %copy-done, s32[1]{0:T(128)} %bitcast.rank_ref, f32[1024,128]{1,0:T(8,128)S(1)} %get-tuple-element.23.states_ref, ...), custom_call_target="tpu_custom_call" | custom-call | bytes 1048576 | tf_op jit(solution)/shard_map/pallas_call | solution.py:73
  10.4 4.0 %collective-permute-start.4 = (bf16[144,256]{1,0:T(8,128)(2,1)S(1)}, bf16[144,256]{1,0:T(8,128)(2,1)S(1)}, u32[]{:S(2)}, u32[]{:S(2)}) collective-permute-start(bf16[144,256]{1,0:T(8,128)(2,1)S(1)} %get-tuple-element.31), channel_id=1, source_target_pairs={{0,24},{1,25},{2,26},{3,27},{4,28},{5,29},{6,30},{7,31},{8,16},{9,... | collective-permute-start | bytes 221192 | tf_op jit(solution)/shard_map/ppermute | solution.py:529
  14.4 0.0 collective-permute-start.2
  14.4 0.6 %collective-permute-start.3 = (bf16[144,256]{1,0:T(8,128)(2,1)S(1)}, bf16[144,256]{1,0:T(8,128)(2,1)S(1)}, u32[]{:S(2)}, u32[]{:S(2)}) collective-permute-start(bf16[144,256]{1,0:T(8,128)(2,1)S(1)} %get-tuple-element.30.refs_0_), channel_id=1, source_target_pairs={{0,16},{1,17},{2,18},{3,19},{4,20},{5,21},{6,22},{7,23},{8,24},{9,... | collective-permute-start | bytes 221192 | tf_op jit(solution)/shard_map/ppermute | solution.py:529
  15.0 1.8 %collective-permute-done.4.refs_3_ = bf16[144,256]{1,0:T(8,128)(2,1)S(1)} collective-permute-done((bf16[144,256]{1,0:T(8,128)(2,1)S(1)}, bf16[144,256]{1,0:T(8,128)(2,1)S(1)}, u32[]{:S(2)}, u32[]{:S(2)}) %collective-permute-start.4) | collective-permute-done | bytes 73760 | tf_op jit(solution)/shard_map/ppermute | solution.py:529
  16.8 4.1 %collective-permute-done.2.refs_1_ = bf16[144,256]{1,0:T(8,128)(2,1)S(1)} collective-permute-done((bf16[144,256]{1,0:T(8,128)(2,1)S(1)}, bf16[144,256]{1,0:T(8,128)(2,1)S(1)}, u32[]{:S(2)}, u32[]{:S(2)}) %collective-permute-start.2) | collective-permute-done | bytes 73760 | tf_op jit(solution)/shard_map/ppermute | solution.py:529
  21.0 0.0 collective-permute-done.3.refs_2_
  21.0 1.1 %shard_map.77.refs_0_ = bf16[144,256]{1,0:T(8,128)(2,1)S(1)} custom-call(s32[4]{0:T(128)S(1)} %copy-done, s32[1]{0:T(128)} %bitcast.rank_ref, bf16[144,256]{1,0:T(8,128)(2,1)S(1)} %get-tuple-element.30.refs_0_, bf16[144,256]{1,0:T(8,128)(2,1)S(1)} %collective-permute-done.2.refs_1_, bf16[144,256]{1,0:T(8,128)(2,1)S(1)} %collective-permute-done.3.refs_2_, ...), custom_call_target="tpu_custom_call" | custom-call | bytes 1048576 | tf_op jit(solution)/shard_map/pallas_call | solution.py:73
  22.1 0.9 %collective-permute-start.5 = (bf16[144,256]{1,0:T(8,128)(2,1)S(1)}, bf16[144,256]{1,0:T(8,128)(2,1)S(1)}, u32[]{:S(2)}, u32[]{:S(2)}) collective-permute-start(bf16[144,256]{1,0:T(8,128)(2,1)S(1)} %shard_map.77.refs_0_), channel_id=1, source_target_pairs={{0,1},{1,0},{2,3},{3,2},{4,5},{5,4},{6,7},{7,6},{8,9},{9,8},{10,11... | collective-permute-start | bytes 221192 | tf_op jit(solution)/shard_map/ppermute | solution.py:529
  23.1 0.9 %collective-permute-done.5.refs_1_ = bf16[144,256]{1,0:T(8,128)(2,1)S(1)} collective-permute-done((bf16[144,256]{1,0:T(8,128)(2,1)S(1)}, bf16[144,256]{1,0:T(8,128)(2,1)S(1)}, u32[]{:S(2)}, u32[]{:S(2)}) %collective-permute-start.5) | collective-permute-done | bytes 73760 | tf_op jit(solution)/shard_map/ppermute | solution.py:529
  24.0 1.0 %collective-permute-start.6 = (bf16[144,256]{1,0:T(8,128)(2,1)S(1)}, bf16[144,256]{1,0:T(8,128)(2,1)S(1)}, u32[]{:S(2)}, u32[]{:S(2)}) collective-permute-start(bf16[144,256]{1,0:T(8,128)(2,1)S(1)} %shard_map.78.refs_0_), channel_id=1, source_target_pairs={{0,8},{1,9},{2,10},{3,11},{4,12},{5,13},{6,14},{7,15},{8,0},{9,1},... | collective-permute-start | bytes 221192 | tf_op jit(solution)/shard_map/ppermute | solution.py:529
  25.0 1.4 %collective-permute-start.11 = (bf16[128,512]{1,0:T(8,128)(2,1)S(1)}, bf16[128,512]{1,0:T(8,128)(2,1)S(1)}, u32[]{:S(2)}, u32[]{:S(2)}) collective-permute-start(bf16[128,512]{1,0:T(8,128)(2,1)S(1)} %get-tuple-element.36.refs_4_), channel_id=1, source_target_pairs={{0,16},{1,17},{2,18},{3,19},{4,20},{5,21},{6,22},{7,23},{8,24},{9,... | collective-permute-start | bytes 393224 | tf_op jit(solution)/shard_map/ppermute | solution.py:529
  26.5 1.5 %collective-permute-start.13 = (bf16[128,512]{1,0:T(8,128)(2,1)S(1)}, bf16[128,512]{1,0:T(8,128)(2,1)S(1)}, u32[]{:S(2)}, u32[]{:S(2)}) collective-permute-start(bf16[128,512]{1,0:T(8,128)(2,1)S(1)} %get-tuple-element.37.refs_8_.refs_4_), channel_id=1, source_target_pairs={{0,16},{1,17},{2,18},{3,19},{4,20},{5,21},{6,22},{7,23},{8,24},{9,... | collective-permute-start | bytes 393224 | tf_op jit(solution)/shard_map/ppermute | solution.py:529
  27.9 1.5 %collective-permute-done.6.refs_1_ = bf16[144,256]{1,0:T(8,128)(2,1)S(1)} collective-permute-done((bf16[144,256]{1,0:T(8,128)(2,1)S(1)}, bf16[144,256]{1,0:T(8,128)(2,1)S(1)}, u32[]{:S(2)}, u32[]{:S(2)}) %collective-permute-start.6) | collective-permute-done | bytes 73760 | tf_op jit(solution)/shard_map/ppermute | solution.py:529
  29.5 1.6 %collective-permute-start.9 = (bf16[144,256]{1,0:T(8,128)(2,1)S(1)}, bf16[144,256]{1,0:T(8,128)(2,1)S(1)}, u32[]{:S(2)}, u32[]{:S(2)}) collective-permute-start(bf16[144,256]{1,0:T(8,128)(2,1)S(1)} %shard_map.79.refs_0_), channel_id=1, source_target_pairs={{0,2},{1,3},{2,0},{3,1},{4,6},{5,7},{6,4},{7,5},{8,10},{9,11},{10,... | collective-permute-start | bytes 221192 | tf_op jit(solution)/shard_map/ppermute | solution.py:529
  31.2 0.8 %collective-permute-start.8 = (bf16[144,256]{1,0:T(8,128)(2,1)S(1)}, bf16[144,256]{1,0:T(8,128)(2,1)S(1)}, u32[]{:S(2)}, u32[]{:S(2)}) collective-permute-start(bf16[144,256]{1,0:T(8,128)(2,1)S(1)} %shard_map.79.refs_0_), channel_id=1, source_target_pairs={{0,4},{1,5},{2,6},{3,7},{4,0},{5,1},{6,2},{7,3},{8,12},{9,13},{10,... | collective-permute-start | bytes 221192 | tf_op jit(solution)/shard_map/ppermute | solution.py:529
  31.9 1.4 %collective-permute-start.7 = (bf16[144,256]{1,0:T(8,128)(2,1)S(1)}, bf16[144,256]{1,0:T(8,128)(2,1)S(1)}, u32[]{:S(2)}, u32[]{:S(2)}) collective-permute-start(bf16[144,256]{1,0:T(8,128)(2,1)S(1)} %shard_map.79.refs_0_), channel_id=1, source_target_pairs={{0,6},{1,7},{2,4},{3,5},{4,2},{5,3},{6,0},{7,1},{8,14},{9,15},{10,... | collective-permute-start | bytes 221192 | tf_op jit(solution)/shard_map/ppermute | solution.py:529
  33.3 4.4 %collective-permute-done.11.refs_6_ = bf16[128,512]{1,0:T(8,128)(2,1)S(1)} collective-permute-done((bf16[128,512]{1,0:T(8,128)(2,1)S(1)}, bf16[128,512]{1,0:T(8,128)(2,1)S(1)}, u32[]{:S(2)}, u32[]{:S(2)}) %collective-permute-start.11) | collective-permute-done | bytes 131104 | tf_op jit(solution)/shard_map/ppermute | solution.py:529
  37.7 0.0 collective-permute-start.10
  37.7 0.0 collective-permute-done.9.refs_3_
  37.7 2.0 %collective-permute-start.12 = (bf16[128,512]{1,0:T(8,128)(2,1)S(1)}, bf16[128,512]{1,0:T(8,128)(2,1)S(1)}, u32[]{:S(2)}, u32[]{:S(2)}) collective-permute-start(bf16[128,512]{1,0:T(8,128)(2,1)S(1)} %collective-permute-done.11.refs_6_), channel_id=1, source_target_pairs={{0,8},{1,9},{2,10},{3,11},{4,12},{5,13},{6,14},{7,15},{8,0},{9,1},... | collective-permute-start | bytes 393224 | tf_op jit(solution)/shard_map/ppermute | solution.py:529
  39.7 0.0 collective-permute-done.8.refs_2_
  39.7 0.0 collective-permute-done.7.refs_1_
  39.7 1.1 %shard_map.80 = (bf16[144,256]{1,0:T(8,128)(2,1)S(1)}, bf16[144,512]{1,0:T(8,128)(2,1)S(1)}) custom-call(bf16[144,256]{1,0:T(8,128)(2,1)S(1)} %shard_map.79.refs_0_, bf16[144,256]{1,0:T(8,128)(2,1)S(1)} %collective-permute-done.7.refs_1_, bf16[144,256]{1,0:T(8,128)(2,1)S(1)} %collective-permute-done.8.refs_2_, ...), custom_call_target="tpu_custom_call" | custom-call | bytes 1048576 | tf_op jit(solution)/shard_map/pallas_call | solution.py:73
  40.8 0.0 collective-permute-done.13.refs_9_.refs_5_
  40.8 0.8 %shard_map.82 = bf16[128,512]{1,0:T(8,128)(2,1)S(1)} custom-call(s32[4]{0:T(128)S(1)} %copy-done, s32[1]{0:T(128)} %bitcast.rank_ref, bf16[144,256]{1,0:T(8,128)(2,1)S(1)} %get-tuple-element.40.left_ref, bf16[144,256]{1,0:T(8,128)(2,1)S(1)} %get-tuple-element.30.refs_0_, bf16[144,256]{1,0:T(8,128)(2,1)S(1)} %collective-permute-done.2.refs_1_, ...), custom_call_target="tpu_custom_call" | custom-call | bytes 1048576 | tf_op jit(solution)/shard_map/pallas_call | solution.py:73
  41.6 0.1 collective-permute-start.14
  41.7 2.4 %collective-permute-done.10.refs_5_ = bf16[128,512]{1,0:T(8,128)(2,1)S(1)} collective-permute-done((bf16[128,512]{1,0:T(8,128)(2,1)S(1)}, bf16[128,512]{1,0:T(8,128)(2,1)S(1)}, u32[]{:S(2)}, u32[]{:S(2)}) %collective-permute-start.10) | collective-permute-done | bytes 131104 | tf_op jit(solution)/shard_map/ppermute | solution.py:529
  44.1 2.6 %collective-permute-done.12.refs_7_ = bf16[128,512]{1,0:T(8,128)(2,1)S(1)} collective-permute-done((bf16[128,512]{1,0:T(8,128)(2,1)S(1)}, bf16[128,512]{1,0:T(8,128)(2,1)S(1)}, u32[]{:S(2)}, u32[]{:S(2)}) %collective-permute-start.12) | collective-permute-done | bytes 131104 | tf_op jit(solution)/shard_map/ppermute | solution.py:529
  46.6 1.0 %shard_map.81 = (f32[128,512]{1,0:T(8,128)S(1)}, f32[128,512]{1,0:T(8,128)S(1)}) custom-call(s32[4]{0:T(128)S(1)} %copy-done, s32[1]{0:T(128)} %bitcast.rank_ref, bf16[144,512]{1,0:T(8,128)(2,1)S(1)} %get-tuple-element.35.left_ref, bf16[144,256]{1,0:T(8,128)(2,1)S(1)} %get-tuple-element.30.refs_0_, bf16[144,256]{1,0:T(8,128)(2,1)S(1)} %collective-permute-done.2.refs_1_, ...), custom_call_target="tpu_custom_call" | custom-call | bytes 1048576 | tf_op jit(solution)/shard_map/pallas_call | solution.py:73
  47.6 0.4 collective-permute-done.14.refs_2_
  48.0 1.4 %shard_map.83 = f32[1024,128]{1,0:T(8,128)} custom-call(s32[4]{0:T(128)S(1)} %copy-done, s32[1]{0:T(128)} %bitcast.rank_ref, f32[128,512]{1,0:T(8,128)S(1)} %get-tuple-element.38.refs_0_, f32[128,512]{1,0:T(8,128)S(1)} %get-tuple-element.39.refs_1_, bf16[128,512]{1,0:T(8,128)(2,1)S(1)} %collective-permute-done.14.refs_2_), custom_call_target="tpu_custom_call" | custom-call | bytes 1048576 | tf_op jit(solution)/shard_map/pallas_call | solution.py:73
  (2 shorter events, 0.1 us)
Async XLA Ops:
  1.2 6.2 %collective-permute-start = (bf16[4,144,128]{2,1,0:T(8,128)(2,1)S(1)}, bf16[4,144,128]{2,1,0:T(8,128)(2,1)S(1)}, u32[]{:S(2)}, u32[]{:S(2)}) collective-permute-start(bf16[4,144,128]{2,1,0:T(8,128)(2,1)S(1)} %get-tuple-element.24), channel_id=1, source_target_pairs={{0,1},{1,2},{2,3},{3,4},{4,5},{5,6},{6,7},{7,0},{8,9},{9,10},{10,1... | collective-permute-start | bytes 442376 | tf_op jit(solution)/shard_map/ppermute | solution.py:489
  1.7 6.1 %collective-permute-start.1 = (bf16[4,144,128]{2,1,0:T(8,128)(2,1)S(1)}, bf16[4,144,128]{2,1,0:T(8,128)(2,1)S(1)}, u32[]{:S(2)}, u32[]{:S(2)}) collective-permute-start(bf16[4,144,128]{2,1,0:T(8,128)(2,1)S(1)} %get-tuple-element.25), channel_id=1, source_target_pairs={{1,0},{2,1},{3,2},{4,3},{5,4},{6,5},{7,6},{0,7},{9,8},{10,9},{11,1... | collective-permute-start | bytes 442376 | tf_op jit(solution)/shard_map/ppermute | solution.py:490
  4.7 1.0 %copy-start.3 = (f32[512]{0:T(512)S(1)}, f32[512]{0:T(512)}, u32[]{:S(2)}) copy-start(f32[512]{0:T(512)} %param.13) | copy-start | bytes 6148
  5.6 0.7 %copy-start.2 = (f32[512]{0:T(512)S(1)}, f32[512]{0:T(512)}, u32[]{:S(2)}) copy-start(f32[512]{0:T(512)} %param.12) | copy-start | bytes 6148
  5.6 0.7 %copy-start.1 = (s32[512]{0:T(512)S(1)}, s32[512]{0:T(512)}, u32[]{:S(2)}) copy-start(s32[512]{0:T(512)} %param.11) | copy-start | bytes 6148
  5.6 0.7 %copy-start = (s32[4]{0:T(128)S(1)}, s32[4]{0:T(128)}, u32[]{:S(2)}) copy-start(s32[4]{0:T(128)} %counts_ref.11) | copy-start | bytes 52
  10.4 6.4 %collective-permute-start.4 = (bf16[144,256]{1,0:T(8,128)(2,1)S(1)}, bf16[144,256]{1,0:T(8,128)(2,1)S(1)}, u32[]{:S(2)}, u32[]{:S(2)}) collective-permute-start(bf16[144,256]{1,0:T(8,128)(2,1)S(1)} %get-tuple-element.31), channel_id=1, source_target_pairs={{0,24},{1,25},{2,26},{3,27},{4,28},{5,29},{6,30},{7,31},{8,16},{9,... | collective-permute-start | bytes 221192 | tf_op jit(solution)/shard_map/ppermute | solution.py:529
  14.4 6.6 %collective-permute-start.2 = (bf16[144,256]{1,0:T(8,128)(2,1)S(1)}, bf16[144,256]{1,0:T(8,128)(2,1)S(1)}, u32[]{:S(2)}, u32[]{:S(2)}) collective-permute-start(bf16[144,256]{1,0:T(8,128)(2,1)S(1)} %get-tuple-element.31), channel_id=1, source_target_pairs={{0,8},{1,9},{2,10},{3,11},{4,12},{5,13},{6,14},{7,15},{8,0},{9,1},... | collective-permute-start | bytes 221192 | tf_op jit(solution)/shard_map/ppermute | solution.py:529
  14.4 6.6 %collective-permute-start.3 = (bf16[144,256]{1,0:T(8,128)(2,1)S(1)}, bf16[144,256]{1,0:T(8,128)(2,1)S(1)}, u32[]{:S(2)}, u32[]{:S(2)}) collective-permute-start(bf16[144,256]{1,0:T(8,128)(2,1)S(1)} %get-tuple-element.30.refs_0_), channel_id=1, source_target_pairs={{0,16},{1,17},{2,18},{3,19},{4,20},{5,21},{6,22},{7,23},{8,24},{9,... | collective-permute-start | bytes 221192 | tf_op jit(solution)/shard_map/ppermute | solution.py:529
  22.1 1.9 %collective-permute-start.5 = (bf16[144,256]{1,0:T(8,128)(2,1)S(1)}, bf16[144,256]{1,0:T(8,128)(2,1)S(1)}, u32[]{:S(2)}, u32[]{:S(2)}) collective-permute-start(bf16[144,256]{1,0:T(8,128)(2,1)S(1)} %shard_map.77.refs_0_), channel_id=1, source_target_pairs={{0,1},{1,0},{2,3},{3,2},{4,5},{5,4},{6,7},{7,6},{8,9},{9,8},{10,11... | collective-permute-start | bytes 221192 | tf_op jit(solution)/shard_map/ppermute | solution.py:529
  24.0 5.5 %collective-permute-start.6 = (bf16[144,256]{1,0:T(8,128)(2,1)S(1)}, bf16[144,256]{1,0:T(8,128)(2,1)S(1)}, u32[]{:S(2)}, u32[]{:S(2)}) collective-permute-start(bf16[144,256]{1,0:T(8,128)(2,1)S(1)} %shard_map.78.refs_0_), channel_id=1, source_target_pairs={{0,8},{1,9},{2,10},{3,11},{4,12},{5,13},{6,14},{7,15},{8,0},{9,1},... | collective-permute-start | bytes 221192 | tf_op jit(solution)/shard_map/ppermute | solution.py:529
  25.0 12.7 %collective-permute-start.11 = (bf16[128,512]{1,0:T(8,128)(2,1)S(1)}, bf16[128,512]{1,0:T(8,128)(2,1)S(1)}, u32[]{:S(2)}, u32[]{:S(2)}) collective-permute-start(bf16[128,512]{1,0:T(8,128)(2,1)S(1)} %get-tuple-element.36.refs_4_), channel_id=1, source_target_pairs={{0,16},{1,17},{2,18},{3,19},{4,20},{5,21},{6,22},{7,23},{8,24},{9,... | collective-permute-start | bytes 393224 | tf_op jit(solution)/shard_map/ppermute | solution.py:529
  26.5 14.3 %collective-permute-start.13 = (bf16[128,512]{1,0:T(8,128)(2,1)S(1)}, bf16[128,512]{1,0:T(8,128)(2,1)S(1)}, u32[]{:S(2)}, u32[]{:S(2)}) collective-permute-start(bf16[128,512]{1,0:T(8,128)(2,1)S(1)} %get-tuple-element.37.refs_8_.refs_4_), channel_id=1, source_target_pairs={{0,16},{1,17},{2,18},{3,19},{4,20},{5,21},{6,22},{7,23},{8,24},{9,... | collective-permute-start | bytes 393224 | tf_op jit(solution)/shard_map/ppermute | solution.py:529
  29.5 8.2 %collective-permute-start.9 = (bf16[144,256]{1,0:T(8,128)(2,1)S(1)}, bf16[144,256]{1,0:T(8,128)(2,1)S(1)}, u32[]{:S(2)}, u32[]{:S(2)}) collective-permute-start(bf16[144,256]{1,0:T(8,128)(2,1)S(1)} %shard_map.79.refs_0_), channel_id=1, source_target_pairs={{0,2},{1,3},{2,0},{3,1},{4,6},{5,7},{6,4},{7,5},{8,10},{9,11},{10,... | collective-permute-start | bytes 221192 | tf_op jit(solution)/shard_map/ppermute | solution.py:529
  31.2 8.6 %collective-permute-start.8 = (bf16[144,256]{1,0:T(8,128)(2,1)S(1)}, bf16[144,256]{1,0:T(8,128)(2,1)S(1)}, u32[]{:S(2)}, u32[]{:S(2)}) collective-permute-start(bf16[144,256]{1,0:T(8,128)(2,1)S(1)} %shard_map.79.refs_0_), channel_id=1, source_target_pairs={{0,4},{1,5},{2,6},{3,7},{4,0},{5,1},{6,2},{7,3},{8,12},{9,13},{10,... | collective-permute-start | bytes 221192 | tf_op jit(solution)/shard_map/ppermute | solution.py:529
  31.9 7.8 %collective-permute-start.7 = (bf16[144,256]{1,0:T(8,128)(2,1)S(1)}, bf16[144,256]{1,0:T(8,128)(2,1)S(1)}, u32[]{:S(2)}, u32[]{:S(2)}) collective-permute-start(bf16[144,256]{1,0:T(8,128)(2,1)S(1)} %shard_map.79.refs_0_), channel_id=1, source_target_pairs={{0,6},{1,7},{2,4},{3,5},{4,2},{5,3},{6,0},{7,1},{8,14},{9,15},{10,... | collective-permute-start | bytes 221192 | tf_op jit(solution)/shard_map/ppermute | solution.py:529
  37.7 6.4 %collective-permute-start.10 = (bf16[128,512]{1,0:T(8,128)(2,1)S(1)}, bf16[128,512]{1,0:T(8,128)(2,1)S(1)}, u32[]{:S(2)}, u32[]{:S(2)}) collective-permute-start(bf16[128,512]{1,0:T(8,128)(2,1)S(1)} %get-tuple-element.36.refs_4_), channel_id=1, source_target_pairs={{0,8},{1,9},{2,10},{3,11},{4,12},{5,13},{6,14},{7,15},{8,0},{9,1},... | collective-permute-start | bytes 393224 | tf_op jit(solution)/shard_map/ppermute | solution.py:529
  37.7 8.9 %collective-permute-start.12 = (bf16[128,512]{1,0:T(8,128)(2,1)S(1)}, bf16[128,512]{1,0:T(8,128)(2,1)S(1)}, u32[]{:S(2)}, u32[]{:S(2)}) collective-permute-start(bf16[128,512]{1,0:T(8,128)(2,1)S(1)} %collective-permute-done.11.refs_6_), channel_id=1, source_target_pairs={{0,8},{1,9},{2,10},{3,11},{4,12},{5,13},{6,14},{7,15},{8,0},{9,1},... | collective-permute-start | bytes 393224 | tf_op jit(solution)/shard_map/ppermute | solution.py:529
  41.6 6.4 %collective-permute-start.14 = (bf16[128,512]{1,0:T(8,128)(2,1)S(1)}, bf16[128,512]{1,0:T(8,128)(2,1)S(1)}, u32[]{:S(2)}, u32[]{:S(2)}) collective-permute-start(bf16[128,512]{1,0:T(8,128)(2,1)S(1)} %shard_map.82), channel_id=1, source_target_pairs={{0,8},{1,9},{2,10},{3,11},{4,12},{5,13},{6,14},{7,15},{8,0},{9,1},... | collective-permute-start | bytes 393224 | tf_op jit(solution)/shard_map/ppermute | solution.py:529

commit v2 on v1

--- a/solution.py
+++ b/solution.py
@@ -50,8 +50,8 @@
     return total
 
 
-def as_row(scalar, width):
-    return jnp.full((1, width), scalar, jnp.int32).astype(F32)
+def count_row(table_ref, step, width):
+    return jnp.tile(table_ref[step : step + 1, :], (1, width // table_ref.shape[1]))
 
 
 def size_of(shape):
@@ -160,14 +160,14 @@
 
 
 def forecast_kernel(
-    slots, rows, shares, counts_ref, rank_ref, states_ref, low_ref, high_ref, own_coef_ref,
-    inner_ref, pick_ref, *rest,
+    slots, rows, shares, table_ref, states_ref, low_ref, high_ref, own_coef_ref, inner_ref,
+    pick_ref, *rest,
 ):
     (coef_ref, value_ref, cells_ref) = rest[-3:]
     seen_refs, part_refs = rest[:shares], rest[shares:-3]
     columns = states_ref.shape[1]
     total_rows = rows + 2 * STEPS
-    count = counts_ref[rank_ref[0]]
+    count = count_row(table_ref, 0, columns)
 
     for row in [*range(1, STEPS), *range(STEPS + rows, total_rows - 1)]:
         block = (low_ref[row] if row < STEPS else high_ref[row - STEPS - rows])[slots:]
@@ -210,14 +210,14 @@
             values = after
         for h in range(halves):
             place = lax.broadcasted_iota(jnp.int32, (8, columns), 0) + (start + 8 * h)
-            live = place < count
+            live = place.astype(F32) < count
             for row in range(rows):
                 u = jnp.where(live, values[row + STEPS][h], 0.0)
                 sums[row] = sums[row] + u
                 value_ref[row, start + 8 * h : start + 8 * h + 8, :] = u
 
-    live = lax.broadcasted_iota(jnp.int32, (slots, columns), 0) < count
-    inverse = 1.0 / as_row(count, columns)
+    live = lax.broadcasted_iota(jnp.int32, (slots, columns), 0).astype(F32) < count
+    inverse = 1.0 / count
     means = []
     for row in range(rows):
         mean = jnp.sum(sums[row], axis=0, keepdims=True) * inverse
@@ -255,7 +255,7 @@
 
 def setup_kernel(
     slots, runners, members, shares, counts_ref, rank_ref, index_ref, value_ref, weight_ref,
-    pick_ref, seen_ref, place_ref, own_ref,
+    pick_ref, seen_ref, place_ref, own_ref, table_ref,
 ):
     rank = rank_ref[0]
     share = index_ref.shape[1] // shares
@@ -272,6 +272,8 @@
         place_ref[:, step * slots : (step + 1) * slots] = placing(
             slots, runners, members, counts_ref, rank ^ step, False
         )
+        count = jnp.full((1, table_ref.shape[1]), counts_ref[rank ^ step], jnp.int32)
+        table_ref[step : step + 1, :] = count.astype(F32)
     for side in range(2):
         own_ref[side] = placing(slots, runners, members, counts_ref, rank ^ (1 - side), True)
 
@@ -283,23 +285,19 @@
     return half, row, column
 
 
-def gram_kernel(slots, runners, members, counts_ref, rank_ref, *refs):
-    seen_refs, (both_ref, place_ref, out_ref) = refs[:runners], refs[runners:]
-    rank = rank_ref[0]
-    counts = [counts_ref[rank ^ step] for step in range(runners)]
+def gram_kernel(slots, runners, members, *refs):
+    seen_refs, (table_ref, both_ref, place_ref, out_ref) = refs[:runners], refs[runners:]
     own_means = [joined(ref[slots:, :], 0) for ref in seen_refs]
     width = both_ref.shape[1]
     mean = 0.0
-    for row, count in zip(own_means, counts):
-        mean = mean + row * as_row(count, width)
+    for step, row in enumerate(own_means):
+        mean = mean + row * count_row(table_ref, step, width)
     mean = mean * (1.0 / members)
     observed = 0.0
     for step, ref in enumerate(seen_refs):
-        live = lax.broadcasted_iota(jnp.int32, (slots, width), 0) < counts[step]
         part = ref[:slots, :].astype(F32) + (own_means[step] - mean)
-        part = jnp.where(live, part, 0.0).astype(BF16)
         place = place_ref[:, step * slots : (step + 1) * slots]
-        observed = observed + jnp.dot(place, part, preferred_element_type=F32)
+        observed = observed + jnp.dot(place, part.astype(BF16), preferred_element_type=F32)
     weighted = (observed * both_ref[1:2, :]).astype(BF16)
     across = (((1,), (1,)), ((), ()))
     gram = lax.dot_general(
@@ -389,7 +387,7 @@
             ).astype(BF16)
 
 
-def own_means_of(slots, members, counts_ref, rank, seen_refs, cells):
+def own_means_of(slots, members, table_ref, seen_refs, cells):
     share = seen_refs[0].shape[1]
     own_means, mean = [], 0.0
     for step, ref in enumerate(seen_refs):
@@ -398,16 +396,16 @@
             [joined(packed, 3 + 3 * index) for index in range(cells // share)], axis=1
         )
         own_means.append(row)
-        mean = mean + row * as_row(counts_ref[rank ^ step], cells)
+        mean = mean + row * count_row(table_ref, step, cells)
     return own_means, mean * (1.0 / members)
 
 
-def product_kernel(slots, members, runners, plan, stride, counts_ref, rank_ref, left_ref, *refs):
+def product_kernel(slots, members, runners, plan, stride, table_ref, left_ref, *refs):
     seen_refs, refs = refs[:runners], refs[runners:]
     cell_refs, out_refs = refs[: -len(plan)], refs[-len(plan) :]
     width = out_refs[0].shape[1]
     own_means, mean = own_means_of(
-        slots, members, counts_ref, rank_ref[0], seen_refs, width * PARTS
+        slots, members, table_ref, seen_refs, width * PARTS
     )
     lefts, sums = {}, {}
     for step in range(0, runners, stride):
@@ -430,16 +428,17 @@
         out_ref[...] = (total[:slots] + shift).astype(out_ref.dtype)
 
 
-def final_kernel(slots, rows, counts_ref, rank_ref, *refs):
+def final_kernel(slots, rows, table_ref, *refs):
     own_refs, refs = refs[:PARTS], refs[PARTS:]
     other_refs, (out_hbm, out_ref, sems) = refs[:-3], refs[-3:]
     columns = out_ref.shape[1]
-    count = counts_ref[rank_ref[0]]
+    count = count_row(table_ref, 0, columns)
     chunk = slots // WRITES
     copies = []
     for index in range(WRITES):
         start = index * chunk
-        live = lax.broadcasted_iota(jnp.int32, (chunk, columns), 0) + start < count
+        slot = lax.broadcasted_iota(jnp.int32, (chunk, columns), 0) + start
+        live = slot.astype(F32) < count
         row = 0
         for part, own_ref in enumerate(own_refs):
             for first in range(0, own_ref.shape[1], columns):
@@ -488,13 +487,14 @@
     backward = [(target, source) for source, target in forward]
     low = lax.ppermute(last, "cells", forward)
     high = lax.ppermute(first, "cells", backward)
-    pick, both, place, own = call(
+    pick, both, place, own, table = call(
         functools.partial(setup_kernel, slots, runners, members, shares),
         [
             shape((cells, seen), BF16),
             shape((8, share), F32),
             shape((members, runners * slots), BF16),
             shape((2, slots, members), BF16),
+            shape((runners, columns), F32),
         ],
         [counts, rank],
         [obs_index[None, :], obs_value[None, :], obs_weight[None, :]],
@@ -514,8 +514,8 @@
         functools.partial(forecast_kernel, slots, rows, shares),
         [shape((slots + lower, share), BF16)] * shares
         + [shape((slots, cells // PARTS), BF16)] * PARTS,
-        [counts, rank],
-        [flat, low, high, coefs, inner, pick],
+        [],
+        [table, flat, low, high, coefs, inner, pick],
         [
             pltpu.VMEM((rows + 2 * STEPS, 5, 8, columns), F32),
             pltpu.VMEM((rows, slots, columns), F32),
@@ -546,8 +546,8 @@
     part = call(
         functools.partial(gram_kernel, slots, runners, members),
         shape((half + PAD, members), BF16),
-        [counts, rank],
-        [*all_seen, both, place],
+        [],
+        [*all_seen, table, both, place],
     )
     stages = [[(0, 1)], [(1, 0)]]
     width = 2
@@ -578,8 +578,8 @@
         return call(
             functools.partial(product_kernel, slots, members, runners, plan, stride),
             [shape((slots, cells // PARTS), dtype)] * len(plan),
-            [counts, rank],
-            [left, *all_seen] + [all_cells[step][part] for part, steps in plan for step in steps],
+            [],
+            [table, left, *all_seen] + [all_cells[step][part] for part, steps in plan for step in steps],
         )
 
     shared = [(part, even) for part in range(GATHERED, PARTS)]
@@ -589,8 +589,8 @@
     analysed = call(
         functools.partial(final_kernel, slots, rows),
         shape((slots * rows, columns), F32),
-        [counts, rank],
-        [*own_products, *other_products],
+        [],
+        [table, *own_products, *other_products],
         [pltpu.VMEM((slots * rows, columns), F32), pltpu.SemaphoreType.DMA((WRITES,))],
         write=True,
     )

time: 49.6 us -> 48 us (0.968)
  Pallas kernels: 10.8 us -> 8.19 us
  waiting for transfers between devices: 18.9 us -> 20 us
    pallas_call x11, Pallas kernels: 10.8 us -> 8.19 us  [call(): pl.pallas_call(kernel, out_shape=out_shape, in_specs=[scalar] * len(scala...]
    ppermute x13, waiting for transfers between devices: 18.2 us -> 19.3 us  [moved(): return lax.ppermute(array, ('runner', 'cells'), partners(count, step))]
  transfers between devices with their start and end apart: 15 -> 15, of which waited for: 10 -> 10; matrix products, arithmetic and copies ran while one was open for 0% -> 0% of each run, Pallas kernels for 9% -> 7%
where the time goes in v2:
time: 48 us; the launch traced here: 47.9 us
  waiting for transfers between devices  20 us (42%)
  starting transfers between devices  18.9 us (39%)
  Pallas kernels  8.19 us (17%)
  local copies, waits for them, and re-layouts  0.67 us (1%)
    ppermute x13, waiting for transfers between devices, moved(): return lax.ppermute(array, ('runner', 'cells'), partners(count, step))  19.3 us
    ppermute x13, starting transfers between devices, moved(): return lax.ppermute(array, ('runner', 'cells'), partners(count, step))  15.4 us
    pallas_call x11, Pallas kernels, call(): pl.pallas_call(kernel, out_shape=out_shape, in_specs=[scalar] * len(scala...  8.19 us
    ppermute x1, starting transfers between devices, body(): high = lax.ppermute(first, 'cells', backward)  2.93 us
  transfers between devices with their start and end apart: 15, of which 10 were waited for; matrix products, arithmetic and copies ran while one was open for 0% of the time, Pallas kernels for 7%

profile of v2, /device:TPU:0, one launch (start us, length us, event | category | flops | bytes accessed | tf_op | source)
XLA Modules:
  0.0 47.9 jit_solution(11757116616257774568)
XLA Ops:
  0.0 1.2 %shard_map.74 = (bf16[4,144,128]{2,1,0:T(8,128)(2,1)S(1)}, bf16[4,144,128]{2,1,0:T(8,128)(2,1)S(1)}, f32[1024,128]{1,0:T(8,128)S(1)}, f32[3,8,128]{2,1,0:T(8,128)S(1)}) custom-call(f32[1024,128]{1,0:T(8,128)} %bitcast.9, f32[8,128]{1,0:T(8,128)} %diff_hbm.1, f32[2,8,128]{2,1,0:T(8,128)} %vel_hbm.1), custom_call_target="tpu_custom_call" | custom-call | bytes 1048576 | tf_op jit(solution)/shard_map/pallas_call | solution.py:73
  1.2 0.5 %collective-permute-start = (bf16[4,144,128]{2,1,0:T(8,128)(2,1)S(1)}, bf16[4,144,128]{2,1,0:T(8,128)(2,1)S(1)}, u32[]{:S(2)}, u32[]{:S(2)}) collective-permute-start(bf16[4,144,128]{2,1,0:T(8,128)(2,1)S(1)} %get-tuple-element.26), channel_id=1, source_target_pairs={{0,1},{1,2},{2,3},{3,4},{4,5},{5,6},{6,7},{7,0},{8,9},{9,10},{10,1... | collective-permute-start | bytes 442376 | tf_op jit(solution)/shard_map/ppermute | solution.py:488
  1.7 2.9 %collective-permute-start.1 = (bf16[4,144,128]{2,1,0:T(8,128)(2,1)S(1)}, bf16[4,144,128]{2,1,0:T(8,128)(2,1)S(1)}, u32[]{:S(2)}, u32[]{:S(2)}) collective-permute-start(bf16[4,144,128]{2,1,0:T(8,128)(2,1)S(1)} %get-tuple-element.27), channel_id=1, source_target_pairs={{1,0},{2,1},{3,2},{4,3},{5,4},{6,5},{7,6},{0,7},{9,8},{10,9},{11,1... | collective-permute-start | bytes 442376 | tf_op jit(solution)/shard_map/ppermute | solution.py:489
  4.7 0.0 copy-start.2
  4.7 0.9 %shard_map.75 = (f32[8,5,8,128]{3,2,1,0:T(8,128)S(1)}, f32[12,128,128]{2,1,0:T(8,128)S(1)}) custom-call(f32[1024,128]{1,0:T(8,128)S(1)} %get-tuple-element.25.states_ref, f32[3,8,128]{2,1,0:T(8,128)S(1)} %get-tuple-element.28.fields_ref), custom_call_target="tpu_custom_call" | custom-call | bytes 1048576 | tf_op jit(solution)/shard_map/pallas_call | solution.py:73
  5.6 0.0 copy-start.1
  5.6 0.0 copy-start
  5.6 0.0 copy-start.3
  5.6 0.0 copy-done.2
  5.7 0.6 %copy-done.1 = f32[512]{0:T(512)S(1)} copy-done((f32[512]{0:T(512)S(1)}, f32[512]{0:T(512)}, u32[]{:S(2)}) %copy-start.1) | copy-done | bytes 2072
  6.3 0.0 copy-done
  6.3 0.0 copy-done.3
  6.3 0.8 %shard_map.73 = (bf16[1024,512]{1,0:T(8,128)(2,1)S(1)}, f32[8,256]{1,0:T(8,128)S(1)}, bf16[256,512]{1,0:T(8,128)(2,1)S(1)}, bf16[2,128,256]{2,1,0:T(8,128)(2,1)S(1)}, f32[4,128]{1,0:T(4,128)S(1)}) custom-call(s32[4]{0:T(128)S(1)} %copy-done.3, s32[1]{0:T(128)} %bitcast.rank_ref, s32[1,512]{1,0:T(1,128)S(1)} %bitcast.6, f32[1,512]{1,0:T(1,128)S(1)} %bitcast.7, ...), custom_call_target="tpu_custom_call" | custom-call | bytes 1048576 | tf_op jit(solution)/shard_map/pallas_call | solution.py:73
  7.1 0.3 collective-permute-done.low_ref
  7.4 0.4 collective-permute-done.1.high_ref
  7.9 2.0 %shard_map.76 = (bf16[144,256]{1,0:T(8,128)(2,1)S(1)}, bf16[144,256]{1,0:T(8,128)(2,1)S(1)}, bf16[128,512]{1,0:T(8,128)(2,1)S(1)}, bf16[128,512]{1,0:T(8,128)(2,1)S(1)}) custom-call(f32[4,128]{1,0:T(4,128)S(1)} %get-tuple-element.24.table_ref.refs_4_, f32[1024,128]{1,0:T(8,128)S(1)} %get-tuple-element.25.states_ref, ...), custom_call_target="tpu_custom_call" | custom-call | bytes 1048576 | tf_op jit(solution)/shard_map/pallas_call | solution.py:73
  9.9 4.0 %collective-permute-start.4 = (bf16[144,256]{1,0:T(8,128)(2,1)S(1)}, bf16[144,256]{1,0:T(8,128)(2,1)S(1)}, u32[]{:S(2)}, u32[]{:S(2)}) collective-permute-start(bf16[144,256]{1,0:T(8,128)(2,1)S(1)} %get-tuple-element.33), channel_id=1, source_target_pairs={{0,24},{1,25},{2,26},{3,27},{4,28},{5,29},{6,30},{7,31},{8,16},{9,... | collective-permute-start | bytes 221192 | tf_op jit(solution)/shard_map/ppermute | solution.py:529
  13.9 0.0 collective-permute-start.2
  13.9 0.6 %collective-permute-start.3 = (bf16[144,256]{1,0:T(8,128)(2,1)S(1)}, bf16[144,256]{1,0:T(8,128)(2,1)S(1)}, u32[]{:S(2)}, u32[]{:S(2)}) collective-permute-start(bf16[144,256]{1,0:T(8,128)(2,1)S(1)} %get-tuple-element.32.refs_0_), channel_id=1, source_target_pairs={{0,16},{1,17},{2,18},{3,19},{4,20},{5,21},{6,22},{7,23},{8,24},{9,... | collective-permute-start | bytes 221192 | tf_op jit(solution)/shard_map/ppermute | solution.py:529
  14.5 1.8 %collective-permute-done.4.refs_3_ = bf16[144,256]{1,0:T(8,128)(2,1)S(1)} collective-permute-done((bf16[144,256]{1,0:T(8,128)(2,1)S(1)}, bf16[144,256]{1,0:T(8,128)(2,1)S(1)}, u32[]{:S(2)}, u32[]{:S(2)}) %collective-permute-start.4) | collective-permute-done | bytes 73760 | tf_op jit(solution)/shard_map/ppermute | solution.py:529
  16.3 4.1 %collective-permute-done.2.refs_1_ = bf16[144,256]{1,0:T(8,128)(2,1)S(1)} collective-permute-done((bf16[144,256]{1,0:T(8,128)(2,1)S(1)}, bf16[144,256]{1,0:T(8,128)(2,1)S(1)}, u32[]{:S(2)}, u32[]{:S(2)}) %collective-permute-start.2) | collective-permute-done | bytes 73760 | tf_op jit(solution)/shard_map/ppermute | solution.py:529
  20.5 0.0 collective-permute-done.3.refs_2_
  20.5 0.6 %shard_map.77.refs_0_ = bf16[144,256]{1,0:T(8,128)(2,1)S(1)} custom-call(bf16[144,256]{1,0:T(8,128)(2,1)S(1)} %get-tuple-element.32.refs_0_, bf16[144,256]{1,0:T(8,128)(2,1)S(1)} %collective-permute-done.2.refs_1_, bf16[144,256]{1,0:T(8,128)(2,1)S(1)} %collective-permute-done.3.refs_2_, bf16[144,256]{1,0:T(8,128)(2,1)S(1)} %collective-permute-done.4.refs_3_, ...), custom_call_target="tpu_custom_call" | custom-call | bytes 1048576 | tf_op jit(solution)/shard_map/pallas_call | solution.py:73
  21.1 1.0 %collective-permute-start.5 = (bf16[144,256]{1,0:T(8,128)(2,1)S(1)}, bf16[144,256]{1,0:T(8,128)(2,1)S(1)}, u32[]{:S(2)}, u32[]{:S(2)}) collective-permute-start(bf16[144,256]{1,0:T(8,128)(2,1)S(1)} %shard_map.77.refs_0_), channel_id=1, source_target_pairs={{0,1},{1,0},{2,3},{3,2},{4,5},{5,4},{6,7},{7,6},{8,9},{9,8},{10,11... | collective-permute-start | bytes 221192 | tf_op jit(solution)/shard_map/ppermute | solution.py:529
  22.0 0.9 %collective-permute-done.5.refs_1_ = bf16[144,256]{1,0:T(8,128)(2,1)S(1)} collective-permute-done((bf16[144,256]{1,0:T(8,128)(2,1)S(1)}, bf16[144,256]{1,0:T(8,128)(2,1)S(1)}, u32[]{:S(2)}, u32[]{:S(2)}) %collective-permute-start.5) | collective-permute-done | bytes 73760 | tf_op jit(solution)/shard_map/ppermute | solution.py:529
  23.0 1.0 %collective-permute-start.6 = (bf16[144,256]{1,0:T(8,128)(2,1)S(1)}, bf16[144,256]{1,0:T(8,128)(2,1)S(1)}, u32[]{:S(2)}, u32[]{:S(2)}) collective-permute-start(bf16[144,256]{1,0:T(8,128)(2,1)S(1)} %shard_map.78.refs_0_), channel_id=1, source_target_pairs={{0,8},{1,9},{2,10},{3,11},{4,12},{5,13},{6,14},{7,15},{8,0},{9,1},... | collective-permute-start | bytes 221192 | tf_op jit(solution)/shard_map/ppermute | solution.py:529
  24.0 1.4 %collective-permute-start.11 = (bf16[128,512]{1,0:T(8,128)(2,1)S(1)}, bf16[128,512]{1,0:T(8,128)(2,1)S(1)}, u32[]{:S(2)}, u32[]{:S(2)}) collective-permute-start(bf16[128,512]{1,0:T(8,128)(2,1)S(1)} %get-tuple-element.38.refs_4_), channel_id=1, source_target_pairs={{0,16},{1,17},{2,18},{3,19},{4,20},{5,21},{6,22},{7,23},{8,24},{9,... | collective-permute-start | bytes 393224 | tf_op jit(solution)/shard_map/ppermute | solution.py:529
  25.4 1.5 %collective-permute-start.13 = (bf16[128,512]{1,0:T(8,128)(2,1)S(1)}, bf16[128,512]{1,0:T(8,128)(2,1)S(1)}, u32[]{:S(2)}, u32[]{:S(2)}) collective-permute-start(bf16[128,512]{1,0:T(8,128)(2,1)S(1)} %get-tuple-element.39.refs_8_.refs_4_), channel_id=1, source_target_pairs={{0,16},{1,17},{2,18},{3,19},{4,20},{5,21},{6,22},{7,23},{8,24},{9,... | collective-permute-start | bytes 393224 | tf_op jit(solution)/shard_map/ppermute | solution.py:529
  26.9 1.6 %collective-permute-done.6.refs_1_ = bf16[144,256]{1,0:T(8,128)(2,1)S(1)} collective-permute-done((bf16[144,256]{1,0:T(8,128)(2,1)S(1)}, bf16[144,256]{1,0:T(8,128)(2,1)S(1)}, u32[]{:S(2)}, u32[]{:S(2)}) %collective-permute-start.6) | collective-permute-done | bytes 73760 | tf_op jit(solution)/shard_map/ppermute | solution.py:529
  28.5 1.6 %collective-permute-start.9 = (bf16[144,256]{1,0:T(8,128)(2,1)S(1)}, bf16[144,256]{1,0:T(8,128)(2,1)S(1)}, u32[]{:S(2)}, u32[]{:S(2)}) collective-permute-start(bf16[144,256]{1,0:T(8,128)(2,1)S(1)} %shard_map.79.refs_0_), channel_id=1, source_target_pairs={{0,2},{1,3},{2,0},{3,1},{4,6},{5,7},{6,4},{7,5},{8,10},{9,11},{10,... | collective-permute-start | bytes 221192 | tf_op jit(solution)/shard_map/ppermute | solution.py:529
  30.1 0.8 %collective-permute-start.8 = (bf16[144,256]{1,0:T(8,128)(2,1)S(1)}, bf16[144,256]{1,0:T(8,128)(2,1)S(1)}, u32[]{:S(2)}, u32[]{:S(2)}) collective-permute-start(bf16[144,256]{1,0:T(8,128)(2,1)S(1)} %shard_map.79.refs_0_), channel_id=1, source_target_pairs={{0,4},{1,5},{2,6},{3,7},{4,0},{5,1},{6,2},{7,3},{8,12},{9,13},{10,... | collective-permute-start | bytes 221192 | tf_op jit(solution)/shard_map/ppermute | solution.py:529
  30.9 1.4 %collective-permute-start.7 = (bf16[144,256]{1,0:T(8,128)(2,1)S(1)}, bf16[144,256]{1,0:T(8,128)(2,1)S(1)}, u32[]{:S(2)}, u32[]{:S(2)}) collective-permute-start(bf16[144,256]{1,0:T(8,128)(2,1)S(1)} %shard_map.79.refs_0_), channel_id=1, source_target_pairs={{0,6},{1,7},{2,4},{3,5},{4,2},{5,3},{6,0},{7,1},{8,14},{9,15},{10,... | collective-permute-start | bytes 221192 | tf_op jit(solution)/shard_map/ppermute | solution.py:529
  32.3 4.4 %collective-permute-done.11.refs_6_ = bf16[128,512]{1,0:T(8,128)(2,1)S(1)} collective-permute-done((bf16[128,512]{1,0:T(8,128)(2,1)S(1)}, bf16[128,512]{1,0:T(8,128)(2,1)S(1)}, u32[]{:S(2)}, u32[]{:S(2)}) %collective-permute-start.11) | collective-permute-done | bytes 131104 | tf_op jit(solution)/shard_map/ppermute | solution.py:529
  36.7 0.0 collective-permute-start.10
  36.7 0.0 collective-permute-done.9.refs_3_
  36.7 2.0 %collective-permute-start.12 = (bf16[128,512]{1,0:T(8,128)(2,1)S(1)}, bf16[128,512]{1,0:T(8,128)(2,1)S(1)}, u32[]{:S(2)}, u32[]{:S(2)}) collective-permute-start(bf16[128,512]{1,0:T(8,128)(2,1)S(1)} %collective-permute-done.11.refs_6_), channel_id=1, source_target_pairs={{0,8},{1,9},{2,10},{3,11},{4,12},{5,13},{6,14},{7,15},{8,0},{9,1},... | collective-permute-start | bytes 393224 | tf_op jit(solution)/shard_map/ppermute | solution.py:529
  38.7 0.0 collective-permute-done.8.refs_2_
  38.7 0.0 collective-permute-done.7.refs_1_
  38.7 1.1 %shard_map.80 = (bf16[144,256]{1,0:T(8,128)(2,1)S(1)}, bf16[144,512]{1,0:T(8,128)(2,1)S(1)}) custom-call(bf16[144,256]{1,0:T(8,128)(2,1)S(1)} %shard_map.79.refs_0_, bf16[144,256]{1,0:T(8,128)(2,1)S(1)} %collective-permute-done.7.refs_1_, bf16[144,256]{1,0:T(8,128)(2,1)S(1)} %collective-permute-done.8.refs_2_, ...), custom_call_target="tpu_custom_call" | custom-call | bytes 1048576 | tf_op jit(solution)/shard_map/pallas_call | solution.py:73
  39.8 0.0 collective-permute-done.13.refs_9_.refs_5_
  39.8 0.3 shard_map.82
  40.0 0.1 collective-permute-start.14
  40.1 2.9 %collective-permute-done.10.refs_5_ = bf16[128,512]{1,0:T(8,128)(2,1)S(1)} collective-permute-done((bf16[128,512]{1,0:T(8,128)(2,1)S(1)}, bf16[128,512]{1,0:T(8,128)(2,1)S(1)}, u32[]{:S(2)}, u32[]{:S(2)}) %collective-permute-start.10) | collective-permute-done | bytes 131104 | tf_op jit(solution)/shard_map/ppermute | solution.py:529
  43.0 2.6 %collective-permute-done.12.refs_7_ = bf16[128,512]{1,0:T(8,128)(2,1)S(1)} collective-permute-done((bf16[128,512]{1,0:T(8,128)(2,1)S(1)}, bf16[128,512]{1,0:T(8,128)(2,1)S(1)}, u32[]{:S(2)}, u32[]{:S(2)}) %collective-permute-start.12) | collective-permute-done | bytes 131104 | tf_op jit(solution)/shard_map/ppermute | solution.py:529
  45.6 0.4 shard_map.81
  46.1 1.0 %collective-permute-done.14.refs_2_ = bf16[128,512]{1,0:T(8,128)(2,1)S(1)} collective-permute-done((bf16[128,512]{1,0:T(8,128)(2,1)S(1)}, bf16[128,512]{1,0:T(8,128)(2,1)S(1)}, u32[]{:S(2)}, u32[]{:S(2)}) %collective-permute-start.14) | collective-permute-done | bytes 131104 | tf_op jit(solution)/shard_map/ppermute | solution.py:529
  47.0 0.8 %shard_map.83 = f32[1024,128]{1,0:T(8,128)} custom-call(f32[4,128]{1,0:T(4,128)S(1)} %get-tuple-element.24.table_ref.refs_4_, f32[128,512]{1,0:T(8,128)S(1)} %get-tuple-element.40.refs_0_, f32[128,512]{1,0:T(8,128)S(1)} %get-tuple-element.41.refs_1_, bf16[128,512]{1,0:T(8,128)(2,1)S(1)} %collective-permute-done.14.refs_2_), custom_call_target="tpu_custom_call" | custom-call | bytes 1048576 | tf_op jit(solution)/shard_map/pallas_call | solution.py:73
  (2 shorter events, 0.1 us)
Async XLA Ops:
  1.2 6.2 %collective-permute-start = (bf16[4,144,128]{2,1,0:T(8,128)(2,1)S(1)}, bf16[4,144,128]{2,1,0:T(8,128)(2,1)S(1)}, u32[]{:S(2)}, u32[]{:S(2)}) collective-permute-start(bf16[4,144,128]{2,1,0:T(8,128)(2,1)S(1)} %get-tuple-element.26), channel_id=1, source_target_pairs={{0,1},{1,2},{2,3},{3,4},{4,5},{5,6},{6,7},{7,0},{8,9},{9,10},{10,1... | collective-permute-start | bytes 442376 | tf_op jit(solution)/shard_map/ppermute | solution.py:488
  1.7 6.1 %collective-permute-start.1 = (bf16[4,144,128]{2,1,0:T(8,128)(2,1)S(1)}, bf16[4,144,128]{2,1,0:T(8,128)(2,1)S(1)}, u32[]{:S(2)}, u32[]{:S(2)}) collective-permute-start(bf16[4,144,128]{2,1,0:T(8,128)(2,1)S(1)} %get-tuple-element.27), channel_id=1, source_target_pairs={{1,0},{2,1},{3,2},{4,3},{5,4},{6,5},{7,6},{0,7},{9,8},{10,9},{11,1... | collective-permute-start | bytes 442376 | tf_op jit(solution)/shard_map/ppermute | solution.py:489
  4.7 1.0 %copy-start.2 = (f32[512]{0:T(512)S(1)}, f32[512]{0:T(512)}, u32[]{:S(2)}) copy-start(f32[512]{0:T(512)} %param.13) | copy-start | bytes 6148
  5.6 0.7 %copy-start.1 = (f32[512]{0:T(512)S(1)}, f32[512]{0:T(512)}, u32[]{:S(2)}) copy-start(f32[512]{0:T(512)} %param.12) | copy-start | bytes 6148
  5.6 0.7 %copy-start = (s32[512]{0:T(512)S(1)}, s32[512]{0:T(512)}, u32[]{:S(2)}) copy-start(s32[512]{0:T(512)} %param.11) | copy-start | bytes 6148
  5.6 0.7 %copy-start.3 = (s32[4]{0:T(128)S(1)}, s32[4]{0:T(128)}, u32[]{:S(2)}) copy-start(s32[4]{0:T(128)} %counts_ref.1) | copy-start | bytes 52
  9.9 6.4 %collective-permute-start.4 = (bf16[144,256]{1,0:T(8,128)(2,1)S(1)}, bf16[144,256]{1,0:T(8,128)(2,1)S(1)}, u32[]{:S(2)}, u32[]{:S(2)}) collective-permute-start(bf16[144,256]{1,0:T(8,128)(2,1)S(1)} %get-tuple-element.33), channel_id=1, source_target_pairs={{0,24},{1,25},{2,26},{3,27},{4,28},{5,29},{6,30},{7,31},{8,16},{9,... | collective-permute-start | bytes 221192 | tf_op jit(solution)/shard_map/ppermute | solution.py:529
  13.9 6.6 %collective-permute-start.2 = (bf16[144,256]{1,0:T(8,128)(2,1)S(1)}, bf16[144,256]{1,0:T(8,128)(2,1)S(1)}, u32[]{:S(2)}, u32[]{:S(2)}) collective-permute-start(bf16[144,256]{1,0:T(8,128)(2,1)S(1)} %get-tuple-element.33), channel_id=1, source_target_pairs={{0,8},{1,9},{2,10},{3,11},{4,12},{5,13},{6,14},{7,15},{8,0},{9,1},... | collective-permute-start | bytes 221192 | tf_op jit(solution)/shard_map/ppermute | solution.py:529
  13.9 6.6 %collective-permute-start.3 = (bf16[144,256]{1,0:T(8,128)(2,1)S(1)}, bf16[144,256]{1,0:T(8,128)(2,1)S(1)}, u32[]{:S(2)}, u32[]{:S(2)}) collective-permute-start(bf16[144,256]{1,0:T(8,128)(2,1)S(1)} %get-tuple-element.32.refs_0_), channel_id=1, source_target_pairs={{0,16},{1,17},{2,18},{3,19},{4,20},{5,21},{6,22},{7,23},{8,24},{9,... | collective-permute-start | bytes 221192 | tf_op jit(solution)/shard_map/ppermute | solution.py:529
  21.1 1.9 %collective-permute-start.5 = (bf16[144,256]{1,0:T(8,128)(2,1)S(1)}, bf16[144,256]{1,0:T(8,128)(2,1)S(1)}, u32[]{:S(2)}, u32[]{:S(2)}) collective-permute-start(bf16[144,256]{1,0:T(8,128)(2,1)S(1)} %shard_map.77.refs_0_), channel_id=1, source_target_pairs={{0,1},{1,0},{2,3},{3,2},{4,5},{5,4},{6,7},{7,6},{8,9},{9,8},{10,11... | collective-permute-start | bytes 221192 | tf_op jit(solution)/shard_map/ppermute | solution.py:529
  23.0 5.5 %collective-permute-start.6 = (bf16[144,256]{1,0:T(8,128)(2,1)S(1)}, bf16[144,256]{1,0:T(8,128)(2,1)S(1)}, u32[]{:S(2)}, u32[]{:S(2)}) collective-permute-start(bf16[144,256]{1,0:T(8,128)(2,1)S(1)} %shard_map.78.refs_0_), channel_id=1, source_target_pairs={{0,8},{1,9},{2,10},{3,11},{4,12},{5,13},{6,14},{7,15},{8,0},{9,1},... | collective-permute-start | bytes 221192 | tf_op jit(solution)/shard_map/ppermute | solution.py:529
  24.0 12.7 %collective-permute-start.11 = (bf16[128,512]{1,0:T(8,128)(2,1)S(1)}, bf16[128,512]{1,0:T(8,128)(2,1)S(1)}, u32[]{:S(2)}, u32[]{:S(2)}) collective-permute-start(bf16[128,512]{1,0:T(8,128)(2,1)S(1)} %get-tuple-element.38.refs_4_), channel_id=1, source_target_pairs={{0,16},{1,17},{2,18},{3,19},{4,20},{5,21},{6,22},{7,23},{8,24},{9,... | collective-permute-start | bytes 393224 | tf_op jit(solution)/shard_map/ppermute | solution.py:529
  25.4 14.3 %collective-permute-start.13 = (bf16[128,512]{1,0:T(8,128)(2,1)S(1)}, bf16[128,512]{1,0:T(8,128)(2,1)S(1)}, u32[]{:S(2)}, u32[]{:S(2)}) collective-permute-start(bf16[128,512]{1,0:T(8,128)(2,1)S(1)} %get-tuple-element.39.refs_8_.refs_4_), channel_id=1, source_target_pairs={{0,16},{1,17},{2,18},{3,19},{4,20},{5,21},{6,22},{7,23},{8,24},{9,... | collective-permute-start | bytes 393224 | tf_op jit(solution)/shard_map/ppermute | solution.py:529
  28.5 8.2 %collective-permute-start.9 = (bf16[144,256]{1,0:T(8,128)(2,1)S(1)}, bf16[144,256]{1,0:T(8,128)(2,1)S(1)}, u32[]{:S(2)}, u32[]{:S(2)}) collective-permute-start(bf16[144,256]{1,0:T(8,128)(2,1)S(1)} %shard_map.79.refs_0_), channel_id=1, source_target_pairs={{0,2},{1,3},{2,0},{3,1},{4,6},{5,7},{6,4},{7,5},{8,10},{9,11},{10,... | collective-permute-start | bytes 221192 | tf_op jit(solution)/shard_map/ppermute | solution.py:529
  30.1 8.6 %collective-permute-start.8 = (bf16[144,256]{1,0:T(8,128)(2,1)S(1)}, bf16[144,256]{1,0:T(8,128)(2,1)S(1)}, u32[]{:S(2)}, u32[]{:S(2)}) collective-permute-start(bf16[144,256]{1,0:T(8,128)(2,1)S(1)} %shard_map.79.refs_0_), channel_id=1, source_target_pairs={{0,4},{1,5},{2,6},{3,7},{4,0},{5,1},{6,2},{7,3},{8,12},{9,13},{10,... | collective-permute-start | bytes 221192 | tf_op jit(solution)/shard_map/ppermute | solution.py:529
  30.9 7.8 %collective-permute-start.7 = (bf16[144,256]{1,0:T(8,128)(2,1)S(1)}, bf16[144,256]{1,0:T(8,128)(2,1)S(1)}, u32[]{:S(2)}, u32[]{:S(2)}) collective-permute-start(bf16[144,256]{1,0:T(8,128)(2,1)S(1)} %shard_map.79.refs_0_), channel_id=1, source_target_pairs={{0,6},{1,7},{2,4},{3,5},{4,2},{5,3},{6,0},{7,1},{8,14},{9,15},{10,... | collective-permute-start | bytes 221192 | tf_op jit(solution)/shard_map/ppermute | solution.py:529
  36.7 6.4 %collective-permute-start.10 = (bf16[128,512]{1,0:T(8,128)(2,1)S(1)}, bf16[128,512]{1,0:T(8,128)(2,1)S(1)}, u32[]{:S(2)}, u32[]{:S(2)}) collective-permute-start(bf16[128,512]{1,0:T(8,128)(2,1)S(1)} %get-tuple-element.38.refs_4_), channel_id=1, source_target_pairs={{0,8},{1,9},{2,10},{3,11},{4,12},{5,13},{6,14},{7,15},{8,0},{9,1},... | collective-permute-start | bytes 393224 | tf_op jit(solution)/shard_map/ppermute | solution.py:529
  36.7 8.9 %collective-permute-start.12 = (bf16[128,512]{1,0:T(8,128)(2,1)S(1)}, bf16[128,512]{1,0:T(8,128)(2,1)S(1)}, u32[]{:S(2)}, u32[]{:S(2)}) collective-permute-start(bf16[128,512]{1,0:T(8,128)(2,1)S(1)} %collective-permute-done.11.refs_6_), channel_id=1, source_target_pairs={{0,8},{1,9},{2,10},{3,11},{4,12},{5,13},{6,14},{7,15},{8,0},{9,1},... | collective-permute-start | bytes 393224 | tf_op jit(solution)/shard_map/ppermute | solution.py:529
  40.0 7.0 %collective-permute-start.14 = (bf16[128,512]{1,0:T(8,128)(2,1)S(1)}, bf16[128,512]{1,0:T(8,128)(2,1)S(1)}, u32[]{:S(2)}, u32[]{:S(2)}) collective-permute-start(bf16[128,512]{1,0:T(8,128)(2,1)S(1)} %shard_map.82), channel_id=1, source_target_pairs={{0,8},{1,9},{2,10},{3,11},{4,12},{5,13},{6,14},{7,15},{8,0},{9,1},... | collective-permute-start | bytes 393224 | tf_op jit(solution)/shard_map/ppermute | solution.py:529

commit v3 on v2

--- a/solution.py
+++ b/solution.py
@@ -330,8 +330,10 @@
     out_ref[half:, :] = stacked([*pieces(bias), *pieces(diagonal)], PAD)
 
 
-def transform_kernel(slots, members, *refs):
-    part_refs, (place_ref, own_ref), out_refs = refs[:-4], refs[-4:-2], refs[-2:]
+def transform_kernel(slots, members, runners, sums, plan, *refs):
+    part_refs, refs = refs[:sums], refs[sums:]
+    (place_ref, own_ref, table_ref), refs = refs[:3], refs[3:]
+    (transform_ref, shift_ref), refs = refs[-2:], refs[:-2]
     half, row, column = triangles(members)
     packed, bias, diagonal = total_of(half, part_refs)
     corner, side = packed[:, :half], packed[:, half:]
@@ -376,15 +378,20 @@
         - 0.3125 * cubed
     ).astype(BF16)
     shift = stacked(pieces(shift), PAD)
-    for side, out_ref in enumerate(out_refs):
-        rows = jnp.dot(own_ref[side], transform, preferred_element_type=F32).astype(BF16)
-        left = jnp.concatenate([rows, shift], axis=0)
-        for index in range(out_ref.shape[1] // slots):
-            step = index if side else 2 * index
-            place = place_ref[:, step * slots : (step + 1) * slots]
-            out_ref[:, index * slots : (index + 1) * slots] = jnp.dot(
-                left, place, preferred_element_type=F32
-            ).astype(BF16)
+    transform_ref[...] = transform
+    shift_ref[...] = shift
+    write_products(
+        slots, members, runners, plan, 0, transform, shift, own_ref, place_ref, table_ref, refs
+    )
+
+
+def keep_kernel(
+    slots, members, runners, plan, transform_ref, shift_ref, own_ref, place_ref, table_ref, *refs
+):
+    transform, shift = transform_ref[...], shift_ref[...]
+    write_products(
+        slots, members, runners, plan, 1, transform, shift, own_ref, place_ref, table_ref, refs
+    )
 
 
 def own_means_of(slots, members, table_ref, seen_refs, cells):
@@ -400,17 +407,19 @@
     return own_means, mean * (1.0 / members)
 
 
-def product_kernel(slots, members, runners, plan, stride, table_ref, left_ref, *refs):
+def write_products(
+    slots, members, runners, plan, side, transform, shift, own_ref, place_ref, table_ref, refs
+):
     seen_refs, refs = refs[:runners], refs[runners:]
     cell_refs, out_refs = refs[: -len(plan)], refs[-len(plan) :]
     width = out_refs[0].shape[1]
-    own_means, mean = own_means_of(
-        slots, members, table_ref, seen_refs, width * PARTS
-    )
+    own_means, mean = own_means_of(slots, members, table_ref, seen_refs, width * PARTS)
+    rows = jnp.dot(own_ref[side], transform, preferred_element_type=F32).astype(BF16)
+    both = jnp.concatenate([rows, shift], axis=0)
     lefts, sums = {}, {}
-    for step in range(0, runners, stride):
-        first = step // stride * slots
-        lefts[step] = left_ref[:, first : first + slots]
+    for step in sorted({step for _, steps in plan for step in steps}):
+        table = place_ref[:, step * slots : (step + 1) * slots]
+        lefts[step] = jnp.dot(both, table, preferred_element_type=F32).astype(BF16)
         sums[step] = jnp.sum(lefts[step].astype(F32), axis=1, keepdims=True)
     place = 0
     for (part, steps), out_ref in zip(plan, out_refs):
@@ -423,7 +432,7 @@
             total = total + sums[step] * (own_means[step] - mean)[:, span]
             place = place + 1
         shift = joined(total[slots:], 0)
-        if stride == 1:
+        if side:
             shift = shift + mean[:, span]
         out_ref[...] = (total[:slots] + shift).astype(out_ref.dtype)
 
@@ -564,28 +573,26 @@
                 [],
                 parts,
             )
-    give, keep = call(
-        functools.partial(transform_kernel, slots, members),
-        [
-            shape((height, runners // 2 * slots), BF16),
-            shape((height, runners * slots), BF16),
-        ],
+
+    def held(plan):
+        return all_seen + [all_cells[step][part] for part, steps in plan for step in steps]
+
+    shared = [(part, even) for part in range(GATHERED, PARTS)]
+    *given_products, transform, shift = call(
+        functools.partial(transform_kernel, slots, members, runners, len(parts), shared),
+        [shape((slots, cells // PARTS), BF16)] * len(shared)
+        + [shape((members, members), BF16), shape((PAD, members), BF16)],
         [],
-        [*parts, place, own],
-    )
-
-    def product(left, plan, stride, dtype):
-        return call(
-            functools.partial(product_kernel, slots, members, runners, plan, stride),
-            [shape((slots, cells // PARTS), dtype)] * len(plan),
-            [],
-            [table, left, *all_seen] + [all_cells[step][part] for part, steps in plan for step in steps],
-        )
-
-    shared = [(part, even) for part in range(GATHERED, PARTS)]
-    other_products = [moved(array, 1) for array in product(give, shared, 2, BF16)]
-    whole = [(part, sorted(all_cells)) for part in range(GATHERED)]
-    own_products = product(keep, whole + shared, 1, F32)
+        [*parts, place, own, table, *held(shared)],
+    )
+    other_products = [moved(array, 1) for array in given_products]
+    plan = [(part, sorted(all_cells)) for part in range(GATHERED)] + shared
+    own_products = call(
+        functools.partial(keep_kernel, slots, members, runners, plan),
+        [shape((slots, cells // PARTS), F32)] * len(plan),
+        [],
+        [transform, shift, own, place, table, *held(plan)],
+    )
     analysed = call(
         functools.partial(final_kernel, slots, rows),
         shape((slots * rows, columns), F32),

time: 48 us -> 48.3 us (level)
    pallas_call x11 -> x10, Pallas kernels: 8.19 us -> 8.13 us  [call(): pl.pallas_call(kernel, out_shape=out_shape, in_specs=[scalar] * len(scala...]
  transfers between devices with their start and end apart: 15 -> 15, of which waited for: 10 -> 11; matrix products, arithmetic and copies ran while one was open for 0% -> 0% of each run, Pallas kernels for 7% -> 7%
where the time goes in v3:
time: 48.3 us; the launch traced here: 48.1 us
  waiting for transfers between devices  20.3 us (42%)
  starting transfers between devices  18.9 us (39%)
  Pallas kernels  8.13 us (17%)
  local copies, waits for them, and re-layouts  0.67 us (1%)
    ppermute x13, waiting for transfers between devices, moved(): return lax.ppermute(array, ('runner', 'cells'), partners(count, step))  19.6 us
    ppermute x13, starting transfers between devices, moved(): return lax.ppermute(array, ('runner', 'cells'), partners(count, step))  15.4 us
    pallas_call x10, Pallas kernels, call(): pl.pallas_call(kernel, out_shape=out_shape, in_specs=[scalar] * len(scala...  8.13 us
    ppermute x1, starting transfers between devices, body(): high = lax.ppermute(first, 'cells', backward)  2.93 us
  transfers between devices with their start and end apart: 15, of which 11 were waited for; matrix products, arithmetic and copies ran while one was open for 0% of the time, Pallas kernels for 7%

profile of v3, /device:TPU:0, one launch (start us, length us, event | category | flops | bytes accessed | tf_op | source)
XLA Modules:
  0.0 48.1 jit_solution(15217139859663345579)
XLA Ops:
  0.0 1.2 %shard_map.74 = (bf16[4,144,128]{2,1,0:T(8,128)(2,1)S(1)}, bf16[4,144,128]{2,1,0:T(8,128)(2,1)S(1)}, f32[1024,128]{1,0:T(8,128)S(1)}, f32[3,8,128]{2,1,0:T(8,128)S(1)}) custom-call(f32[1024,128]{1,0:T(8,128)} %bitcast.9, f32[8,128]{1,0:T(8,128)} %diff_hbm.1, f32[2,8,128]{2,1,0:T(8,128)} %vel_hbm.1), custom_call_target="tpu_custom_call" | custom-call | bytes 1048576 | tf_op jit(solution)/shard_map/pallas_call | solution.py:73
  1.2 0.5 %collective-permute-start = (bf16[4,144,128]{2,1,0:T(8,128)(2,1)S(1)}, bf16[4,144,128]{2,1,0:T(8,128)(2,1)S(1)}, u32[]{:S(2)}, u32[]{:S(2)}) collective-permute-start(bf16[4,144,128]{2,1,0:T(8,128)(2,1)S(1)} %get-tuple-element.27), channel_id=1, source_target_pairs={{0,1},{1,2},{2,3},{3,4},{4,5},{5,6},{6,7},{7,0},{8,9},{9,10},{10,1... | collective-permute-start | bytes 442376 | tf_op jit(solution)/shard_map/ppermute | solution.py:497
  1.7 2.9 %collective-permute-start.1 = (bf16[4,144,128]{2,1,0:T(8,128)(2,1)S(1)}, bf16[4,144,128]{2,1,0:T(8,128)(2,1)S(1)}, u32[]{:S(2)}, u32[]{:S(2)}) collective-permute-start(bf16[4,144,128]{2,1,0:T(8,128)(2,1)S(1)} %get-tuple-element.28), channel_id=1, source_target_pairs={{1,0},{2,1},{3,2},{4,3},{5,4},{6,5},{7,6},{0,7},{9,8},{10,9},{11,1... | collective-permute-start | bytes 442376 | tf_op jit(solution)/shard_map/ppermute | solution.py:498
  4.7 0.0 copy-start.2
  4.7 0.9 %shard_map.75 = (f32[8,5,8,128]{3,2,1,0:T(8,128)S(1)}, f32[12,128,128]{2,1,0:T(8,128)S(1)}) custom-call(f32[1024,128]{1,0:T(8,128)S(1)} %get-tuple-element.26.states_ref, f32[3,8,128]{2,1,0:T(8,128)S(1)} %get-tuple-element.29.fields_ref), custom_call_target="tpu_custom_call" | custom-call | bytes 1048576 | tf_op jit(solution)/shard_map/pallas_call | solution.py:73
  5.6 0.0 copy-start.1
  5.6 0.0 copy-start
  5.6 0.0 copy-start.3
  5.6 0.0 copy-done.2
  5.7 0.6 %copy-done.1 = f32[512]{0:T(512)S(1)} copy-done((f32[512]{0:T(512)S(1)}, f32[512]{0:T(512)}, u32[]{:S(2)}) %copy-start.1) | copy-done | bytes 2072
  6.3 0.0 copy-done
  6.3 0.0 copy-done.3
  6.3 0.8 %shard_map.73 = (bf16[1024,512]{1,0:T(8,128)(2,1)S(1)}, f32[8,256]{1,0:T(8,128)S(1)}, bf16[256,512]{1,0:T(8,128)(2,1)S(1)}, bf16[2,128,256]{2,1,0:T(8,128)(2,1)S(1)}, f32[4,128]{1,0:T(4,128)S(1)}) custom-call(s32[4]{0:T(128)S(1)} %copy-done.3, s32[1]{0:T(128)} %bitcast.rank_ref, s32[1,512]{1,0:T(1,128)S(1)} %bitcast.6, f32[1,512]{1,0:T(1,128)S(1)} %bitcast.7, ...), custom_call_target="tpu_custom_call" | custom-call | bytes 1048576 | tf_op jit(solution)/shard_map/pallas_call | solution.py:73
  7.1 0.3 collective-permute-done.low_ref
  7.4 0.4 collective-permute-done.1.high_ref
  7.9 2.0 %shard_map.76 = (bf16[144,256]{1,0:T(8,128)(2,1)S(1)}, bf16[144,256]{1,0:T(8,128)(2,1)S(1)}, bf16[128,512]{1,0:T(8,128)(2,1)S(1)}, bf16[128,512]{1,0:T(8,128)(2,1)S(1)}) custom-call(f32[4,128]{1,0:T(4,128)S(1)} %get-tuple-element.25.table_ref.refs_4_.refs_6_, f32[1024,128]{1,0:T(8,128)S(1)} %get-tuple-element.26.states_ref, ...), custom_call_target="tpu_custom_call" | custom-call | bytes 1048576 | tf_op jit(solution)/shard_map/pallas_call | solution.py:73
  9.9 4.0 %collective-permute-start.4 = (bf16[144,256]{1,0:T(8,128)(2,1)S(1)}, bf16[144,256]{1,0:T(8,128)(2,1)S(1)}, u32[]{:S(2)}, u32[]{:S(2)}) collective-permute-start(bf16[144,256]{1,0:T(8,128)(2,1)S(1)} %get-tuple-element.34), channel_id=1, source_target_pairs={{0,24},{1,25},{2,26},{3,27},{4,28},{5,29},{6,30},{7,31},{8,16},{9,... | collective-permute-start | bytes 221192 | tf_op jit(solution)/shard_map/ppermute | solution.py:538
  13.9 0.0 collective-permute-start.2
  13.9 0.6 %collective-permute-start.3 = (bf16[144,256]{1,0:T(8,128)(2,1)S(1)}, bf16[144,256]{1,0:T(8,128)(2,1)S(1)}, u32[]{:S(2)}, u32[]{:S(2)}) collective-permute-start(bf16[144,256]{1,0:T(8,128)(2,1)S(1)} %get-tuple-element.33.refs_0_.refs_7_), channel_id=1, source_target_pairs={{0,16},{1,17},{2,18},{3,19},{4,20},{5,21},{6,22},{7,23},{8,24},{9,... | collective-permute-start | bytes 221192 | tf_op jit(solution)/shard_map/ppermute | solution.py:538
  14.5 1.8 %collective-permute-done.4.refs_3_.refs_10_ = bf16[144,256]{1,0:T(8,128)(2,1)S(1)} collective-permute-done((bf16[144,256]{1,0:T(8,128)(2,1)S(1)}, bf16[144,256]{1,0:T(8,128)(2,1)S(1)}, u32[]{:S(2)}, u32[]{:S(2)}) %collective-permute-start.4) | collective-permute-done | bytes 73760 | tf_op jit(solution)/shard_map/ppermute | solution.py:538
  16.3 4.1 %collective-permute-done.2.refs_1_.refs_8_ = bf16[144,256]{1,0:T(8,128)(2,1)S(1)} collective-permute-done((bf16[144,256]{1,0:T(8,128)(2,1)S(1)}, bf16[144,256]{1,0:T(8,128)(2,1)S(1)}, u32[]{:S(2)}, u32[]{:S(2)}) %collective-permute-start.2) | collective-permute-done | bytes 73760 | tf_op jit(solution)/shard_map/ppermute | solution.py:538
  20.5 0.0 collective-permute-done.3.refs_2_.refs_9_
  20.5 0.6 %shard_map.77.refs_0_ = bf16[144,256]{1,0:T(8,128)(2,1)S(1)} custom-call(bf16[144,256]{1,0:T(8,128)(2,1)S(1)} %get-tuple-element.33.refs_0_.refs_7_, bf16[144,256]{1,0:T(8,128)(2,1)S(1)} %collective-permute-done.2.refs_1_.refs_8_, bf16[144,256]{1,0:T(8,128)(2,1)S(1)} %collective-permute-done.3.refs_2_.refs_9_, ...), custom_call_target="tpu_custom_call" | custom-call | bytes 1048576 | tf_op jit(solution)/shard_map/pallas_call | solution.py:73
  21.1 1.0 %collective-permute-start.5 = (bf16[144,256]{1,0:T(8,128)(2,1)S(1)}, bf16[144,256]{1,0:T(8,128)(2,1)S(1)}, u32[]{:S(2)}, u32[]{:S(2)}) collective-permute-start(bf16[144,256]{1,0:T(8,128)(2,1)S(1)} %shard_map.77.refs_0_), channel_id=1, source_target_pairs={{0,1},{1,0},{2,3},{3,2},{4,5},{5,4},{6,7},{7,6},{8,9},{9,8},{10,11... | collective-permute-start | bytes 221192 | tf_op jit(solution)/shard_map/ppermute | solution.py:538
  22.0 0.9 %collective-permute-done.5.refs_1_ = bf16[144,256]{1,0:T(8,128)(2,1)S(1)} collective-permute-done((bf16[144,256]{1,0:T(8,128)(2,1)S(1)}, bf16[144,256]{1,0:T(8,128)(2,1)S(1)}, u32[]{:S(2)}, u32[]{:S(2)}) %collective-permute-start.5) | collective-permute-done | bytes 73760 | tf_op jit(solution)/shard_map/ppermute | solution.py:538
  23.0 1.0 %collective-permute-start.6 = (bf16[144,256]{1,0:T(8,128)(2,1)S(1)}, bf16[144,256]{1,0:T(8,128)(2,1)S(1)}, u32[]{:S(2)}, u32[]{:S(2)}) collective-permute-start(bf16[144,256]{1,0:T(8,128)(2,1)S(1)} %shard_map.78.refs_0_), channel_id=1, source_target_pairs={{0,8},{1,9},{2,10},{3,11},{4,12},{5,13},{6,14},{7,15},{8,0},{9,1},... | collective-permute-start | bytes 221192 | tf_op jit(solution)/shard_map/ppermute | solution.py:538
  24.0 1.4 %collective-permute-start.10 = (bf16[128,512]{1,0:T(8,128)(2,1)S(1)}, bf16[128,512]{1,0:T(8,128)(2,1)S(1)}, u32[]{:S(2)}, u32[]{:S(2)}) collective-permute-start(bf16[128,512]{1,0:T(8,128)(2,1)S(1)} %get-tuple-element.38.refs_11_.refs_8_), channel_id=1, source_target_pairs={{0,16},{1,17},{2,18},{3,19},{4,20},{5,21},{6,22},{7,23},{8,24},{9,... | collective-permute-start | bytes 393224 | tf_op jit(solution)/shard_map/ppermute | solution.py:538
  25.4 1.5 %collective-permute-start.12 = (bf16[128,512]{1,0:T(8,128)(2,1)S(1)}, bf16[128,512]{1,0:T(8,128)(2,1)S(1)}, u32[]{:S(2)}, u32[]{:S(2)}) collective-permute-start(bf16[128,512]{1,0:T(8,128)(2,1)S(1)} %get-tuple-element.41.refs_4_), channel_id=1, source_target_pairs={{0,16},{1,17},{2,18},{3,19},{4,20},{5,21},{6,22},{7,23},{8,24},{9,... | collective-permute-start | bytes 393224 | tf_op jit(solution)/shard_map/ppermute | solution.py:538
  26.9 1.6 %collective-permute-done.6.refs_1_ = bf16[144,256]{1,0:T(8,128)(2,1)S(1)} collective-permute-done((bf16[144,256]{1,0:T(8,128)(2,1)S(1)}, bf16[144,256]{1,0:T(8,128)(2,1)S(1)}, u32[]{:S(2)}, u32[]{:S(2)}) %collective-permute-start.6) | collective-permute-done | bytes 73760 | tf_op jit(solution)/shard_map/ppermute | solution.py:538
  28.5 1.6 %collective-permute-start.9 = (bf16[144,256]{1,0:T(8,128)(2,1)S(1)}, bf16[144,256]{1,0:T(8,128)(2,1)S(1)}, u32[]{:S(2)}, u32[]{:S(2)}) collective-permute-start(bf16[144,256]{1,0:T(8,128)(2,1)S(1)} %shard_map.79.refs_0_), channel_id=1, source_target_pairs={{0,2},{1,3},{2,0},{3,1},{4,6},{5,7},{6,4},{7,5},{8,10},{9,11},{10,... | collective-permute-start | bytes 221192 | tf_op jit(solution)/shard_map/ppermute | solution.py:538
  30.1 0.8 %collective-permute-start.8 = (bf16[144,256]{1,0:T(8,128)(2,1)S(1)}, bf16[144,256]{1,0:T(8,128)(2,1)S(1)}, u32[]{:S(2)}, u32[]{:S(2)}) collective-permute-start(bf16[144,256]{1,0:T(8,128)(2,1)S(1)} %shard_map.79.refs_0_), channel_id=1, source_target_pairs={{0,4},{1,5},{2,6},{3,7},{4,0},{5,1},{6,2},{7,3},{8,12},{9,13},{10,... | collective-permute-start | bytes 221192 | tf_op jit(solution)/shard_map/ppermute | solution.py:538
  30.9 1.4 %collective-permute-start.7 = (bf16[144,256]{1,0:T(8,128)(2,1)S(1)}, bf16[144,256]{1,0:T(8,128)(2,1)S(1)}, u32[]{:S(2)}, u32[]{:S(2)}) collective-permute-start(bf16[144,256]{1,0:T(8,128)(2,1)S(1)} %shard_map.79.refs_0_), channel_id=1, source_target_pairs={{0,6},{1,7},{2,4},{3,5},{4,2},{5,3},{6,0},{7,1},{8,14},{9,15},{10,... | collective-permute-start | bytes 221192 | tf_op jit(solution)/shard_map/ppermute | solution.py:538
  32.3 4.4 %collective-permute-done.10.refs_12_.refs_9_ = bf16[128,512]{1,0:T(8,128)(2,1)S(1)} collective-permute-done((bf16[128,512]{1,0:T(8,128)(2,1)S(1)}, bf16[128,512]{1,0:T(8,128)(2,1)S(1)}, u32[]{:S(2)}, u32[]{:S(2)}) %collective-permute-start.10) | collective-permute-done | bytes 131104 | tf_op jit(solution)/shard_map/ppermute | solution.py:538
  36.7 0.0 collective-permute-start.11
  36.7 2.0 %collective-permute-done.12.refs_6_ = bf16[128,512]{1,0:T(8,128)(2,1)S(1)} collective-permute-done((bf16[128,512]{1,0:T(8,128)(2,1)S(1)}, bf16[128,512]{1,0:T(8,128)(2,1)S(1)}, u32[]{:S(2)}, u32[]{:S(2)}) %collective-permute-start.12) | collective-permute-done | bytes 131104 | tf_op jit(solution)/shard_map/ppermute | solution.py:538
  38.7 0.0 collective-permute-start.13
  38.7 0.0 collective-permute-done.9.refs_3_
  38.7 0.0 collective-permute-done.8.refs_2_
  38.7 0.0 collective-permute-done.7.refs_1_
  38.7 1.0 %shard_map.80 = (bf16[128,512]{1,0:T(8,128)(2,1)S(1)}, bf16[256,256]{1,0:T(8,128)(2,1)S(1)}, bf16[16,256]{1,0:T(8,128)(2,1)S(1)}) custom-call(bf16[144,256]{1,0:T(8,128)(2,1)S(1)} %shard_map.79.refs_0_, bf16[144,256]{1,0:T(8,128)(2,1)S(1)} %collective-permute-done.7.refs_1_, bf16[144,256]{1,0:T(8,128)(2,1)S(1)} %collective-permute-done.8.refs_2_, ...), custom_call_target="tpu_custom_call" | custom-call | bytes 1048576 | tf_op jit(solution)/shard_map/pallas_call | solution.py:73
  39.7 2.1 %collective-permute-start.14 = (bf16[128,512]{1,0:T(8,128)(2,1)S(1)}, bf16[128,512]{1,0:T(8,128)(2,1)S(1)}, u32[]{:S(2)}, u32[]{:S(2)}) collective-permute-start(bf16[128,512]{1,0:T(8,128)(2,1)S(1)} %get-tuple-element.44), channel_id=1, source_target_pairs={{0,8},{1,9},{2,10},{3,11},{4,12},{5,13},{6,14},{7,15},{8,0},{9,1},... | collective-permute-start | bytes 393224 | tf_op jit(solution)/shard_map/ppermute | solution.py:538
  41.8 1.1 %collective-permute-done.11.refs_5_ = bf16[128,512]{1,0:T(8,128)(2,1)S(1)} collective-permute-done((bf16[128,512]{1,0:T(8,128)(2,1)S(1)}, bf16[128,512]{1,0:T(8,128)(2,1)S(1)}, u32[]{:S(2)}, u32[]{:S(2)}) %collective-permute-start.11) | collective-permute-done | bytes 131104 | tf_op jit(solution)/shard_map/ppermute | solution.py:538
  42.9 2.8 %collective-permute-done.13.refs_7_ = bf16[128,512]{1,0:T(8,128)(2,1)S(1)} collective-permute-done((bf16[128,512]{1,0:T(8,128)(2,1)S(1)}, bf16[128,512]{1,0:T(8,128)(2,1)S(1)}, u32[]{:S(2)}, u32[]{:S(2)}) %collective-permute-start.13) | collective-permute-done | bytes 131104 | tf_op jit(solution)/shard_map/ppermute | solution.py:538
  45.7 0.7 %shard_map.81 = (f32[128,512]{1,0:T(8,128)S(1)}, f32[128,512]{1,0:T(8,128)S(1)}) custom-call(bf16[256,256]{1,0:T(8,128)(2,1)S(1)} %get-tuple-element.39.transform_ref, bf16[16,256]{1,0:T(8,128)(2,1)S(1)} %get-tuple-element.40.shift_ref, bf16[2,128,256]{2,1,0:T(8,128)(2,1)S(1)} %get-tuple-element.37.refs_5_.own_ref, ...), custom_call_target="tpu_custom_call" | custom-call | bytes 1048576 | tf_op jit(solution)/shard_map/pallas_call | solution.py:73
  46.4 0.9 %collective-permute-done.14.refs_2_ = bf16[128,512]{1,0:T(8,128)(2,1)S(1)} collective-permute-done((bf16[128,512]{1,0:T(8,128)(2,1)S(1)}, bf16[128,512]{1,0:T(8,128)(2,1)S(1)}, u32[]{:S(2)}, u32[]{:S(2)}) %collective-permute-start.14) | collective-permute-done | bytes 131104 | tf_op jit(solution)/shard_map/ppermute | solution.py:538
  47.3 0.8 %shard_map.82 = f32[1024,128]{1,0:T(8,128)} custom-call(f32[4,128]{1,0:T(4,128)S(1)} %get-tuple-element.25.table_ref.refs_4_.refs_6_, f32[128,512]{1,0:T(8,128)S(1)} %get-tuple-element.42.refs_0_, f32[128,512]{1,0:T(8,128)S(1)} %get-tuple-element.43.refs_1_, bf16[128,512]{1,0:T(8,128)(2,1)S(1)} %collective-permute-done.14.refs_2_), custom_call_target="tpu_custom_call" | custom-call | bytes 1048576 | tf_op jit(solution)/shard_map/pallas_call | solution.py:73
  (2 shorter events, 0.1 us)
Async XLA Ops:
  1.2 6.2 %collective-permute-start = (bf16[4,144,128]{2,1,0:T(8,128)(2,1)S(1)}, bf16[4,144,128]{2,1,0:T(8,128)(2,1)S(1)}, u32[]{:S(2)}, u32[]{:S(2)}) collective-permute-start(bf16[4,144,128]{2,1,0:T(8,128)(2,1)S(1)} %get-tuple-element.27), channel_id=1, source_target_pairs={{0,1},{1,2},{2,3},{3,4},{4,5},{5,6},{6,7},{7,0},{8,9},{9,10},{10,1... | collective-permute-start | bytes 442376 | tf_op jit(solution)/shard_map/ppermute | solution.py:497
  1.7 6.1 %collective-permute-start.1 = (bf16[4,144,128]{2,1,0:T(8,128)(2,1)S(1)}, bf16[4,144,128]{2,1,0:T(8,128)(2,1)S(1)}, u32[]{:S(2)}, u32[]{:S(2)}) collective-permute-start(bf16[4,144,128]{2,1,0:T(8,128)(2,1)S(1)} %get-tuple-element.28), channel_id=1, source_target_pairs={{1,0},{2,1},{3,2},{4,3},{5,4},{6,5},{7,6},{0,7},{9,8},{10,9},{11,1... | collective-permute-start | bytes 442376 | tf_op jit(solution)/shard_map/ppermute | solution.py:498
  4.7 1.0 %copy-start.2 = (f32[512]{0:T(512)S(1)}, f32[512]{0:T(512)}, u32[]{:S(2)}) copy-start(f32[512]{0:T(512)} %param.13) | copy-start | bytes 6148
  5.6 0.7 %copy-start.1 = (f32[512]{0:T(512)S(1)}, f32[512]{0:T(512)}, u32[]{:S(2)}) copy-start(f32[512]{0:T(512)} %param.12) | copy-start | bytes 6148
  5.6 0.7 %copy-start = (s32[512]{0:T(512)S(1)}, s32[512]{0:T(512)}, u32[]{:S(2)}) copy-start(s32[512]{0:T(512)} %param.11) | copy-start | bytes 6148
  5.6 0.7 %copy-start.3 = (s32[4]{0:T(128)S(1)}, s32[4]{0:T(128)}, u32[]{:S(2)}) copy-start(s32[4]{0:T(128)} %counts_ref.1) | copy-start | bytes 52
  9.9 6.4 %collective-permute-start.4 = (bf16[144,256]{1,0:T(8,128)(2,1)S(1)}, bf16[144,256]{1,0:T(8,128)(2,1)S(1)}, u32[]{:S(2)}, u32[]{:S(2)}) collective-permute-start(bf16[144,256]{1,0:T(8,128)(2,1)S(1)} %get-tuple-element.34), channel_id=1, source_target_pairs={{0,24},{1,25},{2,26},{3,27},{4,28},{5,29},{6,30},{7,31},{8,16},{9,... | collective-permute-start | bytes 221192 | tf_op jit(solution)/shard_map/ppermute | solution.py:538
  13.9 6.6 %collective-permute-start.2 = (bf16[144,256]{1,0:T(8,128)(2,1)S(1)}, bf16[144,256]{1,0:T(8,128)(2,1)S(1)}, u32[]{:S(2)}, u32[]{:S(2)}) collective-permute-start(bf16[144,256]{1,0:T(8,128)(2,1)S(1)} %get-tuple-element.34), channel_id=1, source_target_pairs={{0,8},{1,9},{2,10},{3,11},{4,12},{5,13},{6,14},{7,15},{8,0},{9,1},... | collective-permute-start | bytes 221192 | tf_op jit(solution)/shard_map/ppermute | solution.py:538
  13.9 6.6 %collective-permute-start.3 = (bf16[144,256]{1,0:T(8,128)(2,1)S(1)}, bf16[144,256]{1,0:T(8,128)(2,1)S(1)}, u32[]{:S(2)}, u32[]{:S(2)}) collective-permute-start(bf16[144,256]{1,0:T(8,128)(2,1)S(1)} %get-tuple-element.33.refs_0_.refs_7_), channel_id=1, source_target_pairs={{0,16},{1,17},{2,18},{3,19},{4,20},{5,21},{6,22},{7,23},{8,24},{9,... | collective-permute-start | bytes 221192 | tf_op jit(solution)/shard_map/ppermute | solution.py:538
  21.1 1.9 %collective-permute-start.5 = (bf16[144,256]{1,0:T(8,128)(2,1)S(1)}, bf16[144,256]{1,0:T(8,128)(2,1)S(1)}, u32[]{:S(2)}, u32[]{:S(2)}) collective-permute-start(bf16[144,256]{1,0:T(8,128)(2,1)S(1)} %shard_map.77.refs_0_), channel_id=1, source_target_pairs={{0,1},{1,0},{2,3},{3,2},{4,5},{5,4},{6,7},{7,6},{8,9},{9,8},{10,11... | collective-permute-start | bytes 221192 | tf_op jit(solution)/shard_map/ppermute | solution.py:538
  23.0 5.5 %collective-permute-start.6 = (bf16[144,256]{1,0:T(8,128)(2,1)S(1)}, bf16[144,256]{1,0:T(8,128)(2,1)S(1)}, u32[]{:S(2)}, u32[]{:S(2)}) collective-permute-start(bf16[144,256]{1,0:T(8,128)(2,1)S(1)} %shard_map.78.refs_0_), channel_id=1, source_target_pairs={{0,8},{1,9},{2,10},{3,11},{4,12},{5,13},{6,14},{7,15},{8,0},{9,1},... | collective-permute-start | bytes 221192 | tf_op jit(solution)/shard_map/ppermute | solution.py:538
  24.0 12.7 %collective-permute-start.10 = (bf16[128,512]{1,0:T(8,128)(2,1)S(1)}, bf16[128,512]{1,0:T(8,128)(2,1)S(1)}, u32[]{:S(2)}, u32[]{:S(2)}) collective-permute-start(bf16[128,512]{1,0:T(8,128)(2,1)S(1)} %get-tuple-element.38.refs_11_.refs_8_), channel_id=1, source_target_pairs={{0,16},{1,17},{2,18},{3,19},{4,20},{5,21},{6,22},{7,23},{8,24},{9,... | collective-permute-start | bytes 393224 | tf_op jit(solution)/shard_map/ppermute | solution.py:538
  25.4 13.3 %collective-permute-start.12 = (bf16[128,512]{1,0:T(8,128)(2,1)S(1)}, bf16[128,512]{1,0:T(8,128)(2,1)S(1)}, u32[]{:S(2)}, u32[]{:S(2)}) collective-permute-start(bf16[128,512]{1,0:T(8,128)(2,1)S(1)} %get-tuple-element.41.refs_4_), channel_id=1, source_target_pairs={{0,16},{1,17},{2,18},{3,19},{4,20},{5,21},{6,22},{7,23},{8,24},{9,... | collective-permute-start | bytes 393224 | tf_op jit(solution)/shard_map/ppermute | solution.py:538
  28.5 10.2 %collective-permute-start.9 = (bf16[144,256]{1,0:T(8,128)(2,1)S(1)}, bf16[144,256]{1,0:T(8,128)(2,1)S(1)}, u32[]{:S(2)}, u32[]{:S(2)}) collective-permute-start(bf16[144,256]{1,0:T(8,128)(2,1)S(1)} %shard_map.79.refs_0_), channel_id=1, source_target_pairs={{0,2},{1,3},{2,0},{3,1},{4,6},{5,7},{6,4},{7,5},{8,10},{9,11},{10,... | collective-permute-start | bytes 221192 | tf_op jit(solution)/shard_map/ppermute | solution.py:538
  30.1 8.6 %collective-permute-start.8 = (bf16[144,256]{1,0:T(8,128)(2,1)S(1)}, bf16[144,256]{1,0:T(8,128)(2,1)S(1)}, u32[]{:S(2)}, u32[]{:S(2)}) collective-permute-start(bf16[144,256]{1,0:T(8,128)(2,1)S(1)} %shard_map.79.refs_0_), channel_id=1, source_target_pairs={{0,4},{1,5},{2,6},{3,7},{4,0},{5,1},{6,2},{7,3},{8,12},{9,13},{10,... | collective-permute-start | bytes 221192 | tf_op jit(solution)/shard_map/ppermute | solution.py:538
  30.9 7.8 %collective-permute-start.7 = (bf16[144,256]{1,0:T(8,128)(2,1)S(1)}, bf16[144,256]{1,0:T(8,128)(2,1)S(1)}, u32[]{:S(2)}, u32[]{:S(2)}) collective-permute-start(bf16[144,256]{1,0:T(8,128)(2,1)S(1)} %shard_map.79.refs_0_), channel_id=1, source_target_pairs={{0,6},{1,7},{2,4},{3,5},{4,2},{5,3},{6,0},{7,1},{8,14},{9,15},{10,... | collective-permute-start | bytes 221192 | tf_op jit(solution)/shard_map/ppermute | solution.py:538
  36.7 6.2 %collective-permute-start.11 = (bf16[128,512]{1,0:T(8,128)(2,1)S(1)}, bf16[128,512]{1,0:T(8,128)(2,1)S(1)}, u32[]{:S(2)}, u32[]{:S(2)}) collective-permute-start(bf16[128,512]{1,0:T(8,128)(2,1)S(1)} %get-tuple-element.41.refs_4_), channel_id=1, source_target_pairs={{0,8},{1,9},{2,10},{3,11},{4,12},{5,13},{6,14},{7,15},{8,0},{9,1},... | collective-permute-start | bytes 393224 | tf_op jit(solution)/shard_map/ppermute | solution.py:538
  38.7 7.0 %collective-permute-start.13 = (bf16[128,512]{1,0:T(8,128)(2,1)S(1)}, bf16[128,512]{1,0:T(8,128)(2,1)S(1)}, u32[]{:S(2)}, u32[]{:S(2)}) collective-permute-start(bf16[128,512]{1,0:T(8,128)(2,1)S(1)} %collective-permute-done.12.refs_6_), channel_id=1, source_target_pairs={{0,8},{1,9},{2,10},{3,11},{4,12},{5,13},{6,14},{7,15},{8,0},{9,1},... | collective-permute-start | bytes 393224 | tf_op jit(solution)/shard_map/ppermute | solution.py:538
  39.7 7.5 %collective-permute-start.14 = (bf16[128,512]{1,0:T(8,128)(2,1)S(1)}, bf16[128,512]{1,0:T(8,128)(2,1)S(1)}, u32[]{:S(2)}, u32[]{:S(2)}) collective-permute-start(bf16[128,512]{1,0:T(8,128)(2,1)S(1)} %get-tuple-element.44), channel_id=1, source_target_pairs={{0,8},{1,9},{2,10},{3,11},{4,12},{5,13},{6,14},{7,15},{8,0},{9,1},... | collective-permute-start | bytes 393224 | tf_op jit(solution)/shard_map/ppermute | solution.py:538

commit v4 on v3

--- a/solution.py
+++ b/solution.py
@@ -164,7 +164,7 @@
     pick_ref, *rest,
 ):
     (coef_ref, value_ref, cells_ref) = rest[-3:]
-    seen_refs, part_refs = rest[:shares], rest[shares:-3]
+    seen_refs, mean_ref, part_refs = rest[: shares - 1], rest[shares - 1], rest[shares:-3]
     columns = states_ref.shape[1]
     total_rows = rows + 2 * STEPS
     count = count_row(table_ref, 0, columns)
@@ -228,8 +228,9 @@
     width = rows * columns // len(part_refs)
     for index, part_ref in enumerate(part_refs):
         part_ref[...] = cells_ref[:slots, index * width : (index + 1) * width]
-    seen = jnp.dot(cells_ref[...], pick_ref[...], preferred_element_type=F32)
-    share = seen.shape[1] // shares
+    mean_ref[...] = cells_ref[slots:, :]
+    share = pick_ref.shape[1] // shares
+    seen = jnp.dot(cells_ref[...], pick_ref[:, share:], preferred_element_type=F32)
     packed = [jnp.zeros((1, share), F32)] * 3
     for first in range(0, rows, share // columns):
         packed.extend(
@@ -242,6 +243,23 @@
         seen_ref[slots : slots + PAD, :] = part[slots:] + packed[:PAD]
         if packed.shape[0] > PAD:
             seen_ref[slots + PAD :, :] = packed[PAD:]
+
+
+def kept_kernel(slots, mean_ref, given_ref, pick_ref, *refs):
+    part_refs, out_ref = refs[:-1], refs[-1]
+    share = out_ref.shape[1]
+    width = part_refs[0].shape[1]
+    total = 0.0
+    for index, ref in enumerate(part_refs):
+        rows = slice(index * width, (index + 1) * width)
+        total = total + jnp.dot(ref[...], pick_ref[rows, :share], preferred_element_type=F32)
+    means = jnp.dot(mean_ref[...], pick_ref[:, :share], preferred_element_type=F32)
+    lower = given_ref[slots : slots + PAD, :].astype(F32)
+    place = lax.broadcasted_iota(jnp.int32, lower.shape, 0)
+    out_ref[:slots, :] = total.astype(BF16)
+    out_ref[slots : slots + PAD, :] = jnp.where(place < 3, means, lower).astype(BF16)
+    if out_ref.shape[0] > slots + PAD:
+        out_ref[slots + PAD :, :] = given_ref[slots + PAD :, :]
 
 
 def placing(slots, runners, members, counts_ref, runner, by_slot):
@@ -519,9 +537,9 @@
         [flat, fields],
     )
     lower = -(-(3 + 3 * (cells // share)) // PAD) * PAD
-    kept, given, *own_cells = call(
+    given, own_mean, *own_cells = call(
         functools.partial(forecast_kernel, slots, rows, shares),
-        [shape((slots + lower, share), BF16)] * shares
+        [shape((slots + lower, share), BF16), shape((PAD, cells), BF16)]
         + [shape((slots, cells // PARTS), BF16)] * PARTS,
         [],
         [table, flat, low, high, coefs, inner, pick],
@@ -530,6 +548,13 @@
             pltpu.VMEM((rows, slots, columns), F32),
             pltpu.VMEM((height, cells), BF16),
         ],
+    )
+
+    kept = call(
+        functools.partial(kept_kernel, slots),
+        shape((slots + lower, share), BF16),
+        [],
+        [own_mean, given, pick, *own_cells],
     )
 
     def moved(array, runner_bit, block_bit=0):

time: 48.3 us -> 49 us (1.014)
  waiting for transfers between devices: 20.3 us -> 21.5 us
  starting transfers between devices: 18.9 us -> 18.1 us
    ppermute x13, waiting for transfers between devices: 19.6 us -> 20.7 us  [moved(): return lax.ppermute(array, ('runner', 'cells'), partners(count, step))]
    ppermute x13, starting transfers between devices: 15.4 us -> 14.6 us  [moved(): return lax.ppermute(array, ('runner', 'cells'), partners(count, step))]
    pallas_call x10 -> x11, Pallas kernels: 8.13 us -> 8.41 us  [call(): pl.pallas_call(kernel, out_shape=out_shape, in_specs=[scalar] * len(scala...]
  transfers between devices with their start and end apart: 15 -> 15, of which waited for: 11 -> 12; matrix products, arithmetic and copies ran while one was open for 0% -> 0% of each run, Pallas kernels for 7% -> 7%
where the time goes in v4:
time: 49 us; the launch traced here: 48.8 us
  waiting for transfers between devices  21.5 us (44%)
  starting transfers between devices  18.1 us (37%)
  Pallas kernels  8.41 us (17%)
  local copies, waits for them, and re-layouts  0.67 us (1%)
    ppermute x13, waiting for transfers between devices, moved(): return lax.ppermute(array, ('runner', 'cells'), partners(count, step))  20.7 us
    ppermute x13, starting transfers between devices, moved(): return lax.ppermute(array, ('runner', 'cells'), partners(count, step))  14.6 us
    pallas_call x11, Pallas kernels, call(): pl.pallas_call(kernel, out_shape=out_shape, in_specs=[scalar] * len(scala...  8.41 us
    ppermute x1, starting transfers between devices, body(): high = lax.ppermute(first, 'cells', backward)  2.93 us
  transfers between devices with their start and end apart: 15, of which 12 were waited for; matrix products, arithmetic and copies ran while one was open for 0% of the time, Pallas kernels for 7%

profile of v4, /device:TPU:0, one launch (start us, length us, event | category | flops | bytes accessed | tf_op | source)
XLA Modules:
  0.0 48.8 jit_solution(15771472551783350097)
XLA Ops:
  0.0 1.2 %shard_map.74 = (bf16[4,144,128]{2,1,0:T(8,128)(2,1)S(1)}, bf16[4,144,128]{2,1,0:T(8,128)(2,1)S(1)}, f32[1024,128]{1,0:T(8,128)S(1)}, f32[3,8,128]{2,1,0:T(8,128)S(1)}) custom-call(f32[1024,128]{1,0:T(8,128)} %bitcast.9, f32[8,128]{1,0:T(8,128)} %diff_hbm.1, f32[2,8,128]{2,1,0:T(8,128)} %vel_hbm.1), custom_call_target="tpu_custom_call" | custom-call | bytes 1048576 | tf_op jit(solution)/shard_map/pallas_call | solution.py:73
  1.2 0.5 %collective-permute-start = (bf16[4,144,128]{2,1,0:T(8,128)(2,1)S(1)}, bf16[4,144,128]{2,1,0:T(8,128)(2,1)S(1)}, u32[]{:S(2)}, u32[]{:S(2)}) collective-permute-start(bf16[4,144,128]{2,1,0:T(8,128)(2,1)S(1)} %get-tuple-element.27), channel_id=1, source_target_pairs={{0,1},{1,2},{2,3},{3,4},{4,5},{5,6},{6,7},{7,0},{8,9},{9,10},{10,1... | collective-permute-start | bytes 442376 | tf_op jit(solution)/shard_map/ppermute | solution.py:515
  1.7 2.9 %collective-permute-start.1 = (bf16[4,144,128]{2,1,0:T(8,128)(2,1)S(1)}, bf16[4,144,128]{2,1,0:T(8,128)(2,1)S(1)}, u32[]{:S(2)}, u32[]{:S(2)}) collective-permute-start(bf16[4,144,128]{2,1,0:T(8,128)(2,1)S(1)} %get-tuple-element.28), channel_id=1, source_target_pairs={{1,0},{2,1},{3,2},{4,3},{5,4},{6,5},{7,6},{0,7},{9,8},{10,9},{11,1... | collective-permute-start | bytes 442376 | tf_op jit(solution)/shard_map/ppermute | solution.py:516
  4.7 0.0 copy-start.2
  4.7 0.9 %shard_map.75 = (f32[8,5,8,128]{3,2,1,0:T(8,128)S(1)}, f32[12,128,128]{2,1,0:T(8,128)S(1)}) custom-call(f32[1024,128]{1,0:T(8,128)S(1)} %get-tuple-element.26.states_ref, f32[3,8,128]{2,1,0:T(8,128)S(1)} %get-tuple-element.29.fields_ref), custom_call_target="tpu_custom_call" | custom-call | bytes 1048576 | tf_op jit(solution)/shard_map/pallas_call | solution.py:73
  5.6 0.0 copy-start.1
  5.6 0.0 copy-start
  5.6 0.0 copy-start.3
  5.6 0.0 copy-done.2
  5.7 0.6 %copy-done.1 = f32[512]{0:T(512)S(1)} copy-done((f32[512]{0:T(512)S(1)}, f32[512]{0:T(512)}, u32[]{:S(2)}) %copy-start.1) | copy-done | bytes 2072
  6.3 0.0 copy-done
  6.3 0.0 copy-done.3
  6.3 0.8 %shard_map.73 = (bf16[1024,512]{1,0:T(8,128)(2,1)S(1)}, f32[8,256]{1,0:T(8,128)S(1)}, bf16[256,512]{1,0:T(8,128)(2,1)S(1)}, bf16[2,128,256]{2,1,0:T(8,128)(2,1)S(1)}, f32[4,128]{1,0:T(4,128)S(1)}) custom-call(s32[4]{0:T(128)S(1)} %copy-done.3, s32[1]{0:T(128)} %bitcast.rank_ref, s32[1,512]{1,0:T(1,128)S(1)} %bitcast.6, f32[1,512]{1,0:T(1,128)S(1)} %bitcast.7, ...), custom_call_target="tpu_custom_call" | custom-call | bytes 1048576 | tf_op jit(solution)/shard_map/pallas_call | solution.py:73
  7.1 0.3 collective-permute-done.low_ref
  7.4 0.4 collective-permute-done.1.high_ref
  7.9 2.0 %shard_map.76 = (bf16[144,256]{1,0:T(8,128)(2,1)S(1)}, bf16[16,1024]{1,0:T(8,128)(2,1)S(1)}, bf16[128,512]{1,0:T(8,128)(2,1)S(1)}, bf16[128,512]{1,0:T(8,128)(2,1)S(1)}) custom-call(f32[4,128]{1,0:T(4,128)S(1)} %get-tuple-element.25.table_ref.refs_4_.refs_6_, f32[1024,128]{1,0:T(8,128)S(1)} %get-tuple-element.26.states_ref, ...), custom_call_target="tpu_custom_call" | custom-call | bytes 1048576 | tf_op jit(solution)/shard_map/pallas_call | solution.py:73
  9.9 0.3 shard_map.77.refs_0_.refs_7_
  10.2 3.0 %collective-permute-start.3 = (bf16[144,256]{1,0:T(8,128)(2,1)S(1)}, bf16[144,256]{1,0:T(8,128)(2,1)S(1)}, u32[]{:S(2)}, u32[]{:S(2)}) collective-permute-start(bf16[144,256]{1,0:T(8,128)(2,1)S(1)} %shard_map.77.refs_0_.refs_7_), channel_id=1, source_target_pairs={{0,16},{1,17},{2,18},{3,19},{4,20},{5,21},{6,22},{7,23},{8,24},{9,... | collective-permute-start | bytes 221192 | tf_op jit(solution)/shard_map/ppermute | solution.py:563
  13.2 1.3 %collective-permute-start.4 = (bf16[144,256]{1,0:T(8,128)(2,1)S(1)}, bf16[144,256]{1,0:T(8,128)(2,1)S(1)}, u32[]{:S(2)}, u32[]{:S(2)}) collective-permute-start(bf16[144,256]{1,0:T(8,128)(2,1)S(1)} %get-tuple-element.34.given_ref), channel_id=1, source_target_pairs={{0,24},{1,25},{2,26},{3,27},{4,28},{5,29},{6,30},{7,31},{8,16},{9,... | collective-permute-start | bytes 221192 | tf_op jit(solution)/shard_map/ppermute | solution.py:563
  14.5 0.2 collective-permute-start.2
  14.8 0.8 %collective-permute-done.3.refs_2_.refs_9_ = bf16[144,256]{1,0:T(8,128)(2,1)S(1)} collective-permute-done((bf16[144,256]{1,0:T(8,128)(2,1)S(1)}, bf16[144,256]{1,0:T(8,128)(2,1)S(1)}, u32[]{:S(2)}, u32[]{:S(2)}) %collective-permute-start.3) | collective-permute-done | bytes 73760 | tf_op jit(solution)/shard_map/ppermute | solution.py:563
  15.5 4.5 %collective-permute-done.4.refs_3_.refs_10_ = bf16[144,256]{1,0:T(8,128)(2,1)S(1)} collective-permute-done((bf16[144,256]{1,0:T(8,128)(2,1)S(1)}, bf16[144,256]{1,0:T(8,128)(2,1)S(1)}, u32[]{:S(2)}, u32[]{:S(2)}) %collective-permute-start.4) | collective-permute-done | bytes 73760 | tf_op jit(solution)/shard_map/ppermute | solution.py:563
  20.0 1.2 %collective-permute-done.2.refs_1_.refs_8_ = bf16[144,256]{1,0:T(8,128)(2,1)S(1)} collective-permute-done((bf16[144,256]{1,0:T(8,128)(2,1)S(1)}, bf16[144,256]{1,0:T(8,128)(2,1)S(1)}, u32[]{:S(2)}, u32[]{:S(2)}) %collective-permute-start.2) | collective-permute-done | bytes 73760 | tf_op jit(solution)/shard_map/ppermute | solution.py:563
  21.2 0.6 %shard_map.78.refs_0_ = bf16[144,256]{1,0:T(8,128)(2,1)S(1)} custom-call(bf16[144,256]{1,0:T(8,128)(2,1)S(1)} %shard_map.77.refs_0_.refs_7_, bf16[144,256]{1,0:T(8,128)(2,1)S(1)} %collective-permute-done.2.refs_1_.refs_8_, bf16[144,256]{1,0:T(8,128)(2,1)S(1)} %collective-permute-done.3.refs_2_.refs_9_, ...), custom_call_target="tpu_custom_call" | custom-call | bytes 1048576 | tf_op jit(solution)/shard_map/pallas_call | solution.py:73
  21.8 0.1 collective-permute-start.5
  21.9 1.2 %collective-permute-done.5.refs_1_ = bf16[144,256]{1,0:T(8,128)(2,1)S(1)} collective-permute-done((bf16[144,256]{1,0:T(8,128)(2,1)S(1)}, bf16[144,256]{1,0:T(8,128)(2,1)S(1)}, u32[]{:S(2)}, u32[]{:S(2)}) %collective-permute-start.5) | collective-permute-done | bytes 73760 | tf_op jit(solution)/shard_map/ppermute | solution.py:563
  23.1 0.9 %collective-permute-start.6 = (bf16[144,256]{1,0:T(8,128)(2,1)S(1)}, bf16[144,256]{1,0:T(8,128)(2,1)S(1)}, u32[]{:S(2)}, u32[]{:S(2)}) collective-permute-start(bf16[144,256]{1,0:T(8,128)(2,1)S(1)} %shard_map.79.refs_0_), channel_id=1, source_target_pairs={{0,8},{1,9},{2,10},{3,11},{4,12},{5,13},{6,14},{7,15},{8,0},{9,1},... | collective-permute-start | bytes 221192 | tf_op jit(solution)/shard_map/ppermute | solution.py:563
  24.0 3.4 %collective-permute-start.12 = (bf16[128,512]{1,0:T(8,128)(2,1)S(1)}, bf16[128,512]{1,0:T(8,128)(2,1)S(1)}, u32[]{:S(2)}, u32[]{:S(2)}) collective-permute-start(bf16[128,512]{1,0:T(8,128)(2,1)S(1)} %get-tuple-element.35.refs_0_.refs_4_), channel_id=1, source_target_pairs={{0,16},{1,17},{2,18},{3,19},{4,20},{5,21},{6,22},{7,23},{8,24},{9,... | collective-permute-start | bytes 393224 | tf_op jit(solution)/shard_map/ppermute | solution.py:563
  27.4 0.0 collective-permute-start.10
  27.4 0.1 collective-permute-done.6.refs_1_
  27.6 1.5 %collective-permute-start.9 = (bf16[144,256]{1,0:T(8,128)(2,1)S(1)}, bf16[144,256]{1,0:T(8,128)(2,1)S(1)}, u32[]{:S(2)}, u32[]{:S(2)}) collective-permute-start(bf16[144,256]{1,0:T(8,128)(2,1)S(1)} %shard_map.80.refs_0_), channel_id=1, source_target_pairs={{0,2},{1,3},{2,0},{3,1},{4,6},{5,7},{6,4},{7,5},{8,10},{9,11},{10,... | collective-permute-start | bytes 221192 | tf_op jit(solution)/shard_map/ppermute | solution.py:563
  29.1 1.0 %collective-permute-start.8 = (bf16[144,256]{1,0:T(8,128)(2,1)S(1)}, bf16[144,256]{1,0:T(8,128)(2,1)S(1)}, u32[]{:S(2)}, u32[]{:S(2)}) collective-permute-start(bf16[144,256]{1,0:T(8,128)(2,1)S(1)} %shard_map.80.refs_0_), channel_id=1, source_target_pairs={{0,4},{1,5},{2,6},{3,7},{4,0},{5,1},{6,2},{7,3},{8,12},{9,13},{10,... | collective-permute-start | bytes 221192 | tf_op jit(solution)/shard_map/ppermute | solution.py:563
  30.1 1.0 %collective-permute-start.7 = (bf16[144,256]{1,0:T(8,128)(2,1)S(1)}, bf16[144,256]{1,0:T(8,128)(2,1)S(1)}, u32[]{:S(2)}, u32[]{:S(2)}) collective-permute-start(bf16[144,256]{1,0:T(8,128)(2,1)S(1)} %shard_map.80.refs_0_), channel_id=1, source_target_pairs={{0,6},{1,7},{2,4},{3,5},{4,2},{5,3},{6,0},{7,1},{8,14},{9,15},{10,... | collective-permute-start | bytes 221192 | tf_op jit(solution)/shard_map/ppermute | solution.py:563
  31.1 6.2 %collective-permute-done.12.refs_6_ = bf16[128,512]{1,0:T(8,128)(2,1)S(1)} collective-permute-done((bf16[128,512]{1,0:T(8,128)(2,1)S(1)}, bf16[128,512]{1,0:T(8,128)(2,1)S(1)}, u32[]{:S(2)}, u32[]{:S(2)}) %collective-permute-start.12) | collective-permute-done | bytes 131104 | tf_op jit(solution)/shard_map/ppermute | solution.py:563
  37.4 0.0 collective-permute-start.11
  37.4 2.1 %collective-permute-done.10.refs_12_.refs_9_ = bf16[128,512]{1,0:T(8,128)(2,1)S(1)} collective-permute-done((bf16[128,512]{1,0:T(8,128)(2,1)S(1)}, bf16[128,512]{1,0:T(8,128)(2,1)S(1)}, u32[]{:S(2)}, u32[]{:S(2)}) %collective-permute-start.10) | collective-permute-done | bytes 131104 | tf_op jit(solution)/shard_map/ppermute | solution.py:563
  39.5 0.0 collective-permute-start.13
  39.5 0.0 collective-permute-done.9.refs_3_
  39.5 0.0 collective-permute-done.8.refs_2_
  39.5 0.0 collective-permute-done.7.refs_1_
  39.5 1.0 %shard_map.81 = (bf16[128,512]{1,0:T(8,128)(2,1)S(1)}, bf16[256,256]{1,0:T(8,128)(2,1)S(1)}, bf16[16,256]{1,0:T(8,128)(2,1)S(1)}) custom-call(bf16[144,256]{1,0:T(8,128)(2,1)S(1)} %shard_map.80.refs_0_, bf16[144,256]{1,0:T(8,128)(2,1)S(1)} %collective-permute-done.7.refs_1_, bf16[144,256]{1,0:T(8,128)(2,1)S(1)} %collective-permute-done.8.refs_2_, ...), custom_call_target="tpu_custom_call" | custom-call | bytes 1048576 | tf_op jit(solution)/shard_map/pallas_call | solution.py:73
  40.5 2.1 %collective-permute-start.14 = (bf16[128,512]{1,0:T(8,128)(2,1)S(1)}, bf16[128,512]{1,0:T(8,128)(2,1)S(1)}, u32[]{:S(2)}, u32[]{:S(2)}) collective-permute-start(bf16[128,512]{1,0:T(8,128)(2,1)S(1)} %get-tuple-element.44), channel_id=1, source_target_pairs={{0,8},{1,9},{2,10},{3,11},{4,12},{5,13},{6,14},{7,15},{8,0},{9,1},... | collective-permute-start | bytes 393224 | tf_op jit(solution)/shard_map/ppermute | solution.py:563
  42.6 0.8 %collective-permute-done.11.refs_5_ = bf16[128,512]{1,0:T(8,128)(2,1)S(1)} collective-permute-done((bf16[128,512]{1,0:T(8,128)(2,1)S(1)}, bf16[128,512]{1,0:T(8,128)(2,1)S(1)}, u32[]{:S(2)}, u32[]{:S(2)}) %collective-permute-start.11) | collective-permute-done | bytes 131104 | tf_op jit(solution)/shard_map/ppermute | solution.py:563
  43.4 2.8 %collective-permute-done.13.refs_7_ = bf16[128,512]{1,0:T(8,128)(2,1)S(1)} collective-permute-done((bf16[128,512]{1,0:T(8,128)(2,1)S(1)}, bf16[128,512]{1,0:T(8,128)(2,1)S(1)}, u32[]{:S(2)}, u32[]{:S(2)}) %collective-permute-start.13) | collective-permute-done | bytes 131104 | tf_op jit(solution)/shard_map/ppermute | solution.py:563
  46.2 0.7 %shard_map.82 = (f32[128,512]{1,0:T(8,128)S(1)}, f32[128,512]{1,0:T(8,128)S(1)}) custom-call(bf16[256,256]{1,0:T(8,128)(2,1)S(1)} %get-tuple-element.40.transform_ref, bf16[16,256]{1,0:T(8,128)(2,1)S(1)} %get-tuple-element.41.shift_ref, bf16[2,128,256]{2,1,0:T(8,128)(2,1)S(1)} %get-tuple-element.39.refs_5_.own_ref, ...), custom_call_target="tpu_custom_call" | custom-call | bytes 1048576 | tf_op jit(solution)/shard_map/pallas_call | solution.py:73
  46.9 1.1 %collective-permute-done.14.refs_2_ = bf16[128,512]{1,0:T(8,128)(2,1)S(1)} collective-permute-done((bf16[128,512]{1,0:T(8,128)(2,1)S(1)}, bf16[128,512]{1,0:T(8,128)(2,1)S(1)}, u32[]{:S(2)}, u32[]{:S(2)}) %collective-permute-start.14) | collective-permute-done | bytes 131104 | tf_op jit(solution)/shard_map/ppermute | solution.py:563
  48.0 0.8 %shard_map.83 = f32[1024,128]{1,0:T(8,128)} custom-call(f32[4,128]{1,0:T(4,128)S(1)} %get-tuple-element.25.table_ref.refs_4_.refs_6_, f32[128,512]{1,0:T(8,128)S(1)} %get-tuple-element.42.refs_0_, f32[128,512]{1,0:T(8,128)S(1)} %get-tuple-element.43.refs_1_, bf16[128,512]{1,0:T(8,128)(2,1)S(1)} %collective-permute-done.14.refs_2_), custom_call_target="tpu_custom_call" | custom-call | bytes 1048576 | tf_op jit(solution)/shard_map/pallas_call | solution.py:73
  (2 shorter events, 0.1 us)
Async XLA Ops:
  1.2 6.2 %collective-permute-start = (bf16[4,144,128]{2,1,0:T(8,128)(2,1)S(1)}, bf16[4,144,128]{2,1,0:T(8,128)(2,1)S(1)}, u32[]{:S(2)}, u32[]{:S(2)}) collective-permute-start(bf16[4,144,128]{2,1,0:T(8,128)(2,1)S(1)} %get-tuple-element.27), channel_id=1, source_target_pairs={{0,1},{1,2},{2,3},{3,4},{4,5},{5,6},{6,7},{7,0},{8,9},{9,10},{10,1... | collective-permute-start | bytes 442376 | tf_op jit(solution)/shard_map/ppermute | solution.py:515
  1.7 6.1 %collective-permute-start.1 = (bf16[4,144,128]{2,1,0:T(8,128)(2,1)S(1)}, bf16[4,144,128]{2,1,0:T(8,128)(2,1)S(1)}, u32[]{:S(2)}, u32[]{:S(2)}) collective-permute-start(bf16[4,144,128]{2,1,0:T(8,128)(2,1)S(1)} %get-tuple-element.28), channel_id=1, source_target_pairs={{1,0},{2,1},{3,2},{4,3},{5,4},{6,5},{7,6},{0,7},{9,8},{10,9},{11,1... | collective-permute-start | bytes 442376 | tf_op jit(solution)/shard_map/ppermute | solution.py:516
  4.7 1.0 %copy-start.2 = (f32[512]{0:T(512)S(1)}, f32[512]{0:T(512)}, u32[]{:S(2)}) copy-start(f32[512]{0:T(512)} %param.13) | copy-start | bytes 6148
  5.6 0.7 %copy-start.1 = (f32[512]{0:T(512)S(1)}, f32[512]{0:T(512)}, u32[]{:S(2)}) copy-start(f32[512]{0:T(512)} %param.12) | copy-start | bytes 6148
  5.6 0.7 %copy-start = (s32[512]{0:T(512)S(1)}, s32[512]{0:T(512)}, u32[]{:S(2)}) copy-start(s32[512]{0:T(512)} %param.11) | copy-start | bytes 6148
  5.6 0.7 %copy-start.3 = (s32[4]{0:T(128)S(1)}, s32[4]{0:T(128)}, u32[]{:S(2)}) copy-start(s32[4]{0:T(128)} %counts_ref.1) | copy-start | bytes 52
  10.2 5.3 %collective-permute-start.3 = (bf16[144,256]{1,0:T(8,128)(2,1)S(1)}, bf16[144,256]{1,0:T(8,128)(2,1)S(1)}, u32[]{:S(2)}, u32[]{:S(2)}) collective-permute-start(bf16[144,256]{1,0:T(8,128)(2,1)S(1)} %shard_map.77.refs_0_.refs_7_), channel_id=1, source_target_pairs={{0,16},{1,17},{2,18},{3,19},{4,20},{5,21},{6,22},{7,23},{8,24},{9,... | collective-permute-start | bytes 221192 | tf_op jit(solution)/shard_map/ppermute | solution.py:563
  13.2 6.8 %collective-permute-start.4 = (bf16[144,256]{1,0:T(8,128)(2,1)S(1)}, bf16[144,256]{1,0:T(8,128)(2,1)S(1)}, u32[]{:S(2)}, u32[]{:S(2)}) collective-permute-start(bf16[144,256]{1,0:T(8,128)(2,1)S(1)} %get-tuple-element.34.given_ref), channel_id=1, source_target_pairs={{0,24},{1,25},{2,26},{3,27},{4,28},{5,29},{6,30},{7,31},{8,16},{9,... | collective-permute-start | bytes 221192 | tf_op jit(solution)/shard_map/ppermute | solution.py:563
  14.5 6.7 %collective-permute-start.2 = (bf16[144,256]{1,0:T(8,128)(2,1)S(1)}, bf16[144,256]{1,0:T(8,128)(2,1)S(1)}, u32[]{:S(2)}, u32[]{:S(2)}) collective-permute-start(bf16[144,256]{1,0:T(8,128)(2,1)S(1)} %get-tuple-element.34.given_ref), channel_id=1, source_target_pairs={{0,8},{1,9},{2,10},{3,11},{4,12},{5,13},{6,14},{7,15},{8,0},{9,1},... | collective-permute-start | bytes 221192 | tf_op jit(solution)/shard_map/ppermute | solution.py:563
  21.8 1.3 %collective-permute-start.5 = (bf16[144,256]{1,0:T(8,128)(2,1)S(1)}, bf16[144,256]{1,0:T(8,128)(2,1)S(1)}, u32[]{:S(2)}, u32[]{:S(2)}) collective-permute-start(bf16[144,256]{1,0:T(8,128)(2,1)S(1)} %shard_map.78.refs_0_), channel_id=1, source_target_pairs={{0,1},{1,0},{2,3},{3,2},{4,5},{5,4},{6,7},{7,6},{8,9},{9,8},{10,11... | collective-permute-start | bytes 221192 | tf_op jit(solution)/shard_map/ppermute | solution.py:563
  23.1 4.4 %collective-permute-start.6 = (bf16[144,256]{1,0:T(8,128)(2,1)S(1)}, bf16[144,256]{1,0:T(8,128)(2,1)S(1)}, u32[]{:S(2)}, u32[]{:S(2)}) collective-permute-start(bf16[144,256]{1,0:T(8,128)(2,1)S(1)} %shard_map.79.refs_0_), channel_id=1, source_target_pairs={{0,8},{1,9},{2,10},{3,11},{4,12},{5,13},{6,14},{7,15},{8,0},{9,1},... | collective-permute-start | bytes 221192 | tf_op jit(solution)/shard_map/ppermute | solution.py:563
  24.0 13.3 %collective-permute-start.12 = (bf16[128,512]{1,0:T(8,128)(2,1)S(1)}, bf16[128,512]{1,0:T(8,128)(2,1)S(1)}, u32[]{:S(2)}, u32[]{:S(2)}) collective-permute-start(bf16[128,512]{1,0:T(8,128)(2,1)S(1)} %get-tuple-element.35.refs_0_.refs_4_), channel_id=1, source_target_pairs={{0,16},{1,17},{2,18},{3,19},{4,20},{5,21},{6,22},{7,23},{8,24},{9,... | collective-permute-start | bytes 393224 | tf_op jit(solution)/shard_map/ppermute | solution.py:563
  27.4 12.1 %collective-permute-start.10 = (bf16[128,512]{1,0:T(8,128)(2,1)S(1)}, bf16[128,512]{1,0:T(8,128)(2,1)S(1)}, u32[]{:S(2)}, u32[]{:S(2)}) collective-permute-start(bf16[128,512]{1,0:T(8,128)(2,1)S(1)} %get-tuple-element.36.refs_1_.refs_11_.refs_8_), channel_id=1, source_target_pairs={{0,16},{1,17},{2,18},{3,19},{4,20},{5,21},{6,22},{7,23},{8,24},{9,... | collective-permute-start | bytes 393224 | tf_op jit(solution)/shard_map/ppermute | solution.py:563
  27.6 11.9 %collective-permute-start.9 = (bf16[144,256]{1,0:T(8,128)(2,1)S(1)}, bf16[144,256]{1,0:T(8,128)(2,1)S(1)}, u32[]{:S(2)}, u32[]{:S(2)}) collective-permute-start(bf16[144,256]{1,0:T(8,128)(2,1)S(1)} %shard_map.80.refs_0_), channel_id=1, source_target_pairs={{0,2},{1,3},{2,0},{3,1},{4,6},{5,7},{6,4},{7,5},{8,10},{9,11},{10,... | collective-permute-start | bytes 221192 | tf_op jit(solution)/shard_map/ppermute | solution.py:563
  29.1 10.4 %collective-permute-start.8 = (bf16[144,256]{1,0:T(8,128)(2,1)S(1)}, bf16[144,256]{1,0:T(8,128)(2,1)S(1)}, u32[]{:S(2)}, u32[]{:S(2)}) collective-permute-start(bf16[144,256]{1,0:T(8,128)(2,1)S(1)} %shard_map.80.refs_0_), channel_id=1, source_target_pairs={{0,4},{1,5},{2,6},{3,7},{4,0},{5,1},{6,2},{7,3},{8,12},{9,13},{10,... | collective-permute-start | bytes 221192 | tf_op jit(solution)/shard_map/ppermute | solution.py:563
  30.1 9.4 %collective-permute-start.7 = (bf16[144,256]{1,0:T(8,128)(2,1)S(1)}, bf16[144,256]{1,0:T(8,128)(2,1)S(1)}, u32[]{:S(2)}, u32[]{:S(2)}) collective-permute-start(bf16[144,256]{1,0:T(8,128)(2,1)S(1)} %shard_map.80.refs_0_), channel_id=1, source_target_pairs={{0,6},{1,7},{2,4},{3,5},{4,2},{5,3},{6,0},{7,1},{8,14},{9,15},{10,... | collective-permute-start | bytes 221192 | tf_op jit(solution)/shard_map/ppermute | solution.py:563
  37.4 6.0 %collective-permute-start.11 = (bf16[128,512]{1,0:T(8,128)(2,1)S(1)}, bf16[128,512]{1,0:T(8,128)(2,1)S(1)}, u32[]{:S(2)}, u32[]{:S(2)}) collective-permute-start(bf16[128,512]{1,0:T(8,128)(2,1)S(1)} %get-tuple-element.35.refs_0_.refs_4_), channel_id=1, source_target_pairs={{0,8},{1,9},{2,10},{3,11},{4,12},{5,13},{6,14},{7,15},{8,0},{9,1},... | collective-permute-start | bytes 393224 | tf_op jit(solution)/shard_map/ppermute | solution.py:563
  39.5 6.7 %collective-permute-start.13 = (bf16[128,512]{1,0:T(8,128)(2,1)S(1)}, bf16[128,512]{1,0:T(8,128)(2,1)S(1)}, u32[]{:S(2)}, u32[]{:S(2)}) collective-permute-start(bf16[128,512]{1,0:T(8,128)(2,1)S(1)} %collective-permute-done.12.refs_6_), channel_id=1, source_target_pairs={{0,8},{1,9},{2,10},{3,11},{4,12},{5,13},{6,14},{7,15},{8,0},{9,1},... | collective-permute-start | bytes 393224 | tf_op jit(solution)/shard_map/ppermute | solution.py:563
  40.5 7.4 %collective-permute-start.14 = (bf16[128,512]{1,0:T(8,128)(2,1)S(1)}, bf16[128,512]{1,0:T(8,128)(2,1)S(1)}, u32[]{:S(2)}, u32[]{:S(2)}) collective-permute-start(bf16[128,512]{1,0:T(8,128)(2,1)S(1)} %get-tuple-element.44), channel_id=1, source_target_pairs={{0,8},{1,9},{2,10},{3,11},{4,12},{5,13},{6,14},{7,15},{8,0},{9,1},... | collective-permute-start | bytes 393224 | tf_op jit(solution)/shard_map/ppermute | solution.py:563
